TPU v7x, 1024 devices: a whole 4x8x16 slice. The times are simulated.
1024 devices in a mesh: dp: 64 (over z, x_lo, core), tensor: 16 (over x_hi, y).
Axes of the slice: x: 4 (x_hi: 2, x_lo: 2; x = x_hi * 2 + x_lo), y: 8, z: 16, core: 2. Of those that a mesh axis runs over, the one named last changes fastest.
Arguments:
- latent_pre: bfloat16 [32768, 512], P('dp'), may hold values from -16 to 16
- norm_gain: float32 [512], replicated, may hold values from 0.1 to 1.9
- kv_weight: bfloat16 [512, 32768], P(None, 'tensor'), may hold values from -0.25 to 0.25
- down_weight: bfloat16 [7168, 512], P('tensor'), may hold values from -0.25 to 0.25
- grad_kv: bfloat16 [32768, 32768], P('dp', 'tensor'), may hold values from -0.75 to 0.75
- master: float32 [512, 32768], P('dp', 'tensor'), may hold values from -0.25 to 0.25
- first_moment: float32 [512, 32768], P('dp', 'tensor'), may hold values from -120 to 120
- second_moment: float32 [512, 32768], P('dp', 'tensor'), may hold values from 100 to 1000
Outputs:
- grad_hidden: bfloat16 [32768, 7168], P('dp', 'tensor')
- new_master: float32 [512, 32768], P('dp', 'tensor')
- new_first: float32 [512, 32768], P('dp', 'tensor')
- new_second: float32 [512, 32768], P('dp', 'tensor')
- new_replica: bfloat16 [512, 32768], P(None, 'tensor')
All inputs are finite; a program needn't handle non-finite values.
Results may differ from a plain program's by a relative error of at most 0.002.
The roundings to bfloat16 on the way count: a program that leaves them out, or rounds other values in their place, can miss the bound.
Values may be sent and summed in bfloat16 or wider, within the bound.
No kernel may reach another device: no remote copies, remote signals or barrier semaphores. Data moves between devices by JAX's collectives and lax.ppermute only.
A program may use at most 32 MiB of HBM per device.

v0:
```python
import jax
import jax.numpy as jnp
from jax import lax
from jax.sharding import Mesh
from jax.sharding import PartitionSpec as P

TENSOR = ("tensor_0", "tensor_1")
DP = ("dp_0", "dp_1", "dp_2")


bias_first = 0.9999734386011124
bias_second = 0.09520785288629112


def split_up(x, dim, devices):
    shape = x.shape
    blocks = x.reshape(*shape[:dim], devices, shape[dim] // devices, *shape[dim + 1 :])
    return jnp.moveaxis(blocks, dim, 0)


def sum_at_owner(x, axis, dim):
    devices = lax.axis_size(axis)
    blocks = lax.all_to_all(split_up(x, dim, devices), axis, 0, 0, tiled=True)
    return jnp.sum(blocks, axis=0)


def joined_along(blocks, dim):
    blocks = jnp.moveaxis(blocks, 0, dim)
    shape = blocks.shape
    return blocks.reshape(*shape[:dim], shape[dim] * shape[dim + 1], *shape[dim + 2 :])


def all_blocks(x, axes, sequence):
    blocks = x[None]
    for k in sequence:
        blocks = lax.all_gather(blocks, axes[k], axis=0, tiled=True)
    carried = [lax.axis_size(axes[k]) for k in reversed(sequence)]
    blocks = blocks.reshape(*carried, *x.shape)
    turned = sorted(range(len(sequence)), key=lambda place: sequence[len(sequence) - 1 - place])
    return blocks.transpose(*turned, *range(len(sequence), blocks.ndim)).reshape(-1, *x.shape)


def gathered_by_axis(x, axes, sequence, dim):
    return joined_along(all_blocks(x, axes, sequence), dim)


def own_block(blocks, axes, sequence):
    inside = blocks.shape[1:]
    blocks = blocks.reshape(*(lax.axis_size(a) for a in axes), *inside)
    blocks = jnp.moveaxis(blocks, sequence, range(len(axes))).reshape(-1, *inside)
    for k in sequence:
        blocks = lax.psum_scatter(blocks, axes[k], scatter_dimension=0, tiled=True)
    return blocks[0]


def summed_rows(x, axes, sequence, dim):
    devices = lax.axis_size(axes)
    return own_block(split_up(x, dim, devices), axes, sequence)


def norm_backward(latent_rows, norm_gain, grad_rows):
    values = latent_rows.astype(jnp.float32)
    inverse_rms = lax.rsqrt(jnp.mean(values * values, axis=1, keepdims=True) + 1e-06)
    unit = values * inverse_rms
    scaled = grad_rows * norm_gain
    inner = jnp.mean(scaled * unit, axis=1, keepdims=True)
    return (inverse_rms * (scaled - unit * inner)).astype(jnp.bfloat16)


def local(
    latent_pre, norm_gain, kv_weight, down_weight, grad_kv, master, first_moment, second_moment
):
    values = latent_pre.astype(jnp.float32)
    inverse_rms = lax.rsqrt(jnp.mean(values * values, axis=1, keepdims=True) + 1e-06)
    normalized = (values * inverse_rms * norm_gain).astype(jnp.bfloat16)
    share_rows = grad_kv.shape[0] // lax.axis_size(TENSOR)
    grad_share = sum_at_owner(
        lax.dot_general(
            grad_kv, kv_weight, (((1,), (1,)), ((), ())), preferred_element_type=jnp.float32
        ),
        TENSOR,
        0,
    )
    own_start = lax.axis_index(TENSOR) * share_rows
    latent_share = lax.dynamic_slice_in_dim(latent_pre, own_start, share_rows, 0)
    pre_share = norm_backward(latent_share, norm_gain, grad_share)
    grad_pre = gathered_by_axis(pre_share, TENSOR, (0, 1), 0)
    grad_hidden = lax.dot_general(
        grad_pre, down_weight, (((1,), (1,)), ((), ())), preferred_element_type=jnp.float32
    ).astype(jnp.bfloat16)
    weight_grad = summed_rows(
        lax.dot_general(
            normalized, grad_kv, (((0,), (0,)), ((), ())), preferred_element_type=jnp.float32
        ),
        DP,
        (2, 0, 1),
        0,
    )
    new_first = 0.9 * first_moment + 0.1 * weight_grad
    new_second = 0.999 * second_moment + 0.001 * weight_grad * weight_grad
    first_hat = new_first / bias_first
    second_hat = new_second / bias_second
    new_master = master - 0.01 * (first_hat / (jnp.sqrt(second_hat) + 1e-08) + 0.1 * master)
    new_replica = gathered_by_axis(new_master.astype(jnp.bfloat16), DP, (1, 0, 2), 0)
    return (grad_hidden, new_master, new_first, new_second, new_replica)


def solution(mesh):
    torus = Mesh(
        mesh.devices.reshape(16, 2, 2, 2, 8), ("dp_0", "dp_1", "dp_2", "tensor_0", "tensor_1")
    )
    placed = (
        P(DP, None),
        P(),
        P(None, TENSOR),
        P(TENSOR, None),
        P(DP, TENSOR),
        P(DP, TENSOR),
        P(DP, TENSOR),
        P(DP, TENSOR),
    )
    return jax.shard_map(
        local,
        mesh=torus,
        in_specs=placed,
        out_specs=(P(DP, TENSOR), P(DP, TENSOR), P(DP, TENSOR), P(DP, TENSOR), P(None, TENSOR)),
        check_vma=False,
    )
```

profile of v0, /device:TPU:6, one launch (start us, length us, event | category | flops | bytes accessed | tf_op | source)
XLA Modules:
  0.0 282.9 jit_solution(5527344269372160470)
XLA Ops:
  7.2 0.0 copy-start
  7.2 0.0 reduce-scatter.4.cloned.1.call-start
  7.2 1.4 fusion
  8.6 0.3 copy-done
  8.9 2.4 fusion.3
  11.3 2.2 copy.19
  13.6 0.0 reduce-scatter.4.cloned.1.call-update
  13.6 0.0 copy-start.3
  13.6 0.0 reduce-scatter.6.cloned.1.call-start
  13.7 33.4 %reduce-scatter.4.cloned.1.call-done = f32[32,8,2048]{2,1,0:T(8,128)} async-done(((f32[64,8,2048]{2,1,0:T(8,128)}), f32[32,8,2048]{2,1,0:T(8,128)}) %reduce-scatter.4.cloned.1.call-update) | async-done | bytes 2097168 | tf_op jit(solution)/shard_map/reduce_scatter | solution.py:52
  47.1 0.0 reduce-scatter.6.cloned.1.call-update
  47.1 0.0 reduce-scatter.8.cloned.1.call-start
  47.1 83.0 %reduce-scatter.6.cloned.1.call-done = f32[2,8,2048]{2,1,0:T(8,128)} async-done(((f32[32,8,2048]{2,1,0:T(8,128)}), f32[2,8,2048]{2,1,0:T(8,128)}) %reduce-scatter.6.cloned.1.call-update) | async-done | bytes 131088 | tf_op jit(solution)/shard_map/reduce_scatter | solution.py:52
  130.1 0.0 reduce-scatter.8.cloned.1.call-update
  130.1 0.0 all-gather.5.cloned.1.call-start
  130.2 22.8 %reduce-scatter.8.cloned.1.call-done = f32[1,8,2048]{2,1,0:T(8,128)} async-done(((f32[2,8,2048]{2,1,0:T(8,128)}), f32[1,8,2048]{2,1,0:T(8,128)}) %reduce-scatter.8.cloned.1.call-update) | async-done | bytes 65552 | tf_op jit(solution)/shard_map/reduce_scatter | solution.py:52
  153.0 1.5 fusion.16
  154.5 4.7 %all-gather.1 = bf16[16,2048]{1,0:T(8,128)(2,1)} all-gather(bf16[8,2048]{1,0:T(8,128)(2,1)S(1)} %get-tuple-element.5), channel_id=3, replica_groups=mesh['dp_0'=16,'dp_1'=2,'dp_2'=2,'tensor_0'=2,'tensor_1'=8] {'dp_1'}, dimensions={0}, use_global_device_ids=true | all-gather | bytes 98304 | tf_op jit(solution)/shard_map/all_gather | solution.py:36
  159.2 0.0 all-gather.5.cloned.1.call-update
  159.2 3.8 %fusion.19 = f32[512,512]{1,0:T(8,128)} fusion(bf16[512,2048]{1,0:T(8,128)(2,1)S(1)} %copy-done, bf16[512,2048]{1,0:T(8,128)(2,1)} %param.10), kind=kOutput, calls=%fused_computation.27 | convolution fusion | flops 1073741824 | bytes 5242880 | tf_op jit(solution)/shard_map/dot_general | solution.py:78
  163.1 9.9 %all-to-all-start = ((f32[16,32,512]{2,1,0:T(8,128)}), f32[16,32,512]{2,1,0:T(8,128)S(1)}, u32[]{:S(2)}, u32[]{:S(2)}) async-start(f32[16,32,512]{2,1,0:T(8,128)} %bitcast.33), calls=%async_computation | async-start | bytes 2097152 | tf_op jit(solution)/shard_map/all_to_all | solution.py:23
  172.9 0.0 all-gather.7.cloned.1.call-start
  173.0 62.7 %all-gather.5.cloned.1.call-done = bf16[32,8,2048]{2,1,0:T(8,128)(2,1)} async-done(((bf16[2,8,2048]{2,1,0:T(8,128)(2,1)}), bf16[32,8,2048]{2,1,0:T(8,128)(2,1)}) %all-gather.5.cloned.1.call-update) | async-done | bytes 1048592 | tf_op jit(solution)/shard_map/all_gather | solution.py:36
  235.7 0.0 all-gather.7.cloned.1.call-update
  235.7 0.9 fusion.13
  236.6 0.1 reduce_sum.37
  236.7 0.9 fusion.9
  237.6 0.8 fusion.12
  238.5 6.1 %all-gather = bf16[64,512]{1,0:T(8,128)(2,1)S(1)} all-gather(bf16[32,512]{1,0:T(8,128)(2,1)S(1)} %fusion.12), channel_id=2, replica_groups=mesh['dp_0'=16,'dp_1'=2,'dp_2'=2,'tensor_0'=2,'tensor_1'=8] {'tensor_0'}, dimensions={0}, use_global_device_ids=true | all-gather | bytes 98304 | tf_op jit(solution)/shard_map/all_gather | solution.py:36
  244.6 26.3 %all_gather.16 = bf16[16,32,512]{2,1,0:T(8,128)(2,1)S(1)} all-gather(bf16[2,32,512]{2,1,0:T(8,128)(2,1)S(1)} %bitcast.34), channel_id=1, replica_groups=mesh['dp_0'=16,'dp_1'=2,'dp_2'=2,'tensor_0'=2,'tensor_1'=8] {'tensor_1'}, dimensions={0}, use_global_device_ids=true | all-gather | bytes 589824 | tf_op jit(solution)/shard_map/all_gather | solution.py:36
  270.9 2.2 convolution_convert_fusion
  273.2 3.2 %copy.20 = bf16[16,2,2,8,2048]{4,3,2,1,0:T(8,128)(2,1)} copy(bf16[16,2,2,8,2048]{4,3,1,0,2:T(8,128)(2,1)} %bitcast.29) | data formatting | bytes 4194304 | tf_op jit(solution)/shard_map/transpose | solution.py:40
  (13 shorter events, 0.1 us)
Async XLA Ops:
  7.2 1.8 copy-start
  7.2 39.9 %reduce-scatter.4.cloned.1.call-start = ((), (), s32[]{:S(2)}) async-start(), calls=%async_computation.4 | async-start | bytes 6291456 | tf_op jit(solution)/shard_map/reduce_scatter | solution.py:52
  13.6 139.4 %copy-start.2 = (f32[8,2048]{1,0:T(8,128)S(1)}, f32[8,2048]{1,0:T(8,128)}, u32[]{:S(2)}) copy-start(f32[8,2048]{1,0:T(8,128)} %param.13) | copy-start | bytes 196612
  13.6 139.4 %copy-start.3 = (f32[8,2048]{1,0:T(8,128)S(1)}, f32[8,2048]{1,0:T(8,128)}, u32[]{:S(2)}) copy-start(f32[8,2048]{1,0:T(8,128)} %param.14) | copy-start | bytes 196612
  13.6 139.4 %copy-start.4 = (f32[8,2048]{1,0:T(8,128)S(1)}, f32[8,2048]{1,0:T(8,128)}, u32[]{:S(2)}) copy-start(f32[8,2048]{1,0:T(8,128)} %param.15) | copy-start | bytes 196612
  13.6 116.5 %reduce-scatter.6.cloned.1.call-start = ((), (), s32[]{:S(2)}) async-start(), calls=%async_computation.5 | async-start | bytes 2228224 | tf_op jit(solution)/shard_map/reduce_scatter | solution.py:52
  47.1 105.9 %reduce-scatter.8.cloned.1.call-start = ((), (), s32[]{:S(2)}) async-start(), calls=%async_computation.6 | async-start | bytes 196608 | tf_op jit(solution)/shard_map/reduce_scatter | solution.py:52
  130.1 105.6 %all-gather.5.cloned.1.call-start = ((), (), s32[]{:S(2)}) async-start(), calls=%async_computation.7 | async-start | bytes 1114112 | tf_op jit(solution)/shard_map/all_gather | solution.py:36
  163.1 73.6 %copy-start.1 = (f32[512]{0:T(512)S(1)}, f32[512]{0:T(512)}, u32[]{:S(2)}) copy-start(f32[512]{0:T(512)} %param.9) | copy-start | bytes 6148
  163.1 73.5 %all-to-all-start = ((f32[16,32,512]{2,1,0:T(8,128)}), f32[16,32,512]{2,1,0:T(8,128)S(1)}, u32[]{:S(2)}, u32[]{:S(2)}) async-start(f32[16,32,512]{2,1,0:T(8,128)} %bitcast.33), calls=%async_computation | async-start | bytes 2097152 | tf_op jit(solution)/shard_map/all_to_all | solution.py:23
  172.9 100.2 %all-gather.7.cloned.1.call-start = ((), (), s32[]{:S(2)}) async-start(), calls=%async_computation.8 | async-start | bytes 3145728 | tf_op jit(solution)/shard_map/all_gather | solution.py:36
Sparse Core Ops, SparseCore 0:
  13.7 33.3 reduce-scatter.3
  50.5 79.5 reduce-scatter.5
  133.4 19.5 reduce-scatter.7
  159.3 76.2 all-gather.4
  238.2 20.3 all-gather.6
where the time goes:
time: 284 us; the launch traced here: 283 us
  waiting for transfers between devices  202 us (71%)
  blocking collectives  37.1 us (13%)
  between operations  13.9 us (5%)
  starting transfers between devices  10 us (4%)
  matrix products  8.49 us (3%)
  local copies, waits for them, and re-layouts  5.76 us (2%)
  other arithmetic  5.66 us (2%)
    reduce_scatter x3, waiting for transfers between devices, own_block(): blocks = lax.psum_scatter(blocks, axes[k], scatter_dimension=0, tiled=True)  139 us
    all_gather x2, waiting for transfers between devices, all_blocks(): blocks = lax.all_gather(blocks, axes[k], axis=0, tiled=True)  62.7 us
    all_gather x3, blocking collectives, all_blocks(): blocks = lax.all_gather(blocks, axes[k], axis=0, tiled=True)  37.1 us
    all_to_all x1, starting transfers between devices, sum_at_owner(): blocks = lax.all_to_all(split_up(x, dim, devices), axis, 0, 0, tiled=True)  9.85 us
  transfers between devices with their start and end apart: 6, of which 4 were waited for; matrix products, arithmetic and copies ran while one was open for 3% of the time, Pallas kernels for 0%

commit v1 on v0

v1 whole, which is shorter than its diff:
```python
import jax
import jax.numpy as jnp
from jax import lax
from jax.sharding import Mesh
from jax.sharding import PartitionSpec as P

Z = ("zh", "zl")
TENSOR = ("xh", "y")
DP = ("zh", "zl", "xl", "c")
SWAP = [(0, 1), (1, 0)]

bias_first = 0.9999734386011124
bias_second = 0.09520785288629112

F32 = jnp.float32
BF16 = jnp.bfloat16


def at(x, index, dim):
    return lax.dynamic_index_in_dim(x, index, dim, keepdims=False)


def reduce_pair(x, axis, dim):
    me = lax.axis_index(axis)
    got = lax.ppermute(at(x, 1 - me, dim).astype(BF16), axis, SWAP)
    return at(x, me, dim).astype(F32) + got.astype(F32)


def gather_pair(x, axis, dim):
    me = lax.axis_index(axis)
    got = lax.ppermute(x, axis, SWAP)
    first = jnp.where(me == 0, x, got)
    second = jnp.where(me == 0, got, x)
    return jnp.stack([first, second], axis=dim)


def to_all(x, axis):
    n = lax.axis_size(axis)
    return lax.all_to_all(jnp.broadcast_to(x[None], (n, *x.shape)), axis, 0, 0, tiled=True)


def norm_backward(latent_rows, norm_gain, grad_rows):
    values = latent_rows.astype(F32)
    inverse_rms = lax.rsqrt(jnp.mean(values * values, axis=1, keepdims=True) + 1e-06)
    unit = values * inverse_rms
    scaled = grad_rows * norm_gain
    inner = jnp.mean(scaled * unit, axis=1, keepdims=True)
    return (inverse_rms * (scaled - unit * inner)).astype(BF16)


def local(
    latent_pre, norm_gain, kv_weight, down_weight, grad_kv, master, first_moment, second_moment
):
    values = latent_pre.astype(F32)
    inverse_rms = lax.rsqrt(jnp.mean(values * values, axis=1, keepdims=True) + 1e-06)
    normalized = (values * inverse_rms * norm_gain).astype(BF16)
    cols = grad_kv.shape[1]
    half = cols // 2
    zh, zl, xl, c = (lax.axis_size(a) for a in DP)
    part = lax.dot_general(
        normalized, grad_kv, (((0,), (0,)), ((), ())), preferred_element_type=F32
    )
    rows = part.shape[0] // (zh * zl * xl * c)
    part = part.reshape(zh, zl, xl, c, rows, cols)
    part = reduce_pair(part, "c", 3)
    grad_part = lax.dot_general(
        grad_kv, kv_weight, (((1,), (1,)), ((), ())), preferred_element_type=F32
    )
    share = grad_part.shape[0] // lax.axis_size(TENSOR)
    blocks = lax.all_to_all(
        grad_part.reshape(-1, share, grad_part.shape[1]), TENSOR, 0, 0, tiled=True
    )
    grad_share = jnp.sum(blocks, axis=0)
    own_start = lax.axis_index(TENSOR) * share
    latent_share = lax.dynamic_slice_in_dim(latent_pre, own_start, share, 0)
    pre_share = norm_backward(latent_share, norm_gain, grad_share)
    grad_pre = to_all(pre_share, TENSOR).reshape(latent_pre.shape)
    grad_hidden = lax.dot_general(
        grad_pre, down_weight, (((1,), (1,)), ((), ())), preferred_element_type=F32
    ).astype(BF16)
    p = part[..., :half]
    q = part[..., half:]
    p = reduce_pair(p, "xl", 2)
    q = reduce_pair(q, "zl", 1)
    p = reduce_pair(p, "zl", 1)
    q = reduce_pair(q, "xl", 1)
    both = jnp.concatenate([p.astype(BF16), q.astype(BF16)], axis=-1)
    both = lax.all_to_all(both, "zh", 0, 0, tiled=True)
    weight_grad = jnp.sum(both.astype(F32), axis=0)
    new_first = 0.9 * first_moment + 0.1 * weight_grad
    new_second = 0.999 * second_moment + 0.001 * weight_grad * weight_grad
    first_hat = new_first / bias_first
    second_hat = new_second / bias_second
    new_master = master - 0.01 * (first_hat / (jnp.sqrt(second_hat) + 1e-08) + 0.1 * master)
    rep = to_all(new_master.astype(BF16), "zh")
    p = gather_pair(rep[..., :half], "zl", 1)
    q = gather_pair(rep[..., half:], "xl", 1)
    p = gather_pair(p, "xl", 2)
    q = gather_pair(q, "zl", 1)
    both = jnp.concatenate([p, q], axis=-1)
    new_replica = gather_pair(both, "c", 3).reshape(-1, cols)
    return (grad_hidden, new_master, new_first, new_second, new_replica)


def solution(mesh):
    torus = Mesh(mesh.devices.reshape(8, 2, 2, 2, 2, 8), ("zh", "zl", "xl", "c", "xh", "y"))
    placed = (
        P(DP, None),
        P(),
        P(None, TENSOR),
        P(TENSOR, None),
        P(DP, TENSOR),
        P(DP, TENSOR),
        P(DP, TENSOR),
        P(DP, TENSOR),
    )
    return jax.shard_map(
        local,
        mesh=torus,
        in_specs=placed,
        out_specs=(P(DP, TENSOR), P(DP, TENSOR), P(DP, TENSOR), P(DP, TENSOR), P(None, TENSOR)),
        check_vma=False,
    )
```

time: 284 us -> 179 us (0.63)
  waiting for transfers between devices: 202 us -> 72.4 us
  starting transfers between devices: 10 us -> 71.7 us
  blocking collectives: 37.1 us -> 0 us
  between operations: 13.9 us -> 0.98 us
  other arithmetic: 5.66 us -> 16.3 us
    reduce_scatter x3 -> x0, waiting for transfers between devices: 139 us -> none  [own_block(): blocks = lax.psum_scatter(blocks, axes[k], scatter_dimension=0, tiled=True)]
    all_gather x2 -> x0, waiting for transfers between devices: 62.7 us -> none  [all_blocks(): blocks = lax.all_gather(blocks, axes[k], axis=0, tiled=True)]
    all_to_all x1 -> x4, waiting for transfers between devices: 0.01 us -> 56.7 us  [the longest x2 22.5 us: to_all(): lax.all_to_all(jnp.broadcast_to(x[None], (n, *x.shape)), axis, 0, 0, tile...]
    all_gather x3 -> x0, blocking collectives: 37.1 us -> none  [all_blocks(): blocks = lax.all_gather(blocks, axes[k], axis=0, tiled=True)]
    all_to_all x1 -> x4, starting transfers between devices: 9.85 us -> 42.5 us  [the longest x1 17.9 us: local(): both = lax.all_to_all(both, 'zh', 0, 0, tiled=True)]
    ppermute x0 -> x10, starting transfers between devices: none -> 29.3 us  [the longest x5 15.9 us: reduce_pair(): got = lax.ppermute(at(x, 1 - me, dim).astype(BF16), axis, SWAP)]
    ppermute x0 -> x10, waiting for transfers between devices: none -> 15.7 us  [the longest x5 10.2 us: reduce_pair(): got = lax.ppermute(at(x, 1 - me, dim).astype(BF16), axis, SWAP)]
    another operation x0 -> x7, other arithmetic: none -> 5.45 us  [gather_pair(): return jnp.stack([first, second], axis=dim)]
  transfers between devices with their start and end apart: 6 -> 14, of which waited for: 4 -> 10; matrix products, arithmetic and copies ran while one was open for 3% -> 9% of each run, Pallas kernels for 0% -> 0%
where the time goes in v1:
time: 179 us; the launch traced here: 176 us
  waiting for transfers between devices  72.4 us (40%)
  starting transfers between devices  71.7 us (40%)
  other arithmetic  16.3 us (9%)
  matrix products  8.65 us (5%)
  local copies, waits for them, and re-layouts  6 us (3%)
    all_to_all x2, waiting for transfers between devices, to_all(): lax.all_to_all(jnp.broadcast_to(x[None], (n, *x.shape)), axis, 0, 0, tile...  22.5 us
    all_to_all x1, waiting for transfers between devices, local(): lax.all_to_all(grad_part.reshape(-1, share, grad_part.shape[1]), TENSOR,...  19.1 us
    all_to_all x1, starting transfers between devices, local(): both = lax.all_to_all(both, 'zh', 0, 0, tiled=True)  17.9 us
    ppermute x5, starting transfers between devices, reduce_pair(): got = lax.ppermute(at(x, 1 - me, dim).astype(BF16), axis, SWAP)  15.9 us
    all_to_all x1, waiting for transfers between devices, local(): both = lax.all_to_all(both, 'zh', 0, 0, tiled=True)  15.1 us
    all_to_all x2, starting transfers between devices, to_all(): lax.all_to_all(jnp.broadcast_to(x[None], (n, *x.shape)), axis, 0, 0, tile...  14.4 us
    ppermute x5, starting transfers between devices, gather_pair(): got = lax.ppermute(x, axis, SWAP)  13.3 us
    all_to_all x1, starting transfers between devices, local(): lax.all_to_all(grad_part.reshape(-1, share, grad_part.shape[1]), TENSOR,...  10.2 us
  transfers between devices with their start and end apart: 14, of which 10 were waited for; matrix products, arithmetic and copies ran while one was open for 9% of the time, Pallas kernels for 0%

profile of v1, /device:TPU:6, one launch (start us, length us, event | category | flops | bytes accessed | tf_op | source)
XLA Modules:
  0.0 176.1 jit_solution(11375625956757781871)
XLA Ops:
  0.7 1.4 fusion
  2.4 2.4 %fusion.4 = f32[512,2048]{1,0:T(8,128)S(1)} fusion(bf16[512,2048]{1,0:T(8,128)(2,1)S(1)} %copy-done, bf16[512,512]{1,0:T(8,128)(2,1)} %param.8, f32[512]{0:T(512)} %param.9, f32[512]{0:T(512)S(1)} %add_rsqrt_fusion), kind=kOutput, calls=%fused_computation.13 | convolution fusion | flops 1074790400 | bytes 6819840 | tf_op jit(solution)/shard_map/dot_general | solution.py:60
  4.8 1.9 %copy-done.1 = f32[512,2048]{1,0:T(8,128)} copy-done((f32[512,2048]{1,0:T(8,128)}, f32[512,2048]{1,0:T(8,128)S(1)}, u32[]{:S(2)}) %copy-start.1) | copy-done | bytes 4194328
  6.9 1.9 %collective-permute-start = (bf16[8,2,2,8,2048]{4,3,2,1,0:T(8,128)(2,1)S(1)}, bf16[8,2,2,8,2048]{4,3,2,1,0:T(8,128)(2,1)}, u32[]{:S(2)}, u32[]{:S(2)}) collective-permute-start(bf16[8,2,2,8,2048]{4,3,2,1,0:T(8,128)(2,1)S(1)} %fusion.3), channel_id=1, source_target_pairs={{0,16},{16,0},{1,17},{17,1},{2,18},{18,2},{3,19},{19,3},{4,20},{20... | collective-permute-start | bytes 3145736 | tf_op jit(solution)/shard_map/ppermute | solution.py:25
  8.9 2.8 %collective-permute-done = bf16[8,2,2,8,2048]{4,3,2,1,0:T(8,128)(2,1)} collective-permute-done((bf16[8,2,2,8,2048]{4,3,2,1,0:T(8,128)(2,1)S(1)}, bf16[8,2,2,8,2048]{4,3,2,1,0:T(8,128)(2,1)}, u32[]{:S(2)}, u32[]{:S(2)}) %collective-permute-start) | collective-permute-done | bytes 1048608 | tf_op jit(solution)/shard_map/ppermute | solution.py:25
  11.6 2.2 %bitcast_add_fusion = f32[8,2,2,8,2048]{4,3,2,1,0:T(8,128)S(1)} fusion(bf16[8,2,2,8,2048]{4,3,2,1,0:T(8,128)(2,1)} %collective-permute-done, f32[8,2,2,2,8,2048]{5,4,3,2,1,0:T(8,128)} %bitcast.62, s32[]{:T(128)S(6)} %select_n.86), kind=kLoop, calls=%fused_computation.1 | loop fusion | flops 1048576 | bytes 5242884 | tf_op jit(solution)/shard_map/add | solution.py:26
  15.7 2.7 %collective-permute-start.1 = (bf16[8,2,8,1024]{3,2,0,1:T(8,128)(2,1)}, bf16[8,2,8,1024]{3,2,0,1:T(8,128)(2,1)S(1)}, u32[]{:S(2)}, u32[]{:S(2)}) collective-permute-start(bf16[8,2,8,1024]{3,2,0,1:T(8,128)(2,1)} %fusion.10), channel_id=1, source_target_pairs={{0,32},{32,0},{1,33},{33,1},{2,34},{34,2},{3,35},{35,3},{4,36},{36... | collective-permute-start | bytes 786440 | tf_op jit(solution)/shard_map/ppermute | solution.py:25
  18.4 4.3 %collective-permute-start.3 = (bf16[8,2,8,1024]{3,2,1,0:T(8,128)(2,1)S(1)}, bf16[8,2,8,1024]{3,2,1,0:T(8,128)(2,1)S(1)}, u32[]{:S(2)}, u32[]{:S(2)}) collective-permute-start(bf16[8,2,8,1024]{3,2,1,0:T(8,128)(2,1)S(1)} %fusion.9), channel_id=1, source_target_pairs={{0,64},{64,0},{1,65},{65,1},{2,66},{66,2},{3,67},{67,3},{4,68},{68... | collective-permute-start | bytes 786440 | tf_op jit(solution)/shard_map/ppermute | solution.py:25
  22.7 3.4 %collective-permute-done.1 = bf16[8,2,8,1024]{3,2,0,1:T(8,128)(2,1)S(1)} collective-permute-done((bf16[8,2,8,1024]{3,2,0,1:T(8,128)(2,1)}, bf16[8,2,8,1024]{3,2,0,1:T(8,128)(2,1)S(1)}, u32[]{:S(2)}, u32[]{:S(2)}) %collective-permute-start.1) | collective-permute-done | bytes 262176 | tf_op jit(solution)/shard_map/ppermute | solution.py:25
  27.2 4.3 %collective-permute-start.2 = (bf16[8,8,1024]{2,1,0:T(8,128)(2,1)S(1)}, bf16[8,8,1024]{2,1,0:T(8,128)(2,1)S(1)}, u32[]{:S(2)}, u32[]{:S(2)}) collective-permute-start(bf16[8,8,1024]{2,1,0:T(8,128)(2,1)S(1)} %fusion.13), channel_id=1, source_target_pairs={{0,64},{64,0},{1,65},{65,1},{2,66},{66,2},{3,67},{67,3},{4,68},{68... | collective-permute-start | bytes 393224 | tf_op jit(solution)/shard_map/ppermute | solution.py:25
  31.6 2.7 %collective-permute-start.4 = (bf16[8,8,1024]{2,1,0:T(8,128)(2,1)S(1)}, bf16[8,8,1024]{2,1,0:T(8,128)(2,1)S(1)}, u32[]{:S(2)}, u32[]{:S(2)}) collective-permute-start(bf16[8,8,1024]{2,1,0:T(8,128)(2,1)S(1)} %fusion.14), channel_id=1, source_target_pairs={{0,32},{32,0},{1,33},{33,1},{2,34},{34,2},{3,35},{35,3},{4,36},{36... | collective-permute-start | bytes 393224 | tf_op jit(solution)/shard_map/ppermute | solution.py:25
  34.5 4.0 %collective-permute-done.4 = bf16[8,8,1024]{2,1,0:T(8,128)(2,1)S(1)} collective-permute-done((bf16[8,8,1024]{2,1,0:T(8,128)(2,1)S(1)}, bf16[8,8,1024]{2,1,0:T(8,128)(2,1)S(1)}, u32[]{:S(2)}, u32[]{:S(2)}) %collective-permute-start.4) | collective-permute-done | bytes 131104 | tf_op jit(solution)/shard_map/ppermute | solution.py:25
  39.3 17.9 %all-to-all-start.2 = ((bf16[8,8,2048]{2,1,0:T(8,128)(2,1)}), bf16[8,8,2048]{2,1,0:T(8,128)(2,1)S(1)}, u32[]{:S(2)}, u32[]{:S(2)}) async-start(bf16[8,8,2048]{2,1,0:T(8,128)(2,1)} %pad_maximum_fusion.2), calls=%async_computation.2 | async-start | bytes 524288 | tf_op jit(solution)/shard_map/all_to_all | solution.py:88
  57.1 3.8 %fusion.27 = f32[512,512]{1,0:T(8,128)} fusion(bf16[512,2048]{1,0:T(8,128)(2,1)S(1)} %copy-done, bf16[512,2048]{1,0:T(8,128)(2,1)} %param.10), kind=kOutput, calls=%fused_computation.65 | convolution fusion | flops 1073741824 | bytes 5242880 | tf_op jit(solution)/shard_map/dot_general | solution.py:66
  60.9 15.1 %all-to-all-done.2 = bf16[8,8,2048]{2,1,0:T(8,128)(2,1)S(1)} async-done(((bf16[8,8,2048]{2,1,0:T(8,128)(2,1)}), bf16[8,8,2048]{2,1,0:T(8,128)(2,1)S(1)}, u32[]{:S(2)}, u32[]{:S(2)}) %all-to-all-start.2) | async-done | bytes 262176 | tf_op jit(solution)/shard_map/all_to_all | solution.py:88
  76.1 10.2 %all-to-all-start = ((f32[16,32,512]{2,1,0:T(8,128)}), f32[16,32,512]{2,1,0:T(8,128)S(1)}, u32[]{:S(2)}, u32[]{:S(2)}) async-start(f32[16,32,512]{2,1,0:T(8,128)} %bitcast.64), calls=%async_computation | async-start | bytes 2097152 | tf_op jit(solution)/shard_map/all_to_all | solution.py:70
  86.3 1.5 fusion.23
  87.9 19.1 %all-to-all-done = f32[16,32,512]{2,1,0:T(8,128)S(1)} async-done(((f32[16,32,512]{2,1,0:T(8,128)}), f32[16,32,512]{2,1,0:T(8,128)S(1)}, u32[]{:S(2)}, u32[]{:S(2)}) %all-to-all-start) | async-done | bytes 1048608 | tf_op jit(solution)/shard_map/all_to_all | solution.py:70
  107.7 5.6 %all-to-all-start.3 = ((bf16[8,8,2048]{2,1,0:T(8,128)(2,1)}), bf16[8,8,2048]{2,1,0:T(8,128)(2,1)S(1)}, u32[]{:S(2)}, u32[]{:S(2)}) async-start(bf16[8,8,2048]{2,1,0:T(8,128)(2,1)} %broadcast_in_dim.5), calls=%async_computation.3 | async-start | bytes 524288 | tf_op jit(solution)/shard_map/all_to_all | solution.py:39
  115.2 16.1 %all-to-all-done.3 = bf16[8,8,2048]{2,1,0:T(8,128)(2,1)S(1)} async-done(((bf16[8,8,2048]{2,1,0:T(8,128)(2,1)}), bf16[8,8,2048]{2,1,0:T(8,128)(2,1)S(1)}, u32[]{:S(2)}, u32[]{:S(2)}) %all-to-all-start.3) | async-done | bytes 262176 | tf_op jit(solution)/shard_map/all_to_all | solution.py:39
  131.3 1.9 %collective-permute-start.5 = (bf16[8,8,1024]{2,1,0:T(8,128)(2,1)S(1)}, bf16[8,8,1024]{2,1,0:T(8,128)(2,1)S(1)}, u32[]{:S(2)}, u32[]{:S(2)}) collective-permute-start(bf16[8,8,1024]{2,1,0:T(8,128)(2,1)S(1)} %get-tuple-element.23), channel_id=1, source_target_pairs={{0,64},{64,0},{1,65},{65,1},{2,66},{66,2},{3,67},{67,3},{4,68},{68... | collective-permute-start | bytes 393224 | tf_op jit(solution)/shard_map/ppermute | solution.py:31
  133.3 2.7 %collective-permute-start.7 = (bf16[8,8,1024]{2,1,0:T(8,128)(2,1)S(1)}, bf16[8,8,1024]{2,1,0:T(8,128)(2,1)S(1)}, u32[]{:S(2)}, u32[]{:S(2)}) collective-permute-start(bf16[8,8,1024]{2,1,0:T(8,128)(2,1)S(1)} %get-tuple-element.24), channel_id=1, source_target_pairs={{0,32},{32,0},{1,33},{33,1},{2,34},{34,2},{3,35},{35,3},{4,36},{36... | collective-permute-start | bytes 393224 | tf_op jit(solution)/shard_map/ppermute | solution.py:31
  136.0 2.2 %collective-permute-done.5 = bf16[8,8,1024]{2,1,0:T(8,128)(2,1)S(1)} collective-permute-done((bf16[8,8,1024]{2,1,0:T(8,128)(2,1)S(1)}, bf16[8,8,1024]{2,1,0:T(8,128)(2,1)S(1)}, u32[]{:S(2)}, u32[]{:S(2)}) %collective-permute-start.5) | collective-permute-done | bytes 131104 | tf_op jit(solution)/shard_map/ppermute | solution.py:31
  138.2 3.3 %collective-permute-done.7 = bf16[8,8,1024]{2,1,0:T(8,128)(2,1)S(1)} collective-permute-done((bf16[8,8,1024]{2,1,0:T(8,128)(2,1)S(1)}, bf16[8,8,1024]{2,1,0:T(8,128)(2,1)S(1)}, u32[]{:S(2)}, u32[]{:S(2)}) %collective-permute-start.7) | collective-permute-done | bytes 131104 | tf_op jit(solution)/shard_map/ppermute | solution.py:31
  141.6 2.7 %collective-permute-start.6 = (bf16[8,2,8,1024]{3,2,0,1:T(8,128)(2,1)S(1)}, bf16[8,2,8,1024]{3,2,0,1:T(8,128)(2,1)}, u32[]{:S(2)}, u32[]{:S(2)}) collective-permute-start(bf16[8,2,8,1024]{3,2,0,1:T(8,128)(2,1)S(1)} %pad_maximum_fusion.3), channel_id=1, source_target_pairs={{0,32},{32,0},{1,33},{33,1},{2,34},{34,2},{3,35},{35,3},{4,36},{36... | collective-permute-start | bytes 786440 | tf_op jit(solution)/shard_map/ppermute | solution.py:31
  144.4 4.1 %collective-permute-start.8 = (bf16[8,2,8,1024]{3,2,1,0:T(8,128)(2,1)S(1)}, bf16[8,2,8,1024]{3,2,1,0:T(8,128)(2,1)}, u32[]{:S(2)}, u32[]{:S(2)}) collective-permute-start(bf16[8,2,8,1024]{3,2,1,0:T(8,128)(2,1)S(1)} %pad_maximum_fusion.4), channel_id=1, source_target_pairs={{0,64},{64,0},{1,65},{65,1},{2,66},{66,2},{3,67},{67,3},{4,68},{68... | collective-permute-start | bytes 786440 | tf_op jit(solution)/shard_map/ppermute | solution.py:31
  150.2 8.8 %all-to-all-start.1 = ((bf16[16,32,512]{2,1,0:T(8,128)(2,1)}), bf16[16,32,512]{2,1,0:T(8,128)(2,1)}, u32[]{:S(2)}, u32[]{:S(2)}) async-start(bf16[16,32,512]{2,1,0:T(8,128)(2,1)} %broadcast_in_dim.4), calls=%async_computation.1 | async-start | bytes 1048576 | tf_op jit(solution)/shard_map/all_to_all | solution.py:39
  162.1 1.9 %collective-permute-start.9 = (bf16[8,2,2,8,2048]{4,3,2,1,0:T(8,128)(2,1)}, bf16[8,2,2,8,2048]{4,3,2,1,0:T(8,128)(2,1)}, u32[]{:S(2)}, u32[]{:S(2)}) collective-permute-start(bf16[8,2,2,8,2048]{4,3,2,1,0:T(8,128)(2,1)} %maximum_maximum_fusion), channel_id=1, source_target_pairs={{0,16},{16,0},{1,17},{17,1},{2,18},{18,2},{3,19},{19,3},{4,20},{20... | collective-permute-start | bytes 3145736 | tf_op jit(solution)/shard_map/ppermute | solution.py:31
  164.0 6.3 %all-to-all-done.1 = bf16[16,32,512]{2,1,0:T(8,128)(2,1)} async-done(((bf16[16,32,512]{2,1,0:T(8,128)(2,1)}), bf16[16,32,512]{2,1,0:T(8,128)(2,1)}, u32[]{:S(2)}, u32[]{:S(2)}) %all-to-all-start.1) | async-done | bytes 524320 | tf_op jit(solution)/shard_map/all_to_all | solution.py:39
  170.4 2.4 %convolution_convert_fusion = bf16[512,448]{0,1:T(8,128)(2,1)} fusion(bf16[512,512]{1,0:T(8,128)(2,1)} %bitcast.1, bf16[448,512]{1,0:T(8,128)(2,1)} %param.11), kind=kOutput, calls=%fused_computation.5 | convolution fusion | flops 235110400 | bytes 1441792 | tf_op jit(solution)/shard_map/dot_general | solution.py:78
  172.8 1.9 %select_bitcast_fusion.1 = (bf16[8,2,2,1,8,2048]{5,4,3,2,1,0:T(8,128)(2,1)S(1)}, bf16[8,2,2,1,8,2048]{5,4,3,2,1,0:T(8,128)(2,1)S(1)}) fusion(bf16[8,2,2,8,2048]{4,3,2,1,0:T(8,128)(2,1)} %collective-permute-done.9, pred[]{:T(512)S(6)} %eq.6, bf16[8,1,2,8,1024]{4,3,2,1,0:T(8,128)(2,1)S(1)} %get-tuple-element.16, ...), kind=kLoop, calls=%fused_computation.12 | loop fusion | flops 4456448 | bytes 4194305 | tf_op jit(solution)/shard_map/stack | solution.py:34
  174.6 1.5 pad_maximum_fusion
  (48 shorter events, 12.0 us)
Async XLA Ops:
  0.6 1.8 copy-start
  4.8 2.0 %copy-start.1 = (f32[512,2048]{1,0:T(8,128)}, f32[512,2048]{1,0:T(8,128)S(1)}, u32[]{:S(2)}) copy-start(f32[512,2048]{1,0:T(8,128)S(1)} %fusion.4) | copy-start | bytes 12582916
  6.9 4.7 %collective-permute-start = (bf16[8,2,2,8,2048]{4,3,2,1,0:T(8,128)(2,1)S(1)}, bf16[8,2,2,8,2048]{4,3,2,1,0:T(8,128)(2,1)}, u32[]{:S(2)}, u32[]{:S(2)}) collective-permute-start(bf16[8,2,2,8,2048]{4,3,2,1,0:T(8,128)(2,1)S(1)} %fusion.3), channel_id=1, source_target_pairs={{0,16},{16,0},{1,17},{17,1},{2,18},{18,2},{3,19},{19,3},{4,20},{20... | collective-permute-start | bytes 3145736 | tf_op jit(solution)/shard_map/ppermute | solution.py:25
  13.9 1.0 copy-start.2
  15.7 10.4 %collective-permute-start.1 = (bf16[8,2,8,1024]{3,2,0,1:T(8,128)(2,1)}, bf16[8,2,8,1024]{3,2,0,1:T(8,128)(2,1)S(1)}, u32[]{:S(2)}, u32[]{:S(2)}) collective-permute-start(bf16[8,2,8,1024]{3,2,0,1:T(8,128)(2,1)} %fusion.10), channel_id=1, source_target_pairs={{0,32},{32,0},{1,33},{33,1},{2,34},{34,2},{3,35},{35,3},{4,36},{36... | collective-permute-start | bytes 786440 | tf_op jit(solution)/shard_map/ppermute | solution.py:25
  18.4 13.1 %collective-permute-start.3 = (bf16[8,2,8,1024]{3,2,1,0:T(8,128)(2,1)S(1)}, bf16[8,2,8,1024]{3,2,1,0:T(8,128)(2,1)S(1)}, u32[]{:S(2)}, u32[]{:S(2)}) collective-permute-start(bf16[8,2,8,1024]{3,2,1,0:T(8,128)(2,1)S(1)} %fusion.9), channel_id=1, source_target_pairs={{0,64},{64,0},{1,65},{65,1},{2,66},{66,2},{3,67},{67,3},{4,68},{68... | collective-permute-start | bytes 786440 | tf_op jit(solution)/shard_map/ppermute | solution.py:25
  27.2 7.2 %collective-permute-start.2 = (bf16[8,8,1024]{2,1,0:T(8,128)(2,1)S(1)}, bf16[8,8,1024]{2,1,0:T(8,128)(2,1)S(1)}, u32[]{:S(2)}, u32[]{:S(2)}) collective-permute-start(bf16[8,8,1024]{2,1,0:T(8,128)(2,1)S(1)} %fusion.13), channel_id=1, source_target_pairs={{0,64},{64,0},{1,65},{65,1},{2,66},{66,2},{3,67},{67,3},{4,68},{68... | collective-permute-start | bytes 393224 | tf_op jit(solution)/shard_map/ppermute | solution.py:25
  31.6 6.9 %collective-permute-start.4 = (bf16[8,8,1024]{2,1,0:T(8,128)(2,1)S(1)}, bf16[8,8,1024]{2,1,0:T(8,128)(2,1)S(1)}, u32[]{:S(2)}, u32[]{:S(2)}) collective-permute-start(bf16[8,8,1024]{2,1,0:T(8,128)(2,1)S(1)} %fusion.14), channel_id=1, source_target_pairs={{0,32},{32,0},{1,33},{33,1},{2,34},{34,2},{3,35},{35,3},{4,36},{36... | collective-permute-start | bytes 393224 | tf_op jit(solution)/shard_map/ppermute | solution.py:25
  39.3 36.8 %all-to-all-start.2 = ((bf16[8,8,2048]{2,1,0:T(8,128)(2,1)}), bf16[8,8,2048]{2,1,0:T(8,128)(2,1)S(1)}, u32[]{:S(2)}, u32[]{:S(2)}) async-start(bf16[8,8,2048]{2,1,0:T(8,128)(2,1)} %pad_maximum_fusion.2), calls=%async_computation.2 | async-start | bytes 524288 | tf_op jit(solution)/shard_map/all_to_all | solution.py:88
  60.9 25.4 %copy-start.6 = (f32[8,2048]{1,0:T(8,128)S(1)}, f32[8,2048]{1,0:T(8,128)}, u32[]{:S(2)}) copy-start(f32[8,2048]{1,0:T(8,128)} %param.13) | copy-start | bytes 196612
  60.9 25.4 %copy-start.7 = (f32[8,2048]{1,0:T(8,128)S(1)}, f32[8,2048]{1,0:T(8,128)}, u32[]{:S(2)}) copy-start(f32[8,2048]{1,0:T(8,128)} %param.14) | copy-start | bytes 196612
  76.1 38.2 %copy-start.5 = (f32[512]{0:T(512)S(1)}, f32[512]{0:T(512)}, u32[]{:S(2)}) copy-start(f32[512]{0:T(512)} %param.9) | copy-start | bytes 6148
  76.1 30.9 %all-to-all-start = ((f32[16,32,512]{2,1,0:T(8,128)}), f32[16,32,512]{2,1,0:T(8,128)S(1)}, u32[]{:S(2)}, u32[]{:S(2)}) async-start(f32[16,32,512]{2,1,0:T(8,128)} %bitcast.64), calls=%async_computation | async-start | bytes 2097152 | tf_op jit(solution)/shard_map/all_to_all | solution.py:70
  107.7 23.6 %all-to-all-start.3 = ((bf16[8,8,2048]{2,1,0:T(8,128)(2,1)}), bf16[8,8,2048]{2,1,0:T(8,128)(2,1)S(1)}, u32[]{:S(2)}, u32[]{:S(2)}) async-start(bf16[8,8,2048]{2,1,0:T(8,128)(2,1)} %broadcast_in_dim.5), calls=%async_computation.3 | async-start | bytes 524288 | tf_op jit(solution)/shard_map/all_to_all | solution.py:39
  131.3 6.9 %collective-permute-start.5 = (bf16[8,8,1024]{2,1,0:T(8,128)(2,1)S(1)}, bf16[8,8,1024]{2,1,0:T(8,128)(2,1)S(1)}, u32[]{:S(2)}, u32[]{:S(2)}) collective-permute-start(bf16[8,8,1024]{2,1,0:T(8,128)(2,1)S(1)} %get-tuple-element.23), channel_id=1, source_target_pairs={{0,64},{64,0},{1,65},{65,1},{2,66},{66,2},{3,67},{67,3},{4,68},{68... | collective-permute-start | bytes 393224 | tf_op jit(solution)/shard_map/ppermute | solution.py:31
  133.3 8.3 %collective-permute-start.7 = (bf16[8,8,1024]{2,1,0:T(8,128)(2,1)S(1)}, bf16[8,8,1024]{2,1,0:T(8,128)(2,1)S(1)}, u32[]{:S(2)}, u32[]{:S(2)}) collective-permute-start(bf16[8,8,1024]{2,1,0:T(8,128)(2,1)S(1)} %get-tuple-element.24), channel_id=1, source_target_pairs={{0,32},{32,0},{1,33},{33,1},{2,34},{34,2},{3,35},{35,3},{4,36},{36... | collective-permute-start | bytes 393224 | tf_op jit(solution)/shard_map/ppermute | solution.py:31
  141.6 2.8 %copy-start.3 = (bf16[8,1,8,1024]{3,2,1,0:T(8,128)(2,1)}, bf16[8,1,8,1024]{3,2,1,0:T(8,128)(2,1)S(1)}, u32[]{:S(2)}) copy-start(bf16[8,1,8,1024]{3,2,1,0:T(8,128)(2,1)S(1)} %get-tuple-element.22) | copy-start | bytes 393220
  141.6 17.4 %collective-permute-start.6 = (bf16[8,2,8,1024]{3,2,0,1:T(8,128)(2,1)S(1)}, bf16[8,2,8,1024]{3,2,0,1:T(8,128)(2,1)}, u32[]{:S(2)}, u32[]{:S(2)}) collective-permute-start(bf16[8,2,8,1024]{3,2,0,1:T(8,128)(2,1)S(1)} %pad_maximum_fusion.3), channel_id=1, source_target_pairs={{0,32},{32,0},{1,33},{33,1},{2,34},{34,2},{3,35},{35,3},{4,36},{36... | collective-permute-start | bytes 786440 | tf_op jit(solution)/shard_map/ppermute | solution.py:31
  144.4 15.6 %copy-start.4 = (bf16[8,1,8,1024]{3,2,1,0:T(8,128)(2,1)S(1)}, bf16[8,1,8,1024]{3,2,1,0:T(8,128)(2,1)}, u32[]{:S(2)}) copy-start(bf16[8,1,8,1024]{3,2,1,0:T(8,128)(2,1)} %copy-done.3) | copy-start | bytes 393220
  144.4 15.6 %collective-permute-start.8 = (bf16[8,2,8,1024]{3,2,1,0:T(8,128)(2,1)S(1)}, bf16[8,2,8,1024]{3,2,1,0:T(8,128)(2,1)}, u32[]{:S(2)}, u32[]{:S(2)}) collective-permute-start(bf16[8,2,8,1024]{3,2,1,0:T(8,128)(2,1)S(1)} %pad_maximum_fusion.4), channel_id=1, source_target_pairs={{0,64},{64,0},{1,65},{65,1},{2,66},{66,2},{3,67},{67,3},{4,68},{68... | collective-permute-start | bytes 786440 | tf_op jit(solution)/shard_map/ppermute | solution.py:31
  150.2 20.2 %all-to-all-start.1 = ((bf16[16,32,512]{2,1,0:T(8,128)(2,1)}), bf16[16,32,512]{2,1,0:T(8,128)(2,1)}, u32[]{:S(2)}, u32[]{:S(2)}) async-start(bf16[16,32,512]{2,1,0:T(8,128)(2,1)} %broadcast_in_dim.4), calls=%async_computation.1 | async-start | bytes 1048576 | tf_op jit(solution)/shard_map/all_to_all | solution.py:39
  162.1 10.7 %collective-permute-start.9 = (bf16[8,2,2,8,2048]{4,3,2,1,0:T(8,128)(2,1)}, bf16[8,2,2,8,2048]{4,3,2,1,0:T(8,128)(2,1)}, u32[]{:S(2)}, u32[]{:S(2)}) collective-permute-start(bf16[8,2,2,8,2048]{4,3,2,1,0:T(8,128)(2,1)} %maximum_maximum_fusion), channel_id=1, source_target_pairs={{0,16},{16,0},{1,17},{17,1},{2,18},{18,2},{3,19},{19,3},{4,20},{20... | collective-permute-start | bytes 3145736 | tf_op jit(solution)/shard_map/ppermute | solution.py:31

commit v2 on v1

v2 whole, which is shorter than its diff:
```python
import jax
import jax.numpy as jnp
from jax import lax
from jax.experimental import pallas as pl
from jax.experimental.pallas import tpu as pltpu
from jax.sharding import Mesh
from jax.sharding import PartitionSpec as P

TENSOR = ("xh", "y2", "y1", "y0")
DP = ("zh", "zl", "xl", "c")
SWAP = [(0, 1), (1, 0)]

bias_first = 0.9999734386011124
bias_second = 0.09520785288629112

F32 = jnp.float32
BF16 = jnp.bfloat16
VMEM = pltpu.VMEM


def shaped(shape, dtype):
    return jax.ShapeDtypeStruct(shape, dtype)


def pick(second, first_value, second_value):
    return jnp.where(second, second_value, first_value)


def weight_gradient_kernel(ids, latent, gain, grad, send, own, turned):
    @pl.when(pl.program_id(0) == 0)
    def _():
        values = latent[...].astype(F32)
        inverse_rms = lax.rsqrt(jnp.mean(values * values, axis=1, keepdims=True) + 1e-06)
        turned[...] = (values * inverse_rms * gain[...]).T.astype(BF16)

    part = lax.dot_general(
        turned[...], grad[...], (((1,), (0,)), ((), ())), preferred_element_type=F32
    )
    rows, cols = part.shape
    part = part.reshape(rows // 16, 2, 8, cols)
    one = ids[2] == 1
    own[...] = pick(one, part[:, 0], part[:, 1]).reshape(rows // 2, cols)
    send[...] = pick(one, part[:, 1], part[:, 0]).reshape(rows // 2, cols).astype(BF16)


def weight_gradient(ids, latent, gain, grad):
    tokens, latents = latent.shape
    cols = grad.shape[1]
    block = 512
    return pl.pallas_call(
        weight_gradient_kernel,
        grid=(cols // block,),
        in_specs=[
            pl.BlockSpec(memory_space=pltpu.SMEM),
            pl.BlockSpec((tokens, latents), lambda j: (0, 0)),
            pl.BlockSpec((1, latents), lambda j: (0, 0)),
            pl.BlockSpec((tokens, block), lambda j: (0, j)),
        ],
        out_specs=[
            pl.BlockSpec((latents // 2, block), lambda j: (0, j)),
            pl.BlockSpec((latents // 2, block), lambda j: (0, j)),
        ],
        out_shape=[shaped((latents // 2, cols), BF16), shaped((latents // 2, cols), F32)],
        scratch_shapes=[VMEM((latents, tokens), BF16)],
        name="weight_gradient",
    )(ids, latent, gain, grad)


def first_split_kernel(ids, own, got, p_send, p_own, q_send, q_own):
    total = own[...] + got[...].astype(F32)
    rows, cols = total.shape
    half = cols // 2
    total = total.reshape(rows // 32, 2, 2, 8, cols)
    p = total[..., :half]
    q = total[..., half:]
    zl = ids[0] == 1
    xl = ids[1] == 1
    flat = (rows // 2, half)
    p_own[...] = pick(xl, p[:, :, 0], p[:, :, 1]).reshape(flat)
    p_send[...] = pick(xl, p[:, :, 1], p[:, :, 0]).reshape(flat).astype(BF16)
    q_own[...] = pick(zl, q[:, 0], q[:, 1]).reshape(flat)
    q_send[...] = pick(zl, q[:, 1], q[:, 0]).reshape(flat).astype(BF16)


def first_split(ids, own, got):
    rows, cols = own.shape
    half = cols // 2
    block = rows // 4
    row_block = lambda r, n: pl.BlockSpec((r, n), lambda i: (i, 0))
    return pl.pallas_call(
        first_split_kernel,
        grid=(rows // block,),
        in_specs=[pl.BlockSpec(memory_space=pltpu.SMEM), row_block(block, cols), row_block(block, cols)],
        out_specs=[row_block(block // 2, half)] * 4,
        out_shape=[shaped((rows // 2, half), BF16), shaped((rows // 2, half), F32)] * 2,
        name="first_split",
    )(ids, own, got)


def second_split_kernel(which, ids, own, got, send, keep):
    total = own[...] + got[...].astype(F32)
    rows, cols = total.shape
    total = total.reshape(rows // 16, 2, 8, cols)
    one = ids[which] == 1
    keep[...] = pick(one, total[:, 0], total[:, 1]).reshape(rows // 2, cols)
    send[...] = pick(one, total[:, 1], total[:, 0]).reshape(rows // 2, cols).astype(BF16)


def second_split(ids, which, own, got):
    rows, cols = own.shape
    return pl.pallas_call(
        lambda *refs: second_split_kernel(which, *refs),
        in_specs=[pl.BlockSpec(memory_space=pltpu.SMEM)] + [pl.BlockSpec(memory_space=VMEM)] * 2,
        out_specs=[pl.BlockSpec(memory_space=VMEM)] * 2,
        out_shape=[shaped((rows // 2, cols), BF16), shaped((rows // 2, cols), F32)],
        name="second_split",
    )(ids, own, got)


def join_kernel(p_own, p_got, q_own, q_got, out):
    half = p_own.shape[1]
    out[:, :half] = (p_own[...] + p_got[...].astype(F32)).astype(BF16)
    out[:, half:] = (q_own[...] + q_got[...].astype(F32)).astype(BF16)


def join(p_own, p_got, q_own, q_got):
    rows, half = p_own.shape
    return pl.pallas_call(
        join_kernel,
        in_specs=[pl.BlockSpec(memory_space=VMEM)] * 4,
        out_specs=pl.BlockSpec(memory_space=VMEM),
        out_shape=shaped((rows, 2 * half), BF16),
        name="join",
    )(p_own, p_got, q_own, q_got)


def adam_kernel(blocks, master, first, second, new_master, new_first, new_second, copies):
    count = blocks.shape[0] // master.shape[0]
    parts = blocks[...].astype(F32)
    parts = parts.reshape(count, *master.shape)
    weight_grad = jnp.sum(parts, axis=0)
    m1 = 0.9 * first[...] + 0.1 * weight_grad
    m2 = 0.999 * second[...] + 0.001 * weight_grad * weight_grad
    new_first[...] = m1
    new_second[...] = m2
    held = master[...]
    updated = held - 0.01 * (
        (m1 / bias_first) / (jnp.sqrt(m2 / bias_second) + 1e-08) + 0.1 * held
    )
    new_master[...] = updated
    copies[...] = jnp.broadcast_to(updated[None], (count, *updated.shape)).reshape(
        copies.shape
    ).astype(BF16)


def adam(blocks, master, first, second):
    vmem = pl.BlockSpec(memory_space=VMEM)
    return pl.pallas_call(
        adam_kernel,
        in_specs=[vmem] * 4,
        out_specs=[vmem] * 4,
        out_shape=[shaped(master.shape, F32)] * 3 + [shaped(blocks.shape, BF16)],
        name="adam",
    )(blocks, master, first, second)


def copy_all(pairs, sems):
    copies = [pltpu.make_async_copy(a, b, sems.at[k]) for k, (a, b) in enumerate(pairs)]
    for copy in copies:
        copy.start()
    for copy in copies:
        copy.wait()


def replica_kernel(ids, *refs):
    pieces, out, sems = refs[:10], refs[10], refs[11]
    zl, xl, c = ids[0], ids[1], ids[2]
    half = out.shape[-1] // 2
    pairs = []
    for k in range(2):
        rep, rz, rx, dp, dq = pieces[5 * k : 5 * k + 5]
        core = c if k == 0 else 1 - c
        pairs.append((rep, out.at[:, zl, xl, core]))
        pairs.append((rz, out.at[:, 1 - zl, xl, core]))
        pairs.append((rx, out.at[:, zl, 1 - xl, core]))
        pairs.append((dp, out.at[:, 1 - zl, 1 - xl, core, :, pl.ds(0, half)]))
        pairs.append((dq, out.at[:, 1 - zl, 1 - xl, core, :, pl.ds(half, half)]))
    copy_all(pairs, sems)


def place_replica(ids, pieces):
    zh, rows, cols = pieces[0].shape
    anywhere = pl.BlockSpec(memory_space=pl.ANY)
    return pl.pallas_call(
        replica_kernel,
        in_specs=[pl.BlockSpec(memory_space=pltpu.SMEM)] + [anywhere] * 10,
        out_specs=anywhere,
        out_shape=shaped((zh, 2, 2, 2, rows, cols), BF16),
        scratch_shapes=[pltpu.SemaphoreType.DMA((10,))],
        name="place_replica",
    )(ids, *pieces)


def tokens_kernel(ids, own, xh, y2, y1, y0, out, sems):
    me = ids[3]
    pairs = [(own.at[0], out.at[me]), (xh.at[0], out.at[me ^ 8])]
    for k in range(2):
        pairs.append((y2.at[k], out.at[me ^ (4 | 8 * k)]))
    for k in range(4):
        pairs.append((y1.at[k], out.at[me ^ (2 | 8 * (k & 1) | 4 * (k >> 1))]))
    for k in range(8):
        pairs.append((y0.at[k], out.at[me ^ (1 | 8 * (k & 1) | 4 * (k >> 1 & 1) | 2 * (k >> 2))]))
    copy_all(pairs, sems)


def place_tokens(ids, *pieces):
    anywhere = pl.BlockSpec(memory_space=pl.ANY)
    return pl.pallas_call(
        tokens_kernel,
        in_specs=[pl.BlockSpec(memory_space=pltpu.SMEM)] + [anywhere] * 5,
        out_specs=anywhere,
        out_shape=shaped((16, *pieces[0].shape[1:]), BF16),
        scratch_shapes=[pltpu.SemaphoreType.DMA((16,))],
        name="place_tokens",
    )(ids, *pieces)


def swap(x, axis):
    return lax.ppermute(x, axis, SWAP)


def norm_backward(latent_rows, norm_gain, grad_rows):
    values = latent_rows.astype(F32)
    inverse_rms = lax.rsqrt(jnp.mean(values * values, axis=1, keepdims=True) + 1e-06)
    unit = values * inverse_rms
    scaled = grad_rows * norm_gain
    inner = jnp.mean(scaled * unit, axis=1, keepdims=True)
    return (inverse_rms * (scaled - unit * inner)).astype(BF16)


def local(
    latent_pre, norm_gain, kv_weight, down_weight, grad_kv, master, first_moment, second_moment
):
    barrier = lax.optimization_barrier
    cols = grad_kv.shape[1]
    half = cols // 2
    own_place = lax.axis_index(TENSOR)
    ids = jnp.stack([lax.axis_index(a) for a in ("zl", "xl", "c")] + [own_place]).astype(jnp.int32)
    send, own = weight_gradient(ids, latent_pre, norm_gain[None], grad_kv)
    got = swap(send, "c")
    grad_kv_after, _ = barrier((grad_kv, send))
    grad_part = lax.dot_general(
        grad_kv_after, kv_weight, (((1,), (1,)), ((), ())), preferred_element_type=F32
    )
    share = grad_part.shape[0] // lax.axis_size(TENSOR)
    blocks = lax.all_to_all(
        grad_part.reshape(-1, share, grad_part.shape[1]), TENSOR, 0, 0, tiled=True
    )
    p_send, p_own, q_send, q_own = first_split(ids, own, got)
    p_got = swap(p_send, "xl")
    q_got = swap(q_send, "zl")
    p_send, p_own = second_split(ids, 0, p_own, p_got)
    q_send, q_own = second_split(ids, 1, q_own, q_got)
    p_got = swap(p_send, "zl")
    q_got = swap(q_send, "xl")
    both = join(p_own, p_got, q_own, q_got)
    both, blocks = barrier((both, blocks))
    summed = lax.all_to_all(both.reshape(8, -1, cols), "zh", 0, 0, tiled=True)
    grad_share = jnp.sum(blocks, axis=0)
    latent_share = lax.dynamic_slice_in_dim(latent_pre, own_place * share, share, 0)
    t = norm_backward(latent_share, norm_gain, grad_share)[None]
    t_xh = swap(t, "xh")
    summed, t_xh = barrier((summed, t_xh))
    new_master, new_first, new_second, copies = adam(
        summed.reshape(both.shape), master, first_moment, second_moment
    )
    rep = lax.all_to_all(copies.reshape(8, -1, cols), "zh", 0, 0, tiled=True)
    t2 = jnp.concatenate([t, t_xh])
    t_y2 = swap(t2, "y2")
    t4 = jnp.concatenate([t2, t_y2])
    t_y1 = swap(t4, "y1")
    rep, t_y1 = barrier((rep, t_y1))
    rz = swap(rep, "zl")
    rx = swap(rep, "xl")
    t_y0 = swap(jnp.concatenate([t4, t_y1]), "y0")
    rep_c = swap(rep, "c")
    dp = swap(rz[..., :half], "xl")
    dq = swap(rx[..., half:], "zl")
    rz_c = swap(rz, "c")
    rx_c = swap(rx, "c")
    dp_c = swap(dp, "c")
    dq_c = swap(dq, "c")
    grad_pre = place_tokens(ids, t, t_xh, t_y2, t_y1, t_y0).reshape(latent_pre.shape)
    grad_hidden = lax.dot_general(
        grad_pre, down_weight, (((1,), (1,)), ((), ())), preferred_element_type=F32
    ).astype(BF16)
    new_replica = place_replica(
        ids, (rep, rz, rx, dp, dq, rep_c, rz_c, rx_c, dp_c, dq_c)
    ).reshape(-1, cols)
    return (grad_hidden, new_master, new_first, new_second, new_replica)


def solution(mesh):
    torus = Mesh(
        mesh.devices.reshape(8, 2, 2, 2, 2, 2, 2, 2),
        ("zh", "zl", "xl", "c", "xh", "y2", "y1", "y0"),
    )
    placed = (
        P(DP, None),
        P(),
        P(None, TENSOR),
        P(TENSOR, None),
        P(DP, TENSOR),
        P(DP, TENSOR),
        P(DP, TENSOR),
        P(DP, TENSOR),
    )
    return jax.shard_map(
        local,
        mesh=torus,
        in_specs=placed,
        out_specs=(P(DP, TENSOR), P(DP, TENSOR), P(DP, TENSOR), P(DP, TENSOR), P(None, TENSOR)),
        check_vma=False,
    )
```

time: 179 us -> 242 us (1.35)
  Pallas kernels: 0 us -> 99.9 us
  waiting for transfers between devices: 72.4 us -> 27.3 us
  starting transfers between devices: 71.7 us -> 95.3 us
  other arithmetic: 16.3 us -> 3.45 us
  matrix products: 8.65 us -> 6.22 us
    pallas_call x0 -> x8, Pallas kernels: none -> 99.9 us  [the longest x1 65.4 us: place_replica(): pl.pallas_call(replica_kernel, in_specs=[pl.BlockSpec(memory_space=pltpu....]
    ppermute x10 -> x18, starting transfers between devices: 29.3 us -> 67.9 us  [swap(): return lax.ppermute(x, axis, SWAP)]
    all_to_all x3 -> x2, waiting for transfers between devices: 37.6 us -> 9.04 us  [the longest x1 9.04 us: local(): summed = lax.all_to_all(both.reshape(8, -1, cols), 'zh', 0, 0, tiled=True)]
    all_to_all x1, waiting for transfers between devices: 19.1 us -> 0.01 us  [local(): lax.all_to_all(grad_part.reshape(-1, share, grad_part.shape[1]), TENSOR,...]
    all_to_all x3 -> x2, starting transfers between devices: 32.2 us -> 17.3 us  [the longest x1 13.9 us: local(): summed = lax.all_to_all(both.reshape(8, -1, cols), 'zh', 0, 0, tiled=True)]
    another operation x7 -> x1, other arithmetic: 5.45 us -> 0.64 us  [local(): jnp.stack([lax.axis_index(a) for a in ('zl', 'xl', 'c')] + [own_place])]
    add x3 -> x0, other arithmetic: 3.34 us -> none  [reduce_pair(): return at(x, me, dim).astype(F32) + got.astype(F32)]
    ppermute x10 -> x18, waiting for transfers between devices: 15.7 us -> 18.3 us  [swap(): return lax.ppermute(x, axis, SWAP)]
  transfers between devices with their start and end apart: 14 -> 21, of which waited for: 10 -> 6; matrix products, arithmetic and copies ran while one was open for 9% -> 3% of each run, Pallas kernels for 0% -> 11%
where the time goes in v2:
time: 242 us; the launch traced here: 238 us
  Pallas kernels  99.9 us (41%)
  starting transfers between devices  95.3 us (39%)
  waiting for transfers between devices  27.3 us (11%)
  matrix products  6.22 us (3%)
  local copies, waits for them, and re-layouts  5 us (2%)
  other arithmetic  3.45 us (1%)
    ppermute x18, starting transfers between devices, swap(): return lax.ppermute(x, axis, SWAP)  67.9 us
    pallas_call x1, Pallas kernels, place_replica(): pl.pallas_call(replica_kernel, in_specs=[pl.BlockSpec(memory_space=pltpu....  65.4 us
    ppermute x18, waiting for transfers between devices, swap(): return lax.ppermute(x, axis, SWAP)  18.3 us
    pallas_call x1, Pallas kernels, place_tokens(): pl.pallas_call(tokens_kernel, in_specs=[pl.BlockSpec(memory_space=pltpu.S...  17.8 us
    all_to_all x1, starting transfers between devices, local(): summed = lax.all_to_all(both.reshape(8, -1, cols), 'zh', 0, 0, tiled=True)  13.9 us
    all_to_all x1, starting transfers between devices, local(): lax.all_to_all(grad_part.reshape(-1, share, grad_part.shape[1]), TENSOR,...  10.1 us
    all_to_all x1, waiting for transfers between devices, local(): summed = lax.all_to_all(both.reshape(8, -1, cols), 'zh', 0, 0, tiled=True)  9.04 us
    pallas_call x1, Pallas kernels, weight_gradient(): pl.pallas_call(weight_gradient_kernel, grid=(cols // block,), in_specs=[p...  5.33 us
  transfers between devices with their start and end apart: 21, of which 6 were waited for; matrix products, arithmetic and copies ran while one was open for 3% of the time, Pallas kernels for 11%

profile of v2, /device:TPU:6, one launch (start us, length us, event | category | flops | bytes accessed | tf_op | source)
XLA Modules:
  0.0 238.2 jit_solution(7899038103714554525)
XLA Ops:
  1.3 5.3 %weight_gradient.1 = (bf16[256,2048]{1,0:T(8,128)(2,1)}, f32[256,2048]{1,0:T(8,128)}) custom-call(s32[4]{0:T(128)} %pad_add_fusion.ids.refs_0_, bf16[512,512]{1,0:T(8,128)(2,1)} %latent.1, f32[1,512]{1,0:T(1,128)} %bitcast.23, bf16[512,2048]{1,0:T(8,128)(2,1)} %grad.1), custom_call_target="tpu_custom_call" | custom-call | tf_op jit(solution)/shard_map/weight_gradient/pallas_call | solution.py:50
  6.6 3.8 %fusion.8 = f32[512,512]{1,0:T(8,128)} fusion(bf16[512,2048]{1,0:T(8,128)(2,1)} %grad.1, bf16[512,2048]{1,0:T(8,128)(2,1)S(1)} %copy-done), kind=kOutput, calls=%fused_computation.17 | convolution fusion | flops 1073741824 | bytes 5242880 | tf_op jit(solution)/shard_map/dot_general | solution.py:252
  10.5 10.1 %all-to-all-start = ((f32[16,32,512]{2,1,0:T(8,128)}), f32[16,32,512]{2,1,0:T(8,128)S(1)}, u32[]{:S(2)}, u32[]{:S(2)}) async-start(f32[16,32,512]{2,1,0:T(8,128)} %bitcast.20), calls=%async_computation | async-start | bytes 2097152 | tf_op jit(solution)/shard_map/all_to_all | solution.py:256
  22.5 3.0 %collective-permute-done.got = bf16[256,2048]{1,0:T(8,128)(2,1)} collective-permute-done((bf16[256,2048]{1,0:T(8,128)(2,1)}, bf16[256,2048]{1,0:T(8,128)(2,1)}, u32[]{:S(2)}, u32[]{:S(2)}) %collective-permute-start) | collective-permute-done | bytes 1048608 | tf_op jit(solution)/shard_map/ppermute | solution.py:229
  25.4 3.8 %first_split.1 = (bf16[128,1024]{1,0:T(8,128)(2,1)}, f32[128,1024]{1,0:T(8,128)}, bf16[128,1024]{1,0:T(8,128)(2,1)}, f32[128,1024]{1,0:T(8,128)}) custom-call(s32[4]{0:T(128)} %pad_add_fusion.ids.refs_0_, f32[256,2048]{1,0:T(8,128)} %get-tuple-element.26.own, bf16[256,2048]{1,0:T(8,128)(2,1)} %collective-permute-done.got), custom_call_target="tpu_custom_call" | custom-call | tf_op jit(solution)/shard_map/first_split/pallas_call | solution.py:90
  29.3 4.3 %collective-permute-start.3 = (bf16[128,1024]{1,0:T(8,128)(2,1)}, bf16[128,1024]{1,0:T(8,128)(2,1)}, u32[]{:S(2)}, u32[]{:S(2)}) collective-permute-start(bf16[128,1024]{1,0:T(8,128)(2,1)} %get-tuple-element.33), channel_id=1, source_target_pairs={{0,64},{64,0},{1,65},{65,1},{2,66},{66,2},{3,67},{67,3},{4,68},{68... | collective-permute-start | bytes 786440 | tf_op jit(solution)/shard_map/ppermute | solution.py:229
  33.5 6.9 %collective-permute-start.1 = (bf16[128,1024]{1,0:T(8,128)(2,1)}, bf16[128,1024]{1,0:T(8,128)(2,1)S(1)}, u32[]{:S(2)}, u32[]{:S(2)}) collective-permute-start(bf16[128,1024]{1,0:T(8,128)(2,1)} %get-tuple-element.29), channel_id=1, source_target_pairs={{0,32},{32,0},{1,33},{33,1},{2,34},{34,2},{3,35},{35,3},{4,36},{36... | collective-permute-start | bytes 786440 | tf_op jit(solution)/shard_map/ppermute | solution.py:229
  42.4 8.6 %collective-permute-start.4 = (bf16[64,1024]{1,0:T(8,128)(2,1)}, bf16[64,1024]{1,0:T(8,128)(2,1)S(1)}, u32[]{:S(2)}, u32[]{:S(2)}) collective-permute-start(bf16[64,1024]{1,0:T(8,128)(2,1)} %get-tuple-element.35), channel_id=1, source_target_pairs={{0,32},{32,0},{1,33},{33,1},{2,34},{34,2},{3,35},{35,3},{4,36},{36... | collective-permute-start | bytes 393224 | tf_op jit(solution)/shard_map/ppermute | solution.py:229
  51.7 1.9 second_split.2
  53.7 2.2 collective-permute-start.2
  55.9 4.8 %collective-permute-done.2.p_got = bf16[64,1024]{1,0:T(8,128)(2,1)S(1)} collective-permute-done((bf16[64,1024]{1,0:T(8,128)(2,1)}, bf16[64,1024]{1,0:T(8,128)(2,1)S(1)}, u32[]{:S(2)}, u32[]{:S(2)}) %collective-permute-start.2) | collective-permute-done | bytes 131104 | tf_op jit(solution)/shard_map/ppermute | solution.py:229
  63.3 13.9 %all-to-all-start.1 = ((bf16[8,8,2048]{2,1,0:T(8,128)(2,1)}), bf16[8,8,2048]{2,1,0:T(8,128)(2,1)S(1)}, u32[]{:S(2)}, u32[]{:S(2)}) async-start(bf16[8,8,2048]{2,1,0:T(8,128)(2,1)} %bitcast.21), calls=%async_computation.1 | async-start | bytes 524288 | tf_op jit(solution)/shard_map/all_to_all | solution.py:268
  80.0 2.3 collective-permute-start.5
  82.3 5.0 %collective-permute-done.5.xh = bf16[1,32,512]{2,1,0:T(8,128)(2,1)S(1)} collective-permute-done((bf16[1,32,512]{2,1,0:T(8,128)(2,1)S(1)}, bf16[1,32,512]{2,1,0:T(8,128)(2,1)S(1)}, u32[]{:S(2)}, u32[]{:S(2)}) %collective-permute-start.5) | collective-permute-done | bytes 32800 | tf_op jit(solution)/shard_map/ppermute | solution.py:229
  87.3 9.0 %all-to-all-done.1 = bf16[8,8,2048]{2,1,0:T(8,128)(2,1)S(1)} async-done(((bf16[8,8,2048]{2,1,0:T(8,128)(2,1)}), bf16[8,8,2048]{2,1,0:T(8,128)(2,1)S(1)}, u32[]{:S(2)}, u32[]{:S(2)}) %all-to-all-start.1) | async-done | bytes 262176 | tf_op jit(solution)/shard_map/all_to_all | solution.py:268
  98.8 3.4 %all-to-all-start.2 = ((bf16[8,8,2048]{2,1,0:T(8,128)(2,1)}), bf16[8,8,2048]{2,1,0:T(8,128)(2,1)S(1)}, u32[]{:S(2)}, u32[]{:S(2)}) async-start(bf16[8,8,2048]{2,1,0:T(8,128)(2,1)} %bitcast.22), calls=%async_computation.2 | async-start | bytes 524288 | tf_op jit(solution)/shard_map/all_to_all | solution.py:277
  102.3 9.1 %collective-permute-start.6 = (bf16[2,32,512]{2,1,0:T(8,128)(2,1)S(1)}, bf16[2,32,512]{2,1,0:T(8,128)(2,1)S(1)}, u32[]{:S(2)}, u32[]{:S(2)}) collective-permute-start(bf16[2,32,512]{2,1,0:T(8,128)(2,1)S(1)} %pad_maximum_fusion.2), channel_id=1, source_target_pairs={{0,4},{4,0},{1,5},{5,1},{2,6},{6,2},{3,7},{7,3},{8,12},{12,8},{9,1... | collective-permute-start | bytes 196616 | tf_op jit(solution)/shard_map/ppermute | solution.py:229
  111.3 2.5 %collective-permute-done.6.y2 = bf16[2,32,512]{2,1,0:T(8,128)(2,1)S(1)} collective-permute-done((bf16[2,32,512]{2,1,0:T(8,128)(2,1)S(1)}, bf16[2,32,512]{2,1,0:T(8,128)(2,1)S(1)}, u32[]{:S(2)}, u32[]{:S(2)}) %collective-permute-start.6) | collective-permute-done | bytes 65568 | tf_op jit(solution)/shard_map/ppermute | solution.py:229
  113.8 4.8 %collective-permute-start.7 = (bf16[4,32,512]{2,1,0:T(8,128)(2,1)S(1)}, bf16[4,32,512]{2,1,0:T(8,128)(2,1)S(1)}, u32[]{:S(2)}, u32[]{:S(2)}) collective-permute-start(bf16[4,32,512]{2,1,0:T(8,128)(2,1)S(1)} %pad_maximum_fusion.1), channel_id=1, source_target_pairs={{0,2},{2,0},{1,3},{3,1},{4,6},{6,4},{5,7},{7,5},{8,10},{10,8},{9,1... | collective-permute-start | bytes 393224 | tf_op jit(solution)/shard_map/ppermute | solution.py:229
  118.7 2.9 %collective-permute-done.7.y1 = bf16[4,32,512]{2,1,0:T(8,128)(2,1)S(1)} collective-permute-done((bf16[4,32,512]{2,1,0:T(8,128)(2,1)S(1)}, bf16[4,32,512]{2,1,0:T(8,128)(2,1)S(1)}, u32[]{:S(2)}, u32[]{:S(2)}) %collective-permute-start.7) | collective-permute-done | bytes 131104 | tf_op jit(solution)/shard_map/ppermute | solution.py:229
  121.6 4.9 %collective-permute-start.9 = (bf16[8,8,2048]{2,1,0:T(8,128)(2,1)S(1)}, bf16[8,8,2048]{2,1,0:T(8,128)(2,1)S(1)}, u32[]{:S(2)}, u32[]{:S(2)}) collective-permute-start(bf16[8,8,2048]{2,1,0:T(8,128)(2,1)S(1)} %all-to-all-done.2.refs_0_), channel_id=1, source_target_pairs={{0,64},{64,0},{1,65},{65,1},{2,66},{66,2},{3,67},{67,3},{4,68},{68... | collective-permute-start | bytes 786440 | tf_op jit(solution)/shard_map/ppermute | solution.py:229
  126.5 2.4 collective-permute-start.10
  128.9 2.8 %collective-permute-start.8 = (bf16[8,32,512]{2,1,0:T(8,128)(2,1)S(1)}, bf16[8,32,512]{2,1,0:T(8,128)(2,1)S(1)}, u32[]{:S(2)}, u32[]{:S(2)}) collective-permute-start(bf16[8,32,512]{2,1,0:T(8,128)(2,1)S(1)} %pad_maximum_fusion), channel_id=1, source_target_pairs={{0,1},{1,0},{2,3},{3,2},{4,5},{5,4},{6,7},{7,6},{8,9},{9,8},{10,11... | collective-permute-start | bytes 786440 | tf_op jit(solution)/shard_map/ppermute | solution.py:229
  132.4 3.9 %collective-permute-start.11 = (bf16[8,8,1024]{2,1,0:T(8,128)(2,1)}, bf16[8,8,1024]{2,1,0:T(8,128)(2,1)S(1)}, u32[]{:S(2)}, u32[]{:S(2)}) collective-permute-start(bf16[8,8,1024]{2,1,0:T(8,128)(2,1)} %slice.8), channel_id=1, source_target_pairs={{0,32},{32,0},{1,33},{33,1},{2,34},{34,2},{3,35},{35,3},{4,36},{36... | collective-permute-start | bytes 393224 | tf_op jit(solution)/shard_map/ppermute | solution.py:229
  137.1 3.4 %collective-permute-start.12 = (bf16[8,8,1024]{2,1,0:T(8,128)(2,1)}, bf16[8,8,1024]{2,1,0:T(8,128)(2,1)}, u32[]{:S(2)}, u32[]{:S(2)}) collective-permute-start(bf16[8,8,1024]{2,1,0:T(8,128)(2,1)} %slice.9), channel_id=1, source_target_pairs={{0,64},{64,0},{1,65},{65,1},{2,66},{66,2},{3,67},{67,3},{4,68},{68... | collective-permute-start | bytes 393224 | tf_op jit(solution)/shard_map/ppermute | solution.py:229
  140.5 1.9 collective-permute-start.13
  142.4 2.4 %collective-permute-start.14 = (bf16[8,8,2048]{2,1,0:T(8,128)(2,1)S(1)}, bf16[8,8,2048]{2,1,0:T(8,128)(2,1)}, u32[]{:S(2)}, u32[]{:S(2)}) collective-permute-start(bf16[8,8,2048]{2,1,0:T(8,128)(2,1)S(1)} %collective-permute-done.9.refs_1_), channel_id=1, source_target_pairs={{0,16},{16,0},{1,17},{17,1},{2,18},{18,2},{3,19},{19,3},{4,20},{20... | collective-permute-start | bytes 786440 | tf_op jit(solution)/shard_map/ppermute | solution.py:229
  147.5 17.8 %place_tokens.1 = bf16[16,32,512]{2,1,0:T(8,128)(2,1)} custom-call(s32[4]{0:T(128)} %pad_add_fusion.ids.refs_0_, bf16[1,32,512]{2,1,0:T(8,128)(2,1)} %copy-done.3, bf16[1,32,512]{2,1,0:T(8,128)(2,1)} %copy-done.8, bf16[2,32,512]{2,1,0:T(8,128)(2,1)} %copy-done.6, bf16[4,32,512]{2,1,0:T(8,128)(2,1)} %copy-done.7, bf16[8,32,512]{2,1,0:T(8,128)(2,1)} %copy-done.10), custom_call_target="tpu_custom_call" | custom-call | tf_op jit(solution)/shard_map/place_tokens/pallas_call | solution.py:218
  165.3 2.4 %collective-permute-start.16 = (bf16[8,8,1024]{2,1,0:T(8,128)(2,1)S(1)}, bf16[8,8,1024]{2,1,0:T(8,128)(2,1)S(1)}, u32[]{:S(2)}, u32[]{:S(2)}) collective-permute-start(bf16[8,8,1024]{2,1,0:T(8,128)(2,1)S(1)} %collective-permute-done.11.refs_3_), channel_id=1, source_target_pairs={{0,16},{16,0},{1,17},{17,1},{2,18},{18,2},{3,19},{19,3},{4,20},{20... | collective-permute-start | bytes 393224 | tf_op jit(solution)/shard_map/ppermute | solution.py:229
  167.7 1.9 collective-permute-start.17
  169.7 2.4 convolution_convert_fusion
  172.9 65.4 %place_replica.1 = bf16[8,2,2,2,8,2048]{5,4,3,2,1,0:T(8,128)(2,1)} custom-call(s32[4]{0:T(128)} %pad_add_fusion.ids.refs_0_, bf16[8,8,2048]{2,1,0:T(8,128)(2,1)} %copy-done.1, bf16[8,8,2048]{2,1,0:T(8,128)(2,1)} %copy-done.4, bf16[8,8,2048]{2,1,0:T(8,128)(2,1)} %copy-done.5, bf16[8,8,1024]{2,1,0:T(8,128)(2,1)} %copy-done.12, ...), custom_call_target="tpu_custom_call" | custom-call | tf_op jit(solution)/shard_map/place_replica/pallas_call | solution.py:194
  (68 shorter events, 17.9 us)
Async XLA Ops:
  0.6 6.0 %copy-start = (bf16[512,2048]{1,0:T(8,128)(2,1)S(1)}, bf16[512,2048]{1,0:T(8,128)(2,1)}, u32[]{:S(2)}) copy-start(bf16[512,2048]{1,0:T(8,128)(2,1)} %param.10) | copy-start | bytes 6291460
  10.5 52.8 %all-to-all-start = ((f32[16,32,512]{2,1,0:T(8,128)}), f32[16,32,512]{2,1,0:T(8,128)S(1)}, u32[]{:S(2)}, u32[]{:S(2)}) async-start(f32[16,32,512]{2,1,0:T(8,128)} %bitcast.20), calls=%async_computation | async-start | bytes 2097152 | tf_op jit(solution)/shard_map/all_to_all | solution.py:256
  20.6 4.9 %collective-permute-start = (bf16[256,2048]{1,0:T(8,128)(2,1)}, bf16[256,2048]{1,0:T(8,128)(2,1)}, u32[]{:S(2)}, u32[]{:S(2)}) collective-permute-start(bf16[256,2048]{1,0:T(8,128)(2,1)} %get-tuple-element.27), channel_id=1, source_target_pairs={{0,16},{16,0},{1,17},{17,1},{2,18},{18,2},{3,19},{19,3},{4,20},{20... | collective-permute-start | bytes 3145736 | tf_op jit(solution)/shard_map/ppermute | solution.py:229
  29.3 11.2 %collective-permute-start.3 = (bf16[128,1024]{1,0:T(8,128)(2,1)}, bf16[128,1024]{1,0:T(8,128)(2,1)}, u32[]{:S(2)}, u32[]{:S(2)}) collective-permute-start(bf16[128,1024]{1,0:T(8,128)(2,1)} %get-tuple-element.33), channel_id=1, source_target_pairs={{0,64},{64,0},{1,65},{65,1},{2,66},{66,2},{3,67},{67,3},{4,68},{68... | collective-permute-start | bytes 786440 | tf_op jit(solution)/shard_map/ppermute | solution.py:229
  33.5 17.5 %collective-permute-start.1 = (bf16[128,1024]{1,0:T(8,128)(2,1)}, bf16[128,1024]{1,0:T(8,128)(2,1)S(1)}, u32[]{:S(2)}, u32[]{:S(2)}) collective-permute-start(bf16[128,1024]{1,0:T(8,128)(2,1)} %get-tuple-element.29), channel_id=1, source_target_pairs={{0,32},{32,0},{1,33},{33,1},{2,34},{34,2},{3,35},{35,3},{4,36},{36... | collective-permute-start | bytes 786440 | tf_op jit(solution)/shard_map/ppermute | solution.py:229
  40.5 37.7 %copy-start.17 = (f32[512]{0:T(512)S(1)}, f32[512]{0:T(512)}, u32[]{:S(2)}) copy-start(f32[512]{0:T(512)} %param.9) | copy-start | bytes 6148
  42.4 13.4 %collective-permute-start.4 = (bf16[64,1024]{1,0:T(8,128)(2,1)}, bf16[64,1024]{1,0:T(8,128)(2,1)S(1)}, u32[]{:S(2)}, u32[]{:S(2)}) collective-permute-start(bf16[64,1024]{1,0:T(8,128)(2,1)} %get-tuple-element.35), channel_id=1, source_target_pairs={{0,32},{32,0},{1,33},{33,1},{2,34},{34,2},{3,35},{35,3},{4,36},{36... | collective-permute-start | bytes 393224 | tf_op jit(solution)/shard_map/ppermute | solution.py:229
  53.7 7.1 %collective-permute-start.2 = (bf16[64,1024]{1,0:T(8,128)(2,1)}, bf16[64,1024]{1,0:T(8,128)(2,1)S(1)}, u32[]{:S(2)}, u32[]{:S(2)}) collective-permute-start(bf16[64,1024]{1,0:T(8,128)(2,1)} %get-tuple-element.31), channel_id=1, source_target_pairs={{0,64},{64,0},{1,65},{65,1},{2,66},{66,2},{3,67},{67,3},{4,68},{68... | collective-permute-start | bytes 393224 | tf_op jit(solution)/shard_map/ppermute | solution.py:229
  55.9 4.9 %copy-start.15 = (bf16[64,1024]{1,0:T(8,128)(2,1)}, bf16[64,1024]{1,0:T(8,128)(2,1)S(1)}, u32[]{:S(2)}) copy-start(bf16[64,1024]{1,0:T(8,128)(2,1)S(1)} %collective-permute-done.4.q_got) | copy-start | bytes 393220
  63.3 33.1 %all-to-all-start.1 = ((bf16[8,8,2048]{2,1,0:T(8,128)(2,1)}), bf16[8,8,2048]{2,1,0:T(8,128)(2,1)S(1)}, u32[]{:S(2)}, u32[]{:S(2)}) async-start(bf16[8,8,2048]{2,1,0:T(8,128)(2,1)} %bitcast.21), calls=%async_computation.1 | async-start | bytes 524288 | tf_op jit(solution)/shard_map/all_to_all | solution.py:268
  80.0 67.5 %copy-start.3 = (bf16[1,32,512]{2,1,0:T(8,128)(2,1)}, bf16[1,32,512]{2,1,0:T(8,128)(2,1)S(1)}, u32[]{:S(2)}) copy-start(bf16[1,32,512]{2,1,0:T(8,128)(2,1)S(1)} %fusion.7.own) | copy-start | bytes 98308
  80.0 7.3 %collective-permute-start.5 = (bf16[1,32,512]{2,1,0:T(8,128)(2,1)S(1)}, bf16[1,32,512]{2,1,0:T(8,128)(2,1)S(1)}, u32[]{:S(2)}, u32[]{:S(2)}) collective-permute-start(bf16[1,32,512]{2,1,0:T(8,128)(2,1)S(1)} %fusion.7.own), channel_id=1, source_target_pairs={{0,8},{8,0},{1,9},{9,1},{2,10},{10,2},{3,11},{11,3},{4,12},{12,4},... | collective-permute-start | bytes 98312 | tf_op jit(solution)/shard_map/ppermute | solution.py:229
  87.3 60.2 %copy-start.8 = (bf16[1,32,512]{2,1,0:T(8,128)(2,1)}, bf16[1,32,512]{2,1,0:T(8,128)(2,1)S(1)}, u32[]{:S(2)}) copy-start(bf16[1,32,512]{2,1,0:T(8,128)(2,1)S(1)} %collective-permute-done.5.xh) | copy-start | bytes 98308
  98.8 22.8 %all-to-all-start.2 = ((bf16[8,8,2048]{2,1,0:T(8,128)(2,1)}), bf16[8,8,2048]{2,1,0:T(8,128)(2,1)S(1)}, u32[]{:S(2)}, u32[]{:S(2)}) async-start(bf16[8,8,2048]{2,1,0:T(8,128)(2,1)} %bitcast.22), calls=%async_computation.2 | async-start | bytes 524288 | tf_op jit(solution)/shard_map/all_to_all | solution.py:277
  102.3 11.6 %collective-permute-start.6 = (bf16[2,32,512]{2,1,0:T(8,128)(2,1)S(1)}, bf16[2,32,512]{2,1,0:T(8,128)(2,1)S(1)}, u32[]{:S(2)}, u32[]{:S(2)}) collective-permute-start(bf16[2,32,512]{2,1,0:T(8,128)(2,1)S(1)} %pad_maximum_fusion.2), channel_id=1, source_target_pairs={{0,4},{4,0},{1,5},{5,1},{2,6},{6,2},{3,7},{7,3},{8,12},{12,8},{9,1... | collective-permute-start | bytes 196616 | tf_op jit(solution)/shard_map/ppermute | solution.py:229
  113.8 33.6 %copy-start.6 = (bf16[2,32,512]{2,1,0:T(8,128)(2,1)}, bf16[2,32,512]{2,1,0:T(8,128)(2,1)S(1)}, u32[]{:S(2)}) copy-start(bf16[2,32,512]{2,1,0:T(8,128)(2,1)S(1)} %collective-permute-done.6.y2) | copy-start | bytes 196612
  113.8 7.8 %collective-permute-start.7 = (bf16[4,32,512]{2,1,0:T(8,128)(2,1)S(1)}, bf16[4,32,512]{2,1,0:T(8,128)(2,1)S(1)}, u32[]{:S(2)}, u32[]{:S(2)}) collective-permute-start(bf16[4,32,512]{2,1,0:T(8,128)(2,1)S(1)} %pad_maximum_fusion.1), channel_id=1, source_target_pairs={{0,2},{2,0},{1,3},{3,1},{4,6},{6,4},{5,7},{7,5},{8,10},{10,8},{9,1... | collective-permute-start | bytes 393224 | tf_op jit(solution)/shard_map/ppermute | solution.py:229
  121.6 25.9 %copy-start.7 = (bf16[4,32,512]{2,1,0:T(8,128)(2,1)}, bf16[4,32,512]{2,1,0:T(8,128)(2,1)S(1)}, u32[]{:S(2)}) copy-start(bf16[4,32,512]{2,1,0:T(8,128)(2,1)S(1)} %collective-permute-done.7.y1) | copy-start | bytes 393220
  121.6 51.2 %copy-start.1 = (bf16[8,8,2048]{2,1,0:T(8,128)(2,1)}, bf16[8,8,2048]{2,1,0:T(8,128)(2,1)S(1)}, u32[]{:S(2)}) copy-start(bf16[8,8,2048]{2,1,0:T(8,128)(2,1)S(1)} %all-to-all-done.2.refs_0_) | copy-start | bytes 786436
  121.6 10.1 %collective-permute-start.9 = (bf16[8,8,2048]{2,1,0:T(8,128)(2,1)S(1)}, bf16[8,8,2048]{2,1,0:T(8,128)(2,1)S(1)}, u32[]{:S(2)}, u32[]{:S(2)}) collective-permute-start(bf16[8,8,2048]{2,1,0:T(8,128)(2,1)S(1)} %all-to-all-done.2.refs_0_), channel_id=1, source_target_pairs={{0,64},{64,0},{1,65},{65,1},{2,66},{66,2},{3,67},{67,3},{4,68},{68... | collective-permute-start | bytes 786440 | tf_op jit(solution)/shard_map/ppermute | solution.py:229
  126.5 9.8 %collective-permute-start.10 = (bf16[8,8,2048]{2,1,0:T(8,128)(2,1)S(1)}, bf16[8,8,2048]{2,1,0:T(8,128)(2,1)S(1)}, u32[]{:S(2)}, u32[]{:S(2)}) collective-permute-start(bf16[8,8,2048]{2,1,0:T(8,128)(2,1)S(1)} %all-to-all-done.2.refs_0_), channel_id=1, source_target_pairs={{0,32},{32,0},{1,33},{33,1},{2,34},{34,2},{3,35},{35,3},{4,36},{36... | collective-permute-start | bytes 786440 | tf_op jit(solution)/shard_map/ppermute | solution.py:229
  128.9 15.9 %collective-permute-start.8 = (bf16[8,32,512]{2,1,0:T(8,128)(2,1)S(1)}, bf16[8,32,512]{2,1,0:T(8,128)(2,1)S(1)}, u32[]{:S(2)}, u32[]{:S(2)}) collective-permute-start(bf16[8,32,512]{2,1,0:T(8,128)(2,1)S(1)} %pad_maximum_fusion), channel_id=1, source_target_pairs={{0,1},{1,0},{2,3},{3,2},{4,5},{5,4},{6,7},{7,6},{8,9},{9,8},{10,11... | collective-permute-start | bytes 786440 | tf_op jit(solution)/shard_map/ppermute | solution.py:229
  131.7 41.1 %copy-start.4 = (bf16[8,8,2048]{2,1,0:T(8,128)(2,1)}, bf16[8,8,2048]{2,1,0:T(8,128)(2,1)S(1)}, u32[]{:S(2)}) copy-start(bf16[8,8,2048]{2,1,0:T(8,128)(2,1)S(1)} %collective-permute-done.9.refs_1_) | copy-start | bytes 786436
  132.4 32.9 %collective-permute-start.11 = (bf16[8,8,1024]{2,1,0:T(8,128)(2,1)}, bf16[8,8,1024]{2,1,0:T(8,128)(2,1)S(1)}, u32[]{:S(2)}, u32[]{:S(2)}) collective-permute-start(bf16[8,8,1024]{2,1,0:T(8,128)(2,1)} %slice.8), channel_id=1, source_target_pairs={{0,32},{32,0},{1,33},{33,1},{2,34},{34,2},{3,35},{35,3},{4,36},{36... | collective-permute-start | bytes 393224 | tf_op jit(solution)/shard_map/ppermute | solution.py:229
  136.3 36.4 %copy-start.5 = (bf16[8,8,2048]{2,1,0:T(8,128)(2,1)}, bf16[8,8,2048]{2,1,0:T(8,128)(2,1)S(1)}, u32[]{:S(2)}) copy-start(bf16[8,8,2048]{2,1,0:T(8,128)(2,1)S(1)} %collective-permute-done.10.refs_2_) | copy-start | bytes 786436
  137.1 30.6 %collective-permute-start.12 = (bf16[8,8,1024]{2,1,0:T(8,128)(2,1)}, bf16[8,8,1024]{2,1,0:T(8,128)(2,1)}, u32[]{:S(2)}, u32[]{:S(2)}) collective-permute-start(bf16[8,8,1024]{2,1,0:T(8,128)(2,1)} %slice.9), channel_id=1, source_target_pairs={{0,64},{64,0},{1,65},{65,1},{2,66},{66,2},{3,67},{67,3},{4,68},{68... | collective-permute-start | bytes 393224 | tf_op jit(solution)/shard_map/ppermute | solution.py:229
  140.5 31.6 %collective-permute-start.13 = (bf16[8,8,2048]{2,1,0:T(8,128)(2,1)S(1)}, bf16[8,8,2048]{2,1,0:T(8,128)(2,1)S(1)}, u32[]{:S(2)}, u32[]{:S(2)}) collective-permute-start(bf16[8,8,2048]{2,1,0:T(8,128)(2,1)S(1)} %all-to-all-done.2.refs_0_), channel_id=1, source_target_pairs={{0,16},{16,0},{1,17},{17,1},{2,18},{18,2},{3,19},{19,3},{4,20},{20... | collective-permute-start | bytes 786440 | tf_op jit(solution)/shard_map/ppermute | solution.py:229
  142.4 29.7 %collective-permute-start.14 = (bf16[8,8,2048]{2,1,0:T(8,128)(2,1)S(1)}, bf16[8,8,2048]{2,1,0:T(8,128)(2,1)}, u32[]{:S(2)}, u32[]{:S(2)}) collective-permute-start(bf16[8,8,2048]{2,1,0:T(8,128)(2,1)S(1)} %collective-permute-done.9.refs_1_), channel_id=1, source_target_pairs={{0,16},{16,0},{1,17},{17,1},{2,18},{18,2},{3,19},{19,3},{4,20},{20... | collective-permute-start | bytes 786440 | tf_op jit(solution)/shard_map/ppermute | solution.py:229
  145.5 27.2 %collective-permute-start.15 = (bf16[8,8,2048]{2,1,0:T(8,128)(2,1)S(1)}, bf16[8,8,2048]{2,1,0:T(8,128)(2,1)}, u32[]{:S(2)}, u32[]{:S(2)}) collective-permute-start(bf16[8,8,2048]{2,1,0:T(8,128)(2,1)S(1)} %collective-permute-done.10.refs_2_), channel_id=1, source_target_pairs={{0,16},{16,0},{1,17},{17,1},{2,18},{18,2},{3,19},{19,3},{4,20},{20... | collective-permute-start | bytes 786440 | tf_op jit(solution)/shard_map/ppermute | solution.py:229
  165.3 7.5 %copy-start.12 = (bf16[8,8,1024]{2,1,0:T(8,128)(2,1)}, bf16[8,8,1024]{2,1,0:T(8,128)(2,1)S(1)}, u32[]{:S(2)}) copy-start(bf16[8,8,1024]{2,1,0:T(8,128)(2,1)S(1)} %collective-permute-done.11.refs_3_) | copy-start | bytes 393220
  165.3 6.7 %collective-permute-start.16 = (bf16[8,8,1024]{2,1,0:T(8,128)(2,1)S(1)}, bf16[8,8,1024]{2,1,0:T(8,128)(2,1)S(1)}, u32[]{:S(2)}, u32[]{:S(2)}) collective-permute-start(bf16[8,8,1024]{2,1,0:T(8,128)(2,1)S(1)} %collective-permute-done.11.refs_3_), channel_id=1, source_target_pairs={{0,16},{16,0},{1,17},{17,1},{2,18},{18,2},{3,19},{19,3},{4,20},{20... | collective-permute-start | bytes 393224 | tf_op jit(solution)/shard_map/ppermute | solution.py:229
  167.7 4.3 %collective-permute-start.17 = (bf16[8,8,1024]{2,1,0:T(8,128)(2,1)}, bf16[8,8,1024]{2,1,0:T(8,128)(2,1)S(1)}, u32[]{:S(2)}, u32[]{:S(2)}) collective-permute-start(bf16[8,8,1024]{2,1,0:T(8,128)(2,1)} %collective-permute-done.12.refs_4_), channel_id=1, source_target_pairs={{0,16},{16,0},{1,17},{17,1},{2,18},{18,2},{3,19},{19,3},{4,20},{20... | collective-permute-start | bytes 393224 | tf_op jit(solution)/shard_map/ppermute | solution.py:229
  (7 other events, 5.0 us)

commit v3 on v1

v3 whole, which is shorter than its diff:
```python
import jax
import jax.numpy as jnp
from jax import lax
from jax.sharding import Mesh
from jax.sharding import PartitionSpec as P

TENSOR = ("xh", "y")
DP = ("zh", "zl", "xl", "c")
SWAP = [(0, 1), (1, 0)]

bias_first = 0.9999734386011124
bias_second = 0.09520785288629112

F32 = jnp.float32
BF16 = jnp.bfloat16


def at(x, index, dim):
    return lax.dynamic_index_in_dim(x, index, dim, keepdims=False)


def gather_pair(x, axis, dim):
    got = jnp.expand_dims(lax.ppermute(x, axis, SWAP), dim)
    x = jnp.expand_dims(x, dim)
    place = lax.broadcasted_iota(jnp.int32, tuple(2 if d == dim else 1 for d in range(x.ndim)), dim)
    return jnp.where(place == lax.axis_index(axis), x, got)


def to_all(x, axis):
    n = lax.axis_size(axis)
    return lax.all_to_all(jnp.broadcast_to(x[None], (n, *x.shape)), axis, 0, 0, tiled=True)


def norm_backward(latent_rows, norm_gain, grad_rows):
    values = latent_rows.astype(F32)
    inverse_rms = lax.rsqrt(jnp.mean(values * values, axis=1, keepdims=True) + 1e-06)
    unit = values * inverse_rms
    scaled = grad_rows * norm_gain
    inner = jnp.mean(scaled * unit, axis=1, keepdims=True)
    return (inverse_rms * (scaled - unit * inner)).astype(BF16)


def local(
    latent_pre, norm_gain, kv_weight, down_weight, grad_kv, master, first_moment, second_moment
):
    values = latent_pre.astype(F32)
    inverse_rms = lax.rsqrt(jnp.mean(values * values, axis=1, keepdims=True) + 1e-06)
    normalized = (values * inverse_rms * norm_gain).astype(BF16)
    latents = normalized.shape[1]
    cols = grad_kv.shape[1]
    zh, zl, xl, c = (lax.axis_size(a) for a in DP)
    my_zl, my_xl, my_c = (lax.axis_index(a) for a in DP[1:])
    half = zh // 2
    rows = latents // (zh * zl * xl * c)
    grad_part = lax.dot_general(
        grad_kv, kv_weight, (((1,), (1,)), ((), ())), preferred_element_type=F32
    )
    share = grad_part.shape[0] // lax.axis_size(TENSOR)
    blocks = lax.all_to_all(
        grad_part.reshape(-1, share, grad_part.shape[1]), TENSOR, 0, 0, tiled=True
    )
    grad_kv_after, _ = lax.optimization_barrier((grad_kv, grad_part))

    def rows_of(core, dtype):
        place = lax.broadcasted_iota(jnp.int32, (latents // c, latents), 0)
        latent = lax.broadcasted_iota(jnp.int32, (latents // c, latents), 1)
        wanted = (place // rows * c + core) * rows + place % rows
        chosen = lax.dot_general(
            (latent == wanted).astype(BF16),
            normalized,
            (((1,), (1,)), ((), ())),
            preferred_element_type=F32,
        ).astype(BF16)
        part = lax.dot_general(
            chosen, grad_kv_after, (((1,), (0,)), ((), ())), preferred_element_type=F32
        )
        return part.astype(dtype)

    got = lax.ppermute(rows_of(1 - my_c, BF16), "c", SWAP)
    own = rows_of(my_c, F32)

    def piece(x, start, z=None, x_lo=None):
        starts = (start, 0 if z is None else z, 0 if x_lo is None else x_lo, 0, 0)
        sizes = (half, zl if z is None else 1, xl if x_lo is None else 1, rows, cols)
        block = lax.dynamic_slice(x.reshape(zh, zl, xl, rows, cols), starts, sizes)
        return block.reshape(*(n for n in sizes if n > 1)).astype(F32)

    def pair_sum(start, z=None, x_lo=None):
        return piece(own, start, z, x_lo) + piece(got, start, z, x_lo)

    p_got = lax.ppermute(pair_sum(0, None, 1 - my_xl).astype(BF16), "xl", SWAP)
    q_got = lax.ppermute(pair_sum(half, 1 - my_zl, None).astype(BF16), "zl", SWAP)
    p_send = (pair_sum(0, 1 - my_zl, my_xl) + at(p_got, 1 - my_zl, 1).astype(F32)).astype(BF16)
    p_last = lax.ppermute(p_send, "zl", SWAP)
    q_send = (pair_sum(half, my_zl, 1 - my_xl) + at(q_got, 1 - my_xl, 1).astype(F32)).astype(BF16)
    q_last = lax.ppermute(q_send, "xl", SWAP)
    p_last, q_last = lax.optimization_barrier((p_last, q_last))
    p = pair_sum(0, my_zl, my_xl) + at(p_got, my_zl, 1).astype(F32) + p_last.astype(F32)
    q = pair_sum(half, my_zl, my_xl) + at(q_got, my_xl, 1).astype(F32) + q_last.astype(F32)
    p = p.astype(BF16)
    q = q.astype(BF16)
    both = jnp.concatenate([p, q])
    both, blocks = lax.optimization_barrier((both, blocks))
    both = lax.all_to_all(both, "zh", 0, 0, tiled=True)
    grad_share = jnp.sum(blocks, axis=0)
    own_start = lax.axis_index(TENSOR) * share
    latent_share = lax.dynamic_slice_in_dim(latent_pre, own_start, share, 0)
    pre_share = norm_backward(latent_share, norm_gain, grad_share)
    both, pre_share = lax.optimization_barrier((both, pre_share))
    weight_grad = jnp.sum(both.astype(F32), axis=0)
    new_first = 0.9 * first_moment + 0.1 * weight_grad
    new_second = 0.999 * second_moment + 0.001 * weight_grad * weight_grad
    first_hat = new_first / bias_first
    second_hat = new_second / bias_second
    new_master = master - 0.01 * (first_hat / (jnp.sqrt(second_hat) + 1e-08) + 0.1 * master)
    rep = to_all(new_master.astype(BF16), "zh")
    rep, pre_share = lax.optimization_barrier((rep, pre_share))
    p = gather_pair(rep[:half], "zl", 1)
    q = gather_pair(rep[half:], "xl", 1)
    grad_pre = to_all(pre_share, TENSOR).reshape(latent_pre.shape)
    p = gather_pair(p, "xl", 2)
    q = gather_pair(q, "zl", 1)
    grad_hidden = lax.dot_general(
        grad_pre, down_weight, (((1,), (1,)), ((), ())), preferred_element_type=F32
    ).astype(BF16)
    new_replica = gather_pair(jnp.concatenate([p, q]), "c", 3).reshape(-1, cols)
    return (grad_hidden, new_master, new_first, new_second, new_replica)


def solution(mesh):
    torus = Mesh(mesh.devices.reshape(8, 2, 2, 2, 2, 8), ("zh", "zl", "xl", "c", "xh", "y"))
    placed = (
        P(DP, None),
        P(),
        P(None, TENSOR),
        P(TENSOR, None),
        P(DP, TENSOR),
        P(DP, TENSOR),
        P(DP, TENSOR),
        P(DP, TENSOR),
    )
    return jax.shard_map(
        local,
        mesh=torus,
        in_specs=placed,
        out_specs=(P(DP, TENSOR), P(DP, TENSOR), P(DP, TENSOR), P(DP, TENSOR), P(None, TENSOR)),
        check_vma=False,
    )
```

time: 179 us -> 150 us (0.84)
  waiting for transfers between devices: 72.4 us -> 33.8 us
  blocking collectives: 0 us -> 21.3 us
  starting transfers between devices: 71.7 us -> 63.5 us
  local copies, waits for them, and re-layouts: 6 us -> 2.62 us
  matrix products: 8.65 us -> 11.9 us
  other arithmetic: 16.3 us -> 14.2 us
    all_to_all x2 -> x1, waiting for transfers between devices: 22.5 us -> 0.01 us  [to_all(): lax.all_to_all(jnp.broadcast_to(x[None], (n, *x.shape)), axis, 0, 0, tile...]
    all_to_all x0 -> x1, blocking collectives: none -> 21.3 us  [to_all(): lax.all_to_all(jnp.broadcast_to(x[None], (n, *x.shape)), axis, 0, 0, tile...]
    all_to_all x1, waiting for transfers between devices: 19.1 us -> 0.01 us  [local(): lax.all_to_all(grad_part.reshape(-1, share, grad_part.shape[1]), TENSOR,...]
    convert_element_type x2 -> x4, other arithmetic: 0.06 us -> 5.67 us  [the longest x1 1.89 us: local(): pair_sum(half, 1 - my_zl, None).astype(BF16)]
    another operation x7 -> x0, other arithmetic: 5.45 us -> none  [gather_pair(): return jnp.stack([first, second], axis=dim)]
    all_to_all x2 -> x1, starting transfers between devices: 14.4 us -> 9.1 us  [to_all(): lax.all_to_all(jnp.broadcast_to(x[None], (n, *x.shape)), axis, 0, 0, tile...]
    all_to_all x1, starting transfers between devices: 17.9 us -> 13.1 us  [local(): both = lax.all_to_all(both, 'zh', 0, 0, tiled=True)]
    add x3 -> x1, other arithmetic: 3.34 us -> 0.01 us  [rows_of(): wanted = (place // rows * c + core) * rows + place % rows]
  transfers between devices with their start and end apart: 14 -> 13, of which waited for: 10 -> 8; matrix products, arithmetic and copies ran while one was open for 9% -> 11% of each run, Pallas kernels for 0% -> 0%
where the time goes in v3:
time: 150 us; the launch traced here: 148 us
  starting transfers between devices  63.5 us (42%)
  waiting for transfers between devices  33.8 us (23%)
  blocking collectives  21.3 us (14%)
  other arithmetic  14.2 us (9%)
  matrix products  11.9 us (8%)
  local copies, waits for them, and re-layouts  2.62 us (2%)
    all_to_all x1, blocking collectives, to_all(): lax.all_to_all(jnp.broadcast_to(x[None], (n, *x.shape)), axis, 0, 0, tile...  21.3 us
    all_to_all x1, waiting for transfers between devices, local(): both = lax.all_to_all(both, 'zh', 0, 0, tiled=True)  16.3 us
    ppermute x5, starting transfers between devices, gather_pair(): got = jnp.expand_dims(lax.ppermute(x, axis, SWAP), dim)  13.6 us
    all_to_all x1, starting transfers between devices, local(): both = lax.all_to_all(both, 'zh', 0, 0, tiled=True)  13.1 us
    all_to_all x1, starting transfers between devices, local(): lax.all_to_all(grad_part.reshape(-1, share, grad_part.shape[1]), TENSOR,...  10.1 us
    ppermute x1, starting transfers between devices, local(): p_got = lax.ppermute(pair_sum(0, None, 1 - my_xl).astype(BF16), 'xl', SWAP)  9.27 us
    all_to_all x1, starting transfers between devices, to_all(): lax.all_to_all(jnp.broadcast_to(x[None], (n, *x.shape)), axis, 0, 0, tile...  9.1 us
    ppermute x1, waiting for transfers between devices, local(): p_got = lax.ppermute(pair_sum(0, None, 1 - my_xl).astype(BF16), 'xl', SWAP)  6.77 us
  transfers between devices with their start and end apart: 13, of which 8 were waited for; matrix products, arithmetic and copies ran while one was open for 11% of the time, Pallas kernels for 0%

profile of v3, /device:TPU:6, one launch (start us, length us, event | category | flops | bytes accessed | tf_op | source)
XLA Modules:
  0.0 148.2 jit_solution(7158531462075424906)
XLA Ops:
  0.7 1.5 %copy-done = bf16[512,2048]{1,0:T(8,128)(2,1)S(1)} copy-done((bf16[512,2048]{1,0:T(8,128)(2,1)S(1)}, bf16[512,2048]{1,0:T(8,128)(2,1)}, u32[]{:S(2)}) %copy-start) | copy-done | bytes 2097176
  2.2 3.9 %fusion.87 = f32[512,512]{1,0:T(8,128)} fusion(bf16[512,2048]{1,0:T(8,128)(2,1)S(1)} %copy-done, bf16[512,2048]{1,0:T(8,128)(2,1)} %param.10), kind=kOutput, calls=%fused_computation.100 | convolution fusion | flops 1073741824 | bytes 5242880 | tf_op jit(solution)/shard_map/dot_general | solution.py:55
  6.3 2.1 %convolution_convert_fusion = bf16[256,2048]{1,0:T(8,128)(2,1)} fusion(bf16[512,2048]{1,0:T(8,128)(2,1)S(1)} %copy-done, s32[]{:T(128)S(6)} %sub.31, s32[256]{0:T(256)S(1)} %get-tuple-element.36, s32[256]{0:T(256)S(1)} %get-tuple-element.37, s32[256]{0:T(256)S(1)} %get-tuple-element.35, s32[256]{0:T(256)S(1)} %get-tuple-element.38, ...), kind=kOutput, calls=%fused_computation | convolution fusion | flops 673710080 | bytes 3678724 | tf_op jit(solution)/shard_map/dot_general | solution.py:74
  8.5 1.9 %collective-permute-start = (bf16[256,2048]{1,0:T(8,128)(2,1)}, bf16[256,2048]{1,0:T(8,128)(2,1)}, u32[]{:S(2)}, u32[]{:S(2)}) collective-permute-start(bf16[256,2048]{1,0:T(8,128)(2,1)} %convolution_convert_fusion), channel_id=1, source_target_pairs={{0,16},{16,0},{1,17},{17,1},{2,18},{18,2},{3,19},{19,3},{4,20},{20... | collective-permute-start | bytes 3145736 | tf_op jit(solution)/shard_map/ppermute | solution.py:79
  10.4 10.1 %all-to-all-start = ((f32[16,32,512]{2,1,0:T(8,128)}), f32[16,32,512]{2,1,0:T(8,128)S(1)}, u32[]{:S(2)}, u32[]{:S(2)}) async-start(f32[16,32,512]{2,1,0:T(8,128)} %bitcast.88), calls=%async_computation | async-start | bytes 2097152 | tf_op jit(solution)/shard_map/all_to_all | solution.py:59
  20.5 3.5 %fusion = f32[256,2048]{1,0:T(8,128)} fusion(bf16[512,2048]{1,0:T(8,128)(2,1)S(1)} %copy-done, s32[256]{0:T(256)S(1)} %get-tuple-element.36, s32[256]{0:T(256)S(1)} %get-tuple-element.37, s32[]{:T(128)S(6)} %axis_index.33, s32[256]{0:T(256)S(1)} %get-tuple-element.35, s32[256]{0:T(256)S(1)} %get-tuple-element.38, pred[256]{0:T(512)(128)(4,1)S(1)} %get-tuple-element.33, ...), kind=kOutput, calls=%fused_computation.7 | convolution fusion | flops 673185792 | bytes 4727300 | tf_op jit(solution)/shard_map/dot_general | solution.py:74
  24.0 1.2 fusion.12
  25.2 9.3 %collective-permute-start.1 = (bf16[4,2,8,2048]{3,2,0,1:T(8,128)(2,1)S(1)}, bf16[4,2,8,2048]{3,2,0,1:T(8,128)(2,1)}, u32[]{:S(2)}, u32[]{:S(2)}) collective-permute-start(bf16[4,2,8,2048]{3,2,0,1:T(8,128)(2,1)S(1)} %fusion.12), channel_id=1, source_target_pairs={{0,32},{32,0},{1,33},{33,1},{2,34},{34,2},{3,35},{35,3},{4,36},{36... | collective-permute-start | bytes 786440 | tf_op jit(solution)/shard_map/ppermute | solution.py:91
  34.5 1.9 %fusion.13 = bf16[4,2,8,2048]{3,2,0,1:T(8,128)(2,1)} fusion(bf16[8,2,2,8,2048]{4,3,2,1,0:T(8,128)(2,1)} %bitcast.1, s32[]{:T(128)S(6)} %select_n.88, f32[8,2,2,8,2048]{4,3,2,1,0:T(8,128)} %bitcast.85), kind=kLoop, calls=%fused_computation.25 | loop fusion | flops 393216 | bytes 1049600 | tf_op jit(solution)/shard_map/convert_element_type | solution.py:92
  36.4 1.9 %collective-permute-start.3 = (bf16[4,2,8,2048]{3,2,0,1:T(8,128)(2,1)}, bf16[4,2,8,2048]{3,2,0,1:T(8,128)(2,1)}, u32[]{:S(2)}, u32[]{:S(2)}) collective-permute-start(bf16[4,2,8,2048]{3,2,0,1:T(8,128)(2,1)} %fusion.13), channel_id=1, source_target_pairs={{0,64},{64,0},{1,65},{65,1},{2,66},{66,2},{3,67},{67,3},{4,68},{68... | collective-permute-start | bytes 786440 | tf_op jit(solution)/shard_map/ppermute | solution.py:92
  38.3 6.8 %collective-permute-done.1 = bf16[4,2,8,2048]{3,2,0,1:T(8,128)(2,1)} collective-permute-done((bf16[4,2,8,2048]{3,2,0,1:T(8,128)(2,1)S(1)}, bf16[4,2,8,2048]{3,2,0,1:T(8,128)(2,1)}, u32[]{:S(2)}, u32[]{:S(2)}) %collective-permute-start.1) | collective-permute-done | bytes 262176 | tf_op jit(solution)/shard_map/ppermute | solution.py:91
  45.0 1.7 %collective-permute-done.3 = bf16[4,2,8,2048]{3,2,0,1:T(8,128)(2,1)} collective-permute-done((bf16[4,2,8,2048]{3,2,0,1:T(8,128)(2,1)}, bf16[4,2,8,2048]{3,2,0,1:T(8,128)(2,1)}, u32[]{:S(2)}, u32[]{:S(2)}) %collective-permute-start.3) | collective-permute-done | bytes 262176 | tf_op jit(solution)/shard_map/ppermute | solution.py:92
  46.7 1.3 fusion.16
  48.0 2.2 %collective-permute-start.2 = (bf16[4,8,2048]{2,1,0:T(8,128)(2,1)S(1)}, bf16[4,8,2048]{2,1,0:T(8,128)(2,1)S(1)}, u32[]{:S(2)}, u32[]{:S(2)}) collective-permute-start(bf16[4,8,2048]{2,1,0:T(8,128)(2,1)S(1)} %get-tuple-element.30), channel_id=1, source_target_pairs={{0,64},{64,0},{1,65},{65,1},{2,66},{66,2},{3,67},{67,3},{4,68},{68... | collective-permute-start | bytes 393224 | tf_op jit(solution)/shard_map/ppermute | solution.py:94
  50.2 2.3 %collective-permute-start.4 = (bf16[4,8,2048]{2,1,0:T(8,128)(2,1)S(1)}, bf16[4,8,2048]{2,1,0:T(8,128)(2,1)S(1)}, u32[]{:S(2)}, u32[]{:S(2)}) collective-permute-start(bf16[4,8,2048]{2,1,0:T(8,128)(2,1)S(1)} %get-tuple-element.29), channel_id=1, source_target_pairs={{0,32},{32,0},{1,33},{33,1},{2,34},{34,2},{3,35},{35,3},{4,36},{36... | collective-permute-start | bytes 393224 | tf_op jit(solution)/shard_map/ppermute | solution.py:96
  52.6 2.3 %collective-permute-done.2 = bf16[4,8,2048]{2,1,0:T(8,128)(2,1)S(1)} collective-permute-done((bf16[4,8,2048]{2,1,0:T(8,128)(2,1)S(1)}, bf16[4,8,2048]{2,1,0:T(8,128)(2,1)S(1)}, u32[]{:S(2)}, u32[]{:S(2)}) %collective-permute-start.2) | collective-permute-done | bytes 131104 | tf_op jit(solution)/shard_map/ppermute | solution.py:94
  54.9 2.4 %collective-permute-done.4 = bf16[4,8,2048]{2,1,0:T(8,128)(2,1)S(1)} collective-permute-done((bf16[4,8,2048]{2,1,0:T(8,128)(2,1)S(1)}, bf16[4,8,2048]{2,1,0:T(8,128)(2,1)S(1)}, u32[]{:S(2)}, u32[]{:S(2)}) %collective-permute-start.4) | collective-permute-done | bytes 131104 | tf_op jit(solution)/shard_map/ppermute | solution.py:96
  57.2 1.3 fusion.23
  59.3 13.1 %all-to-all-start.1 = ((bf16[8,8,2048]{2,1,0:T(8,128)(2,1)}), bf16[8,8,2048]{2,1,0:T(8,128)(2,1)S(1)}, u32[]{:S(2)}, u32[]{:S(2)}) async-start(bf16[8,8,2048]{2,1,0:T(8,128)(2,1)} %pad_maximum_fusion.1), calls=%async_computation.1 | async-start | bytes 524288 | tf_op jit(solution)/shard_map/all_to_all | solution.py:104
  73.3 0.9 fusion.68
  75.1 16.3 %all-to-all-done.1 = bf16[8,8,2048]{2,1,0:T(8,128)(2,1)S(1)} async-done(((bf16[8,8,2048]{2,1,0:T(8,128)(2,1)}), bf16[8,8,2048]{2,1,0:T(8,128)(2,1)S(1)}, u32[]{:S(2)}, u32[]{:S(2)}) %all-to-all-start.1) | async-done | bytes 262176 | tf_op jit(solution)/shard_map/all_to_all | solution.py:104
  91.5 1.6 %fusion.84 = (bf16[8,2048]{1,0:T(8,128)(2,1)S(1)}, f32[8,2048]{1,0:T(8,128)}, f32[8,2048]{1,0:T(8,128)}, f32[8,2048]{1,0:T(8,128)}) fusion(f32[8,2048]{1,0:T(8,128)S(1)} %copy-done.2, f32[8,2048]{1,0:T(8,128)S(1)} %convert_reduce_fusion, f32[8,2048]{1,0:T(8,128)} %param.14, f32[8,2048]{1,0:T(8,128)} %param.15), kind=kLoop, calls=%fused_computation.98 | loop fusion | flops 262144 | bytes 491520 | tf_op jit(solution)/shard_map/convert_element_type | solution.py:116
  93.0 21.3 %all_to_all.20 = bf16[8,8,2048]{2,1,0:T(8,128)(2,1)S(1)} all-to-all(bf16[8,8,2048]{2,1,0:T(8,128)(2,1)S(1)} %broadcast_in_dim.146), channel_id=1, replica_groups=mesh['zh'=8,'zl'=2,'xl'=2,'c'=2,'xh'=2,'y'=8] {'zh'}, dimensions={0} | all-to-all | bytes 524288 | tf_op jit(solution)/shard_map/all_to_all | solution.py:31
  114.3 1.9 %collective-permute-start.5 = (bf16[4,8,2048]{2,1,0:T(8,128)(2,1)S(1)}, bf16[4,8,2048]{2,1,0:T(8,128)(2,1)S(1)}, u32[]{:S(2)}, u32[]{:S(2)}) collective-permute-start(bf16[4,8,2048]{2,1,0:T(8,128)(2,1)S(1)} %get-tuple-element.31), channel_id=1, source_target_pairs={{0,64},{64,0},{1,65},{65,1},{2,66},{66,2},{3,67},{67,3},{4,68},{68... | collective-permute-start | bytes 393224 | tf_op jit(solution)/shard_map/ppermute | solution.py:23
  116.3 3.1 %collective-permute-start.7 = (bf16[4,8,2048]{2,1,0:T(8,128)(2,1)S(1)}, bf16[4,8,2048]{2,1,0:T(8,128)(2,1)S(1)}, u32[]{:S(2)}, u32[]{:S(2)}) collective-permute-start(bf16[4,8,2048]{2,1,0:T(8,128)(2,1)S(1)} %get-tuple-element.32), channel_id=1, source_target_pairs={{0,32},{32,0},{1,33},{33,1},{2,34},{34,2},{3,35},{35,3},{4,36},{36... | collective-permute-start | bytes 393224 | tf_op jit(solution)/shard_map/ppermute | solution.py:23
  120.3 9.1 %all-to-all-start.3 = ((bf16[16,32,512]{2,1,0:T(8,128)(2,1)}), bf16[16,32,512]{2,1,0:T(8,128)(2,1)}, u32[]{:S(2)}, u32[]{:S(2)}) async-start(bf16[16,32,512]{2,1,0:T(8,128)(2,1)} %broadcast_in_dim.147), calls=%async_computation.3 | async-start | bytes 1048576 | tf_op jit(solution)/shard_map/all_to_all | solution.py:31
  129.5 2.7 %collective-permute-start.6 = (bf16[4,2,8,2048]{3,2,1,0:T(8,128)(2,1)S(1)}, bf16[4,2,8,2048]{3,2,1,0:T(8,128)(2,1)S(1)}, u32[]{:S(2)}, u32[]{:S(2)}) collective-permute-start(bf16[4,2,8,2048]{3,2,1,0:T(8,128)(2,1)S(1)} %broadcast_select_fusion.3), channel_id=1, source_target_pairs={{0,32},{32,0},{1,33},{33,1},{2,34},{34,2},{3,35},{35,3},{4,36},{36... | collective-permute-start | bytes 786440 | tf_op jit(solution)/shard_map/ppermute | solution.py:23
  132.3 3.9 %collective-permute-start.8 = (bf16[4,2,8,2048]{3,2,1,0:T(8,128)(2,1)S(1)}, bf16[4,2,8,2048]{3,2,1,0:T(8,128)(2,1)S(1)}, u32[]{:S(2)}, u32[]{:S(2)}) collective-permute-start(bf16[4,2,8,2048]{3,2,1,0:T(8,128)(2,1)S(1)} %broadcast_select_fusion.2), channel_id=1, source_target_pairs={{0,64},{64,0},{1,65},{65,1},{2,66},{66,2},{3,67},{67,3},{4,68},{68... | collective-permute-start | bytes 786440 | tf_op jit(solution)/shard_map/ppermute | solution.py:23
  136.2 3.7 %collective-permute-done.6 = bf16[4,2,8,2048]{3,2,1,0:T(8,128)(2,1)S(1)} collective-permute-done((bf16[4,2,8,2048]{3,2,1,0:T(8,128)(2,1)S(1)}, bf16[4,2,8,2048]{3,2,1,0:T(8,128)(2,1)S(1)}, u32[]{:S(2)}, u32[]{:S(2)}) %collective-permute-start.6) | collective-permute-done | bytes 262176 | tf_op jit(solution)/shard_map/ppermute | solution.py:23
  140.8 1.9 %collective-permute-start.9 = (bf16[8,2,2,8,2048]{4,3,2,1,0:T(8,128)(2,1)S(1)}, bf16[8,2,2,8,2048]{4,3,2,1,0:T(8,128)(2,1)}, u32[]{:S(2)}, u32[]{:S(2)}) collective-permute-start(bf16[8,2,2,8,2048]{4,3,2,1,0:T(8,128)(2,1)S(1)} %pad_maximum_fusion), channel_id=1, source_target_pairs={{0,16},{16,0},{1,17},{17,1},{2,18},{18,2},{3,19},{19,3},{4,20},{20... | collective-permute-start | bytes 3145736 | tf_op jit(solution)/shard_map/ppermute | solution.py:23
  142.9 2.4 %convolution_convert_fusion.1 = bf16[512,448]{0,1:T(8,128)(2,1)} fusion(bf16[512,512]{1,0:T(8,128)(2,1)} %bitcast.13, bf16[448,512]{1,0:T(8,128)(2,1)} %param.11), kind=kOutput, calls=%fused_computation.4 | convolution fusion | flops 235110400 | bytes 1441792 | tf_op jit(solution)/shard_map/dot_general | solution.py:123
  145.4 2.7 %bitcast_select_fusion = bf16[512,2048]{1,0:T(8,128)(2,1)} fusion(pred[512]{0:T(512)(128)(4,1)S(1)} %broadcast_in_dim.149, bf16[8,2,2,8,2048]{4,3,2,1,0:T(8,128)(2,1)} %collective-permute-done.9, bf16[8,2,2,8,2048]{4,3,2,1,0:T(8,128)(2,1)S(1)} %pad_maximum_fusion), kind=kLoop, calls=%fused_computation.1 | loop fusion | flops 1048576 | bytes 4194816 | tf_op jit(solution)/shard_map/jit(_where)/select_n | solution.py:26
  (39 shorter events, 5.0 us)
Async XLA Ops:
  0.6 1.6 %copy-start = (bf16[512,2048]{1,0:T(8,128)(2,1)S(1)}, bf16[512,2048]{1,0:T(8,128)(2,1)}, u32[]{:S(2)}) copy-start(bf16[512,2048]{1,0:T(8,128)(2,1)} %param.12) | copy-start | bytes 6291460
  2.2 3.9 %copy-start.1 = (bf16[512,512]{1,0:T(8,128)(2,1)S(1)}, bf16[512,512]{1,0:T(8,128)(2,1)}, u32[]{:S(2)}) copy-start(bf16[512,512]{1,0:T(8,128)(2,1)} %param.8) | copy-start | bytes 1572868
  2.2 4.1 %copy-start.3 = (f32[512]{0:T(512)S(1)}, f32[512]{0:T(512)}, u32[]{:S(2)}) copy-start(f32[512]{0:T(512)} %param.9) | copy-start | bytes 6148
  8.5 15.5 %collective-permute-start = (bf16[256,2048]{1,0:T(8,128)(2,1)}, bf16[256,2048]{1,0:T(8,128)(2,1)}, u32[]{:S(2)}, u32[]{:S(2)}) collective-permute-start(bf16[256,2048]{1,0:T(8,128)(2,1)} %convolution_convert_fusion), channel_id=1, source_target_pairs={{0,16},{16,0},{1,17},{17,1},{2,18},{18,2},{3,19},{19,3},{4,20},{20... | collective-permute-start | bytes 3145736 | tf_op jit(solution)/shard_map/ppermute | solution.py:79
  10.4 48.9 %all-to-all-start = ((f32[16,32,512]{2,1,0:T(8,128)}), f32[16,32,512]{2,1,0:T(8,128)S(1)}, u32[]{:S(2)}, u32[]{:S(2)}) async-start(f32[16,32,512]{2,1,0:T(8,128)} %bitcast.88), calls=%async_computation | async-start | bytes 2097152 | tf_op jit(solution)/shard_map/all_to_all | solution.py:59
  25.2 19.9 %collective-permute-start.1 = (bf16[4,2,8,2048]{3,2,0,1:T(8,128)(2,1)S(1)}, bf16[4,2,8,2048]{3,2,0,1:T(8,128)(2,1)}, u32[]{:S(2)}, u32[]{:S(2)}) collective-permute-start(bf16[4,2,8,2048]{3,2,0,1:T(8,128)(2,1)S(1)} %fusion.12), channel_id=1, source_target_pairs={{0,32},{32,0},{1,33},{33,1},{2,34},{34,2},{3,35},{35,3},{4,36},{36... | collective-permute-start | bytes 786440 | tf_op jit(solution)/shard_map/ppermute | solution.py:91
  36.4 10.3 %collective-permute-start.3 = (bf16[4,2,8,2048]{3,2,0,1:T(8,128)(2,1)}, bf16[4,2,8,2048]{3,2,0,1:T(8,128)(2,1)}, u32[]{:S(2)}, u32[]{:S(2)}) collective-permute-start(bf16[4,2,8,2048]{3,2,0,1:T(8,128)(2,1)} %fusion.13), channel_id=1, source_target_pairs={{0,64},{64,0},{1,65},{65,1},{2,66},{66,2},{3,67},{67,3},{4,68},{68... | collective-permute-start | bytes 786440 | tf_op jit(solution)/shard_map/ppermute | solution.py:92
  48.0 6.9 %collective-permute-start.2 = (bf16[4,8,2048]{2,1,0:T(8,128)(2,1)S(1)}, bf16[4,8,2048]{2,1,0:T(8,128)(2,1)S(1)}, u32[]{:S(2)}, u32[]{:S(2)}) collective-permute-start(bf16[4,8,2048]{2,1,0:T(8,128)(2,1)S(1)} %get-tuple-element.30), channel_id=1, source_target_pairs={{0,64},{64,0},{1,65},{65,1},{2,66},{66,2},{3,67},{67,3},{4,68},{68... | collective-permute-start | bytes 393224 | tf_op jit(solution)/shard_map/ppermute | solution.py:94
  50.2 41.2 %copy-start.2 = (f32[8,2048]{1,0:T(8,128)S(1)}, f32[8,2048]{1,0:T(8,128)}, u32[]{:S(2)}) copy-start(f32[8,2048]{1,0:T(8,128)} %param.13) | copy-start | bytes 196612
  50.2 7.0 %collective-permute-start.4 = (bf16[4,8,2048]{2,1,0:T(8,128)(2,1)S(1)}, bf16[4,8,2048]{2,1,0:T(8,128)(2,1)S(1)}, u32[]{:S(2)}, u32[]{:S(2)}) collective-permute-start(bf16[4,8,2048]{2,1,0:T(8,128)(2,1)S(1)} %get-tuple-element.29), channel_id=1, source_target_pairs={{0,32},{32,0},{1,33},{33,1},{2,34},{34,2},{3,35},{35,3},{4,36},{36... | collective-permute-start | bytes 393224 | tf_op jit(solution)/shard_map/ppermute | solution.py:96
  59.3 32.1 %all-to-all-start.1 = ((bf16[8,8,2048]{2,1,0:T(8,128)(2,1)}), bf16[8,8,2048]{2,1,0:T(8,128)(2,1)S(1)}, u32[]{:S(2)}, u32[]{:S(2)}) async-start(bf16[8,8,2048]{2,1,0:T(8,128)(2,1)} %pad_maximum_fusion.1), calls=%async_computation.1 | async-start | bytes 524288 | tf_op jit(solution)/shard_map/all_to_all | solution.py:104
  114.3 15.0 %collective-permute-start.5 = (bf16[4,8,2048]{2,1,0:T(8,128)(2,1)S(1)}, bf16[4,8,2048]{2,1,0:T(8,128)(2,1)S(1)}, u32[]{:S(2)}, u32[]{:S(2)}) collective-permute-start(bf16[4,8,2048]{2,1,0:T(8,128)(2,1)S(1)} %get-tuple-element.31), channel_id=1, source_target_pairs={{0,64},{64,0},{1,65},{65,1},{2,66},{66,2},{3,67},{67,3},{4,68},{68... | collective-permute-start | bytes 393224 | tf_op jit(solution)/shard_map/ppermute | solution.py:23
  116.3 15.9 %collective-permute-start.7 = (bf16[4,8,2048]{2,1,0:T(8,128)(2,1)S(1)}, bf16[4,8,2048]{2,1,0:T(8,128)(2,1)S(1)}, u32[]{:S(2)}, u32[]{:S(2)}) collective-permute-start(bf16[4,8,2048]{2,1,0:T(8,128)(2,1)S(1)} %get-tuple-element.32), channel_id=1, source_target_pairs={{0,32},{32,0},{1,33},{33,1},{2,34},{34,2},{3,35},{35,3},{4,36},{36... | collective-permute-start | bytes 393224 | tf_op jit(solution)/shard_map/ppermute | solution.py:23
  120.3 22.6 %all-to-all-start.3 = ((bf16[16,32,512]{2,1,0:T(8,128)(2,1)}), bf16[16,32,512]{2,1,0:T(8,128)(2,1)}, u32[]{:S(2)}, u32[]{:S(2)}) async-start(bf16[16,32,512]{2,1,0:T(8,128)(2,1)} %broadcast_in_dim.147), calls=%async_computation.3 | async-start | bytes 1048576 | tf_op jit(solution)/shard_map/all_to_all | solution.py:31
  129.5 10.5 %collective-permute-start.6 = (bf16[4,2,8,2048]{3,2,1,0:T(8,128)(2,1)S(1)}, bf16[4,2,8,2048]{3,2,1,0:T(8,128)(2,1)S(1)}, u32[]{:S(2)}, u32[]{:S(2)}) collective-permute-start(bf16[4,2,8,2048]{3,2,1,0:T(8,128)(2,1)S(1)} %broadcast_select_fusion.3), channel_id=1, source_target_pairs={{0,32},{32,0},{1,33},{33,1},{2,34},{34,2},{3,35},{35,3},{4,36},{36... | collective-permute-start | bytes 786440 | tf_op jit(solution)/shard_map/ppermute | solution.py:23
  132.3 8.3 %collective-permute-start.8 = (bf16[4,2,8,2048]{3,2,1,0:T(8,128)(2,1)S(1)}, bf16[4,2,8,2048]{3,2,1,0:T(8,128)(2,1)S(1)}, u32[]{:S(2)}, u32[]{:S(2)}) collective-permute-start(bf16[4,2,8,2048]{3,2,1,0:T(8,128)(2,1)S(1)} %broadcast_select_fusion.2), channel_id=1, source_target_pairs={{0,64},{64,0},{1,65},{65,1},{2,66},{66,2},{3,67},{67,3},{4,68},{68... | collective-permute-start | bytes 786440 | tf_op jit(solution)/shard_map/ppermute | solution.py:23
  140.8 4.7 %collective-permute-start.9 = (bf16[8,2,2,8,2048]{4,3,2,1,0:T(8,128)(2,1)S(1)}, bf16[8,2,2,8,2048]{4,3,2,1,0:T(8,128)(2,1)}, u32[]{:S(2)}, u32[]{:S(2)}) collective-permute-start(bf16[8,2,2,8,2048]{4,3,2,1,0:T(8,128)(2,1)S(1)} %pad_maximum_fusion), channel_id=1, source_target_pairs={{0,16},{16,0},{1,17},{17,1},{2,18},{18,2},{3,19},{19,3},{4,20},{20... | collective-permute-start | bytes 3145736 | tf_op jit(solution)/shard_map/ppermute | solution.py:23

commit v4 on v3

--- a/solution.py
+++ b/solution.py
@@ -3,6 +3,7 @@
 from jax import lax
 from jax.sharding import Mesh
 from jax.sharding import PartitionSpec as P
+
 
 TENSOR = ("xh", "y")
 DP = ("zh", "zl", "xl", "c")
@@ -52,32 +53,34 @@
     my_zl, my_xl, my_c = (lax.axis_index(a) for a in DP[1:])
     half = zh // 2
     rows = latents // (zh * zl * xl * c)
+
+    def rows_of(core):
+        place = lax.broadcasted_iota(jnp.int32, (latents // c, latents), 0)
+        latent = lax.broadcasted_iota(jnp.int32, (latents // c, latents), 1)
+        return latent == (place // rows * c + core) * rows + place % rows
+
+    picks = jnp.concatenate([rows_of(1 - my_c), rows_of(my_c)]).astype(BF16)
+    picked = lax.dot_general(
+        picks, normalized, (((1,), (1,)), ((), ())), preferred_element_type=F32
+    ).astype(BF16)
+    picked = lax.optimization_barrier(picked)
+
+    def product(lhs, rhs):
+        return lax.dot_general(lhs, rhs, (((1,), (0,)), ((), ())), preferred_element_type=F32)
+
+    send = product(picked[: latents // c], grad_kv).astype(BF16)
+    got = lax.ppermute(send, "c", SWAP)
+    grad_kv, _ = lax.optimization_barrier((grad_kv, send))
     grad_part = lax.dot_general(
         grad_kv, kv_weight, (((1,), (1,)), ((), ())), preferred_element_type=F32
     )
-    share = grad_part.shape[0] // lax.axis_size(TENSOR)
+    pair = grad_part.shape[0] // lax.axis_size("y")
+    share = pair // lax.axis_size("xh")
     blocks = lax.all_to_all(
-        grad_part.reshape(-1, share, grad_part.shape[1]), TENSOR, 0, 0, tiled=True
+        grad_part.reshape(-1, pair, grad_part.shape[1]), "y", 0, 0, tiled=True
     )
-    grad_kv_after, _ = lax.optimization_barrier((grad_kv, grad_part))
-
-    def rows_of(core, dtype):
-        place = lax.broadcasted_iota(jnp.int32, (latents // c, latents), 0)
-        latent = lax.broadcasted_iota(jnp.int32, (latents // c, latents), 1)
-        wanted = (place // rows * c + core) * rows + place % rows
-        chosen = lax.dot_general(
-            (latent == wanted).astype(BF16),
-            normalized,
-            (((1,), (1,)), ((), ())),
-            preferred_element_type=F32,
-        ).astype(BF16)
-        part = lax.dot_general(
-            chosen, grad_kv_after, (((1,), (0,)), ((), ())), preferred_element_type=F32
-        )
-        return part.astype(dtype)
-
-    got = lax.ppermute(rows_of(1 - my_c, BF16), "c", SWAP)
-    own = rows_of(my_c, F32)
+    grad_kv, _ = lax.optimization_barrier((grad_kv, grad_part))
+    own = product(picked[latents // c :], grad_kv)
 
     def piece(x, start, z=None, x_lo=None):
         starts = (start, 0 if z is None else z, 0 if x_lo is None else x_lo, 0, 0)
@@ -102,8 +105,10 @@
     both = jnp.concatenate([p, q])
     both, blocks = lax.optimization_barrier((both, blocks))
     both = lax.all_to_all(both, "zh", 0, 0, tiled=True)
-    grad_share = jnp.sum(blocks, axis=0)
-    own_start = lax.axis_index(TENSOR) * share
+    grad_pair = jnp.sum(blocks, axis=0).reshape(-1, share, blocks.shape[2])
+    my_xh = lax.axis_index("xh")
+    grad_share = at(grad_pair, my_xh, 0) + lax.ppermute(at(grad_pair, 1 - my_xh, 0), "xh", SWAP)
+    own_start = lax.axis_index("y") * pair + my_xh * share
     latent_share = lax.dynamic_slice_in_dim(latent_pre, own_start, share, 0)
     pre_share = norm_backward(latent_share, norm_gain, grad_share)
     both, pre_share = lax.optimization_barrier((both, pre_share))
@@ -114,10 +119,11 @@
     second_hat = new_second / bias_second
     new_master = master - 0.01 * (first_hat / (jnp.sqrt(second_hat) + 1e-08) + 0.1 * master)
     rep = to_all(new_master.astype(BF16), "zh")
-    rep, pre_share = lax.optimization_barrier((rep, pre_share))
+    pre_pair = gather_pair(pre_share, "xh", 0).reshape(pair, -1)
+    rep, pre_pair = lax.optimization_barrier((rep, pre_pair))
     p = gather_pair(rep[:half], "zl", 1)
     q = gather_pair(rep[half:], "xl", 1)
-    grad_pre = to_all(pre_share, TENSOR).reshape(latent_pre.shape)
+    grad_pre = to_all(pre_pair, "y").reshape(latent_pre.shape)
     p = gather_pair(p, "xl", 2)
     q = gather_pair(q, "zl", 1)
     grad_hidden = lax.dot_general(

time: 150 us -> 149 us (level)
  the two profiles are of different devices: /device:TPU:6 before, /device:TPU:1 now
where the time goes in v4:
time: 149 us; the launch traced here: 147 us
  starting transfers between devices  80.8 us (54%)
  waiting for transfers between devices  36.1 us (24%)
  other arithmetic  15.8 us (11%)
  matrix products  10.9 us (7%)
  local copies, waits for them, and re-layouts  2.73 us (2%)
    ppermute x6, starting transfers between devices, gather_pair(): got = jnp.expand_dims(lax.ppermute(x, axis, SWAP), dim)  26.6 us
    ppermute x1, starting transfers between devices, local(): got = lax.ppermute(send, 'c', SWAP)  16 us
    all_to_all x2, starting transfers between devices, to_all(): lax.all_to_all(jnp.broadcast_to(x[None], (n, *x.shape)), axis, 0, 0, tile...  10.6 us
    all_to_all x1, starting transfers between devices, local(): both = lax.all_to_all(both, 'zh', 0, 0, tiled=True)  10.6 us
    all_to_all x2, waiting for transfers between devices, to_all(): lax.all_to_all(jnp.broadcast_to(x[None], (n, *x.shape)), axis, 0, 0, tile...  9.8 us
    all_to_all x1, waiting for transfers between devices, local(): both = lax.all_to_all(both, 'zh', 0, 0, tiled=True)  7.98 us
    ppermute x1, waiting for transfers between devices, local(): lax.ppermute(pair_sum(half, 1 - my_zl, None).astype(BF16), 'zl', SWAP)  6.2 us
    ppermute x6, waiting for transfers between devices, gather_pair(): got = jnp.expand_dims(lax.ppermute(x, axis, SWAP), dim)  5.27 us
  transfers between devices with their start and end apart: 16, of which 10 were waited for; matrix products, arithmetic and copies ran while one was open for 13% of the time, Pallas kernels for 0%

profile of v4, /device:TPU:1, one launch (start us, length us, event | category | flops | bytes accessed | tf_op | source)
XLA Modules:
  0.0 147.3 jit_solution(13529826071092511762)
XLA Ops:
  2.4 1.6 %convolution_convert_fusion.1 = bf16[512,512]{1,0:T(8,128)(2,1)S(1)} fusion(pred[256,512]{1,0:T(32,128)(4,1)S(1)} %get-tuple-element.36, pred[256,512]{1,0:T(32,128)(4,1)S(1)} %get-tuple-element.35, bf16[512,512]{1,0:T(8,128)(2,1)} %param.8, f32[512]{0:T(512)} %param.9, f32[512]{0:T(512)S(1)} %add_rsqrt_fusion), kind=kOutput, calls=%fused_computation.4 | convolution fusion | flops 270008320 | bytes 1314816 | tf_op jit(solution)/shard_map/dot_general | solution.py:63
  4.8 1.7 %convolution_convert_fusion = bf16[256,2048]{1,0:T(8,128)(2,1)} fusion(bf16[512,2048]{1,0:T(8,128)(2,1)S(1)} %copy-done, bf16[512,512]{1,0:T(8,128)(2,1)S(1)} %convolution_convert_fusion.1), kind=kOutput, calls=%fused_computation | convolution fusion | flops 537395200 | bytes 3407872 | tf_op jit(solution)/shard_map/dot_general | solution.py:69
  6.5 16.0 %collective-permute-start = (bf16[256,2048]{1,0:T(8,128)(2,1)}, bf16[256,2048]{1,0:T(8,128)(2,1)}, u32[]{:S(2)}, u32[]{:S(2)}) collective-permute-start(bf16[256,2048]{1,0:T(8,128)(2,1)} %convolution_convert_fusion), channel_id=1, source_target_pairs={{0,16},{16,0},{1,17},{17,1},{2,18},{18,2},{3,19},{19,3},{4,20},{20... | collective-permute-start | bytes 3145736 | tf_op jit(solution)/shard_map/ppermute | solution.py:72
  22.5 2.3 %fusion.45 = f32[512,512]{1,0:T(8,128)} fusion(bf16[512,2048]{1,0:T(8,128)(2,1)S(1)} %copy-done, bf16[512,2048]{1,0:T(8,128)(2,1)S(1)} %copy-done.3), kind=kOutput, calls=%fused_computation.90 | convolution fusion | flops 1073741824 | bytes 5242880 | tf_op jit(solution)/shard_map/dot_general | solution.py:74
  24.8 3.6 %all-to-all-start = ((f32[8,64,512]{2,1,0:T(8,128)}), f32[8,64,512]{2,1,0:T(8,128)S(1)}, u32[]{:S(2)}, u32[]{:S(2)}) async-start(f32[8,64,512]{2,1,0:T(8,128)} %bitcast.103), calls=%async_computation | async-start | bytes 2097152 | tf_op jit(solution)/shard_map/all_to_all | solution.py:79
  28.3 3.0 %fusion.16 = f32[256,2048]{1,0:T(8,128)} fusion(bf16[512,2048]{1,0:T(8,128)(2,1)S(1)} %copy-done, bf16[512,512]{1,0:T(8,128)(2,1)} %copy-done.1), kind=kOutput, calls=%fused_computation.30 | convolution fusion | flops 536870912 | bytes 4456448 | tf_op jit(solution)/shard_map/dot_general | solution.py:69
  32.5 1.9 %fusion.14 = bf16[4,2,8,2048]{3,2,0,1:T(8,128)(2,1)} fusion(bf16[8,2,2,8,2048]{4,3,2,1,0:T(8,128)(2,1)} %bitcast.1, s32[]{:T(128)S(6)} %select_n.100, f32[8,2,2,8,2048]{4,3,2,1,0:T(8,128)} %bitcast.100), kind=kLoop, calls=%fused_computation.28 | loop fusion | flops 393216 | bytes 1049600 | tf_op jit(solution)/shard_map/convert_element_type | solution.py:95
  34.4 1.9 %collective-permute-start.3 = (bf16[4,2,8,2048]{3,2,0,1:T(8,128)(2,1)}, bf16[4,2,8,2048]{3,2,0,1:T(8,128)(2,1)}, u32[]{:S(2)}, u32[]{:S(2)}) collective-permute-start(bf16[4,2,8,2048]{3,2,0,1:T(8,128)(2,1)} %fusion.14), channel_id=1, source_target_pairs={{0,64},{64,0},{1,65},{65,1},{2,66},{66,2},{3,67},{67,3},{4,68},{68... | collective-permute-start | bytes 786440 | tf_op jit(solution)/shard_map/ppermute | solution.py:95
  36.3 1.9 %collective-permute-start.1 = (bf16[4,2,8,2048]{3,2,0,1:T(8,128)(2,1)S(1)}, bf16[4,2,8,2048]{3,2,0,1:T(8,128)(2,1)}, u32[]{:S(2)}, u32[]{:S(2)}) collective-permute-start(bf16[4,2,8,2048]{3,2,0,1:T(8,128)(2,1)S(1)} %fusion.13), channel_id=1, source_target_pairs={{0,32},{32,0},{1,33},{33,1},{2,34},{34,2},{3,35},{35,3},{4,36},{36... | collective-permute-start | bytes 786440 | tf_op jit(solution)/shard_map/ppermute | solution.py:94
  38.2 6.2 %collective-permute-done.3 = bf16[4,2,8,2048]{3,2,0,1:T(8,128)(2,1)} collective-permute-done((bf16[4,2,8,2048]{3,2,0,1:T(8,128)(2,1)}, bf16[4,2,8,2048]{3,2,0,1:T(8,128)(2,1)}, u32[]{:S(2)}, u32[]{:S(2)}) %collective-permute-start.3) | collective-permute-done | bytes 262176 | tf_op jit(solution)/shard_map/ppermute | solution.py:95
  44.4 1.7 %collective-permute-done.1 = bf16[4,2,8,2048]{3,2,0,1:T(8,128)(2,1)} collective-permute-done((bf16[4,2,8,2048]{3,2,0,1:T(8,128)(2,1)S(1)}, bf16[4,2,8,2048]{3,2,0,1:T(8,128)(2,1)}, u32[]{:S(2)}, u32[]{:S(2)}) %collective-permute-start.1) | collective-permute-done | bytes 262176 | tf_op jit(solution)/shard_map/ppermute | solution.py:94
  47.5 2.2 %collective-permute-start.4 = (bf16[4,8,2048]{2,1,0:T(8,128)(2,1)S(1)}, bf16[4,8,2048]{2,1,0:T(8,128)(2,1)S(1)}, u32[]{:S(2)}, u32[]{:S(2)}) collective-permute-start(bf16[4,8,2048]{2,1,0:T(8,128)(2,1)S(1)} %get-tuple-element.31), channel_id=1, source_target_pairs={{0,32},{32,0},{1,33},{33,1},{2,34},{34,2},{3,35},{35,3},{4,36},{36... | collective-permute-start | bytes 393224 | tf_op jit(solution)/shard_map/ppermute | solution.py:99
  49.7 3.1 %collective-permute-start.2 = (bf16[4,8,2048]{2,1,0:T(8,128)(2,1)S(1)}, bf16[4,8,2048]{2,1,0:T(8,128)(2,1)S(1)}, u32[]{:S(2)}, u32[]{:S(2)}) collective-permute-start(bf16[4,8,2048]{2,1,0:T(8,128)(2,1)S(1)} %get-tuple-element.32), channel_id=1, source_target_pairs={{0,64},{64,0},{1,65},{65,1},{2,66},{66,2},{3,67},{67,3},{4,68},{68... | collective-permute-start | bytes 393224 | tf_op jit(solution)/shard_map/ppermute | solution.py:97
  53.5 2.2 %collective-permute-done.2 = bf16[4,8,2048]{2,1,0:T(8,128)(2,1)S(1)} collective-permute-done((bf16[4,8,2048]{2,1,0:T(8,128)(2,1)S(1)}, bf16[4,8,2048]{2,1,0:T(8,128)(2,1)S(1)}, u32[]{:S(2)}, u32[]{:S(2)}) %collective-permute-start.2) | collective-permute-done | bytes 131104 | tf_op jit(solution)/shard_map/ppermute | solution.py:97
  57.8 10.6 %all-to-all-start.1 = ((bf16[8,8,2048]{2,1,0:T(8,128)(2,1)}), bf16[8,8,2048]{2,1,0:T(8,128)(2,1)S(1)}, u32[]{:S(2)}, u32[]{:S(2)}) async-start(bf16[8,8,2048]{2,1,0:T(8,128)(2,1)} %pad_maximum_fusion.1), calls=%async_computation.1 | async-start | bytes 524288 | tf_op jit(solution)/shard_map/all_to_all | solution.py:107
  69.4 4.4 %collective-permute-start.5 = (f32[32,512]{1,0:T(8,128)S(1)}, f32[32,512]{1,0:T(8,128)S(1)}, u32[]{:S(2)}, u32[]{:S(2)}) collective-permute-start(f32[32,512]{1,0:T(8,128)S(1)} %dynamic-slice_bitcast_fusion), channel_id=1, source_target_pairs={{0,8},{8,0},{1,9},{9,1},{2,10},{10,2},{3,11},{11,3},{4,12},{12,4},... | collective-permute-start | bytes 196616 | tf_op jit(solution)/shard_map/ppermute | solution.py:110
  73.7 2.1 %collective-permute-done.5 = f32[32,512]{1,0:T(8,128)S(1)} collective-permute-done((f32[32,512]{1,0:T(8,128)S(1)}, f32[32,512]{1,0:T(8,128)S(1)}, u32[]{:S(2)}, u32[]{:S(2)}) %collective-permute-start.5) | collective-permute-done | bytes 65568 | tf_op jit(solution)/shard_map/ppermute | solution.py:110
  77.7 8.0 %all-to-all-done.1 = bf16[8,8,2048]{2,1,0:T(8,128)(2,1)S(1)} async-done(((bf16[8,8,2048]{2,1,0:T(8,128)(2,1)}), bf16[8,8,2048]{2,1,0:T(8,128)(2,1)S(1)}, u32[]{:S(2)}, u32[]{:S(2)}) %all-to-all-start.1) | async-done | bytes 262176 | tf_op jit(solution)/shard_map/all_to_all | solution.py:107
  85.7 1.6 %fusion.42 = (bf16[8,2048]{1,0:T(8,128)(2,1)S(1)}, f32[8,2048]{1,0:T(8,128)}, f32[8,2048]{1,0:T(8,128)}, f32[8,2048]{1,0:T(8,128)}) fusion(f32[8,2048]{1,0:T(8,128)} %param.13, f32[8,2048]{1,0:T(8,128)S(1)} %convert_reduce_fusion, f32[8,2048]{1,0:T(8,128)} %param.14, f32[8,2048]{1,0:T(8,128)} %param.15), kind=kLoop, calls=%fused_computation.88 | loop fusion | flops 262144 | bytes 491520 | tf_op jit(solution)/shard_map/convert_element_type | solution.py:121
  88.0 5.6 %all-to-all-start.2 = ((bf16[8,8,2048]{2,1,0:T(8,128)(2,1)}), bf16[8,8,2048]{2,1,0:T(8,128)(2,1)S(1)}, u32[]{:S(2)}, u32[]{:S(2)}) async-start(bf16[8,8,2048]{2,1,0:T(8,128)(2,1)} %broadcast_in_dim.180), calls=%async_computation.2 | async-start | bytes 524288 | tf_op jit(solution)/shard_map/all_to_all | solution.py:32
  93.6 4.3 %collective-permute-start.6 = (bf16[32,512]{1,0:T(8,128)(2,1)S(1)}, bf16[32,512]{1,0:T(8,128)(2,1)S(1)}, u32[]{:S(2)}, u32[]{:S(2)}) collective-permute-start(bf16[32,512]{1,0:T(8,128)(2,1)S(1)} %fusion.35), channel_id=1, source_target_pairs={{0,8},{8,0},{1,9},{9,1},{2,10},{10,2},{3,11},{11,3},{4,12},{12,4},... | collective-permute-start | bytes 98312 | tf_op jit(solution)/shard_map/ppermute | solution.py:24
  98.1 1.6 %collective-permute-done.6 = bf16[32,512]{1,0:T(8,128)(2,1)S(1)} collective-permute-done((bf16[32,512]{1,0:T(8,128)(2,1)S(1)}, bf16[32,512]{1,0:T(8,128)(2,1)S(1)}, u32[]{:S(2)}, u32[]{:S(2)}) %collective-permute-start.6) | collective-permute-done | bytes 32800 | tf_op jit(solution)/shard_map/ppermute | solution.py:24
  99.8 9.8 %all-to-all-done.2 = bf16[8,8,2048]{2,1,0:T(8,128)(2,1)S(1)} async-done(((bf16[8,8,2048]{2,1,0:T(8,128)(2,1)}), bf16[8,8,2048]{2,1,0:T(8,128)(2,1)S(1)}, u32[]{:S(2)}, u32[]{:S(2)}) %all-to-all-start.2) | async-done | bytes 262176 | tf_op jit(solution)/shard_map/all_to_all | solution.py:32
  109.6 2.8 %collective-permute-start.9 = (bf16[4,8,2048]{2,1,0:T(8,128)(2,1)S(1)}, bf16[4,8,2048]{2,1,0:T(8,128)(2,1)S(1)}, u32[]{:S(2)}, u32[]{:S(2)}) collective-permute-start(bf16[4,8,2048]{2,1,0:T(8,128)(2,1)S(1)} %get-tuple-element.34), channel_id=1, source_target_pairs={{0,32},{32,0},{1,33},{33,1},{2,34},{34,2},{3,35},{35,3},{4,36},{36... | collective-permute-start | bytes 393224 | tf_op jit(solution)/shard_map/ppermute | solution.py:24
  112.5 1.9 %collective-permute-start.7 = (bf16[4,8,2048]{2,1,0:T(8,128)(2,1)S(1)}, bf16[4,8,2048]{2,1,0:T(8,128)(2,1)S(1)}, u32[]{:S(2)}, u32[]{:S(2)}) collective-permute-start(bf16[4,8,2048]{2,1,0:T(8,128)(2,1)S(1)} %get-tuple-element.33), channel_id=1, source_target_pairs={{0,64},{64,0},{1,65},{65,1},{2,66},{66,2},{3,67},{67,3},{4,68},{68... | collective-permute-start | bytes 393224 | tf_op jit(solution)/shard_map/ppermute | solution.py:24
  115.3 5.0 %all-to-all-start.3 = ((bf16[8,64,512]{2,1,0:T(8,128)(2,1)}), bf16[8,64,512]{2,1,0:T(8,128)(2,1)}, u32[]{:S(2)}, u32[]{:S(2)}) async-start(bf16[8,64,512]{2,1,0:T(8,128)(2,1)} %broadcast_in_dim.188), calls=%async_computation.3 | async-start | bytes 1048576 | tf_op jit(solution)/shard_map/all_to_all | solution.py:32
  120.4 2.6 %collective-permute-start.10 = (bf16[4,2,8,2048]{3,2,1,0:T(8,128)(2,1)S(1)}, bf16[4,2,8,2048]{3,2,1,0:T(8,128)(2,1)S(1)}, u32[]{:S(2)}, u32[]{:S(2)}) collective-permute-start(bf16[4,2,8,2048]{3,2,1,0:T(8,128)(2,1)S(1)} %broadcast_select_fusion.2), channel_id=1, source_target_pairs={{0,64},{64,0},{1,65},{65,1},{2,66},{66,2},{3,67},{67,3},{4,68},{68... | collective-permute-start | bytes 786440 | tf_op jit(solution)/shard_map/ppermute | solution.py:24
  123.1 3.4 %collective-permute-start.8 = (bf16[4,2,8,2048]{3,2,1,0:T(8,128)(2,1)S(1)}, bf16[4,2,8,2048]{3,2,1,0:T(8,128)(2,1)S(1)}, u32[]{:S(2)}, u32[]{:S(2)}) collective-permute-start(bf16[4,2,8,2048]{3,2,1,0:T(8,128)(2,1)S(1)} %broadcast_select_fusion.3), channel_id=1, source_target_pairs={{0,32},{32,0},{1,33},{33,1},{2,34},{34,2},{3,35},{35,3},{4,36},{36... | collective-permute-start | bytes 786440 | tf_op jit(solution)/shard_map/ppermute | solution.py:24
  127.6 2.6 %collective-permute-done.8 = bf16[4,2,8,2048]{3,2,1,0:T(8,128)(2,1)S(1)} collective-permute-done((bf16[4,2,8,2048]{3,2,1,0:T(8,128)(2,1)S(1)}, bf16[4,2,8,2048]{3,2,1,0:T(8,128)(2,1)S(1)}, u32[]{:S(2)}, u32[]{:S(2)}) %collective-permute-start.8) | collective-permute-done | bytes 262176 | tf_op jit(solution)/shard_map/ppermute | solution.py:24
  130.4 11.5 %collective-permute-start.11 = (bf16[8,2,2,8,2048]{4,3,2,1,0:T(8,128)(2,1)S(1)}, bf16[8,2,2,8,2048]{4,3,2,1,0:T(8,128)(2,1)}, u32[]{:S(2)}, u32[]{:S(2)}) collective-permute-start(bf16[8,2,2,8,2048]{4,3,2,1,0:T(8,128)(2,1)S(1)} %pad_maximum_fusion), channel_id=1, source_target_pairs={{0,16},{16,0},{1,17},{17,1},{2,18},{18,2},{3,19},{19,3},{4,20},{20... | collective-permute-start | bytes 3145736 | tf_op jit(solution)/shard_map/ppermute | solution.py:24
  142.2 2.4 %convolution_convert_fusion.2 = bf16[512,448]{0,1:T(8,128)(2,1)} fusion(bf16[512,512]{1,0:T(8,128)(2,1)} %bitcast.18, bf16[448,512]{1,0:T(8,128)(2,1)} %param.11), kind=kOutput, calls=%fused_computation.5 | convolution fusion | flops 235110400 | bytes 1441792 | tf_op jit(solution)/shard_map/dot_general | solution.py:129
  144.6 2.8 %bitcast_select_fusion = bf16[512,2048]{1,0:T(8,128)(2,1)} fusion(pred[512]{0:T(512)(128)(4,1)S(1)} %broadcast_in_dim.190, bf16[8,2,2,8,2048]{4,3,2,1,0:T(8,128)(2,1)} %collective-permute-done.11, bf16[8,2,2,8,2048]{4,3,2,1,0:T(8,128)(2,1)S(1)} %pad_maximum_fusion), kind=kLoop, calls=%fused_computation.1 | loop fusion | flops 1048576 | bytes 4194816 | tf_op jit(solution)/shard_map/jit(_where)/select_n | solution.py:27
  (51 shorter events, 14.1 us)
Async XLA Ops:
  0.6 4.2 %copy-start = (bf16[512,2048]{1,0:T(8,128)(2,1)S(1)}, bf16[512,2048]{1,0:T(8,128)(2,1)}, u32[]{:S(2)}) copy-start(bf16[512,2048]{1,0:T(8,128)(2,1)} %param.12) | copy-start | bytes 6291460
  4.0 0.8 copy-start.1
  4.8 17.7 %copy-start.3 = (bf16[512,2048]{1,0:T(8,128)(2,1)S(1)}, bf16[512,2048]{1,0:T(8,128)(2,1)}, u32[]{:S(2)}) copy-start(bf16[512,2048]{1,0:T(8,128)(2,1)} %param.10) | copy-start | bytes 6291460
  6.5 24.9 %collective-permute-start = (bf16[256,2048]{1,0:T(8,128)(2,1)}, bf16[256,2048]{1,0:T(8,128)(2,1)}, u32[]{:S(2)}, u32[]{:S(2)}) collective-permute-start(bf16[256,2048]{1,0:T(8,128)(2,1)} %convolution_convert_fusion), channel_id=1, source_target_pairs={{0,16},{16,0},{1,17},{17,1},{2,18},{18,2},{3,19},{19,3},{4,20},{20... | collective-permute-start | bytes 3145736 | tf_op jit(solution)/shard_map/ppermute | solution.py:72
  24.8 33.0 %all-to-all-start = ((f32[8,64,512]{2,1,0:T(8,128)}), f32[8,64,512]{2,1,0:T(8,128)S(1)}, u32[]{:S(2)}, u32[]{:S(2)}) async-start(f32[8,64,512]{2,1,0:T(8,128)} %bitcast.103), calls=%async_computation | async-start | bytes 2097152 | tf_op jit(solution)/shard_map/all_to_all | solution.py:79
  34.4 10.0 %collective-permute-start.3 = (bf16[4,2,8,2048]{3,2,0,1:T(8,128)(2,1)}, bf16[4,2,8,2048]{3,2,0,1:T(8,128)(2,1)}, u32[]{:S(2)}, u32[]{:S(2)}) collective-permute-start(bf16[4,2,8,2048]{3,2,0,1:T(8,128)(2,1)} %fusion.14), channel_id=1, source_target_pairs={{0,64},{64,0},{1,65},{65,1},{2,66},{66,2},{3,67},{67,3},{4,68},{68... | collective-permute-start | bytes 786440 | tf_op jit(solution)/shard_map/ppermute | solution.py:95
  36.3 9.8 %collective-permute-start.1 = (bf16[4,2,8,2048]{3,2,0,1:T(8,128)(2,1)S(1)}, bf16[4,2,8,2048]{3,2,0,1:T(8,128)(2,1)}, u32[]{:S(2)}, u32[]{:S(2)}) collective-permute-start(bf16[4,2,8,2048]{3,2,0,1:T(8,128)(2,1)S(1)} %fusion.13), channel_id=1, source_target_pairs={{0,32},{32,0},{1,33},{33,1},{2,34},{34,2},{3,35},{35,3},{4,36},{36... | collective-permute-start | bytes 786440 | tf_op jit(solution)/shard_map/ppermute | solution.py:94
  47.4 28.4 %copy-start.2 = (f32[512]{0:T(512)S(1)}, f32[512]{0:T(512)}, u32[]{:S(2)}) copy-start(f32[512]{0:T(512)} %param.9) | copy-start | bytes 6148
  47.5 6.1 %collective-permute-start.4 = (bf16[4,8,2048]{2,1,0:T(8,128)(2,1)S(1)}, bf16[4,8,2048]{2,1,0:T(8,128)(2,1)S(1)}, u32[]{:S(2)}, u32[]{:S(2)}) collective-permute-start(bf16[4,8,2048]{2,1,0:T(8,128)(2,1)S(1)} %get-tuple-element.31), channel_id=1, source_target_pairs={{0,32},{32,0},{1,33},{33,1},{2,34},{34,2},{3,35},{35,3},{4,36},{36... | collective-permute-start | bytes 393224 | tf_op jit(solution)/shard_map/ppermute | solution.py:99
  49.7 6.1 %collective-permute-start.2 = (bf16[4,8,2048]{2,1,0:T(8,128)(2,1)S(1)}, bf16[4,8,2048]{2,1,0:T(8,128)(2,1)S(1)}, u32[]{:S(2)}, u32[]{:S(2)}) collective-permute-start(bf16[4,8,2048]{2,1,0:T(8,128)(2,1)S(1)} %get-tuple-element.32), channel_id=1, source_target_pairs={{0,64},{64,0},{1,65},{65,1},{2,66},{66,2},{3,67},{67,3},{4,68},{68... | collective-permute-start | bytes 393224 | tf_op jit(solution)/shard_map/ppermute | solution.py:97
  57.8 27.9 %all-to-all-start.1 = ((bf16[8,8,2048]{2,1,0:T(8,128)(2,1)}), bf16[8,8,2048]{2,1,0:T(8,128)(2,1)S(1)}, u32[]{:S(2)}, u32[]{:S(2)}) async-start(bf16[8,8,2048]{2,1,0:T(8,128)(2,1)} %pad_maximum_fusion.1), calls=%async_computation.1 | async-start | bytes 524288 | tf_op jit(solution)/shard_map/all_to_all | solution.py:107
  69.4 6.5 %collective-permute-start.5 = (f32[32,512]{1,0:T(8,128)S(1)}, f32[32,512]{1,0:T(8,128)S(1)}, u32[]{:S(2)}, u32[]{:S(2)}) collective-permute-start(f32[32,512]{1,0:T(8,128)S(1)} %dynamic-slice_bitcast_fusion), channel_id=1, source_target_pairs={{0,8},{8,0},{1,9},{9,1},{2,10},{10,2},{3,11},{11,3},{4,12},{12,4},... | collective-permute-start | bytes 196616 | tf_op jit(solution)/shard_map/ppermute | solution.py:110
  88.0 21.6 %all-to-all-start.2 = ((bf16[8,8,2048]{2,1,0:T(8,128)(2,1)}), bf16[8,8,2048]{2,1,0:T(8,128)(2,1)S(1)}, u32[]{:S(2)}, u32[]{:S(2)}) async-start(bf16[8,8,2048]{2,1,0:T(8,128)(2,1)} %broadcast_in_dim.180), calls=%async_computation.2 | async-start | bytes 524288 | tf_op jit(solution)/shard_map/all_to_all | solution.py:32
  93.6 6.2 %collective-permute-start.6 = (bf16[32,512]{1,0:T(8,128)(2,1)S(1)}, bf16[32,512]{1,0:T(8,128)(2,1)S(1)}, u32[]{:S(2)}, u32[]{:S(2)}) collective-permute-start(bf16[32,512]{1,0:T(8,128)(2,1)S(1)} %fusion.35), channel_id=1, source_target_pairs={{0,8},{8,0},{1,9},{9,1},{2,10},{10,2},{3,11},{11,3},{4,12},{12,4},... | collective-permute-start | bytes 98312 | tf_op jit(solution)/shard_map/ppermute | solution.py:24
  109.6 10.7 %collective-permute-start.9 = (bf16[4,8,2048]{2,1,0:T(8,128)(2,1)S(1)}, bf16[4,8,2048]{2,1,0:T(8,128)(2,1)S(1)}, u32[]{:S(2)}, u32[]{:S(2)}) collective-permute-start(bf16[4,8,2048]{2,1,0:T(8,128)(2,1)S(1)} %get-tuple-element.34), channel_id=1, source_target_pairs={{0,32},{32,0},{1,33},{33,1},{2,34},{34,2},{3,35},{35,3},{4,36},{36... | collective-permute-start | bytes 393224 | tf_op jit(solution)/shard_map/ppermute | solution.py:24
  112.5 10.5 %collective-permute-start.7 = (bf16[4,8,2048]{2,1,0:T(8,128)(2,1)S(1)}, bf16[4,8,2048]{2,1,0:T(8,128)(2,1)S(1)}, u32[]{:S(2)}, u32[]{:S(2)}) collective-permute-start(bf16[4,8,2048]{2,1,0:T(8,128)(2,1)S(1)} %get-tuple-element.33), channel_id=1, source_target_pairs={{0,64},{64,0},{1,65},{65,1},{2,66},{66,2},{3,67},{67,3},{4,68},{68... | collective-permute-start | bytes 393224 | tf_op jit(solution)/shard_map/ppermute | solution.py:24
  115.3 26.9 %all-to-all-start.3 = ((bf16[8,64,512]{2,1,0:T(8,128)(2,1)}), bf16[8,64,512]{2,1,0:T(8,128)(2,1)}, u32[]{:S(2)}, u32[]{:S(2)}) async-start(bf16[8,64,512]{2,1,0:T(8,128)(2,1)} %broadcast_in_dim.188), calls=%async_computation.3 | async-start | bytes 1048576 | tf_op jit(solution)/shard_map/all_to_all | solution.py:32
  120.4 7.1 %collective-permute-start.10 = (bf16[4,2,8,2048]{3,2,1,0:T(8,128)(2,1)S(1)}, bf16[4,2,8,2048]{3,2,1,0:T(8,128)(2,1)S(1)}, u32[]{:S(2)}, u32[]{:S(2)}) collective-permute-start(bf16[4,2,8,2048]{3,2,1,0:T(8,128)(2,1)S(1)} %broadcast_select_fusion.2), channel_id=1, source_target_pairs={{0,64},{64,0},{1,65},{65,1},{2,66},{66,2},{3,67},{67,3},{4,68},{68... | collective-permute-start | bytes 786440 | tf_op jit(solution)/shard_map/ppermute | solution.py:24
  123.1 7.1 %collective-permute-start.8 = (bf16[4,2,8,2048]{3,2,1,0:T(8,128)(2,1)S(1)}, bf16[4,2,8,2048]{3,2,1,0:T(8,128)(2,1)S(1)}, u32[]{:S(2)}, u32[]{:S(2)}) collective-permute-start(bf16[4,2,8,2048]{3,2,1,0:T(8,128)(2,1)S(1)} %broadcast_select_fusion.3), channel_id=1, source_target_pairs={{0,32},{32,0},{1,33},{33,1},{2,34},{34,2},{3,35},{35,3},{4,36},{36... | collective-permute-start | bytes 786440 | tf_op jit(solution)/shard_map/ppermute | solution.py:24
  130.4 14.1 %collective-permute-start.11 = (bf16[8,2,2,8,2048]{4,3,2,1,0:T(8,128)(2,1)S(1)}, bf16[8,2,2,8,2048]{4,3,2,1,0:T(8,128)(2,1)}, u32[]{:S(2)}, u32[]{:S(2)}) collective-permute-start(bf16[8,2,2,8,2048]{4,3,2,1,0:T(8,128)(2,1)S(1)} %pad_maximum_fusion), channel_id=1, source_target_pairs={{0,16},{16,0},{1,17},{17,1},{2,18},{18,2},{3,19},{19,3},{4,20},{20... | collective-permute-start | bytes 3145736 | tf_op jit(solution)/shard_map/ppermute | solution.py:24

commit v5 on v4

--- a/solution.py
+++ b/solution.py
@@ -23,7 +23,8 @@
 def gather_pair(x, axis, dim):
     got = jnp.expand_dims(lax.ppermute(x, axis, SWAP), dim)
     x = jnp.expand_dims(x, dim)
-    place = lax.broadcasted_iota(jnp.int32, tuple(2 if d == dim else 1 for d in range(x.ndim)), dim)
+    shape = tuple(2 if d == dim else n for d, n in enumerate(x.shape))
+    place = lax.broadcasted_iota(jnp.int32, shape, dim)
     return jnp.where(place == lax.axis_index(axis), x, got)
 
 
@@ -54,21 +55,19 @@
     half = zh // 2
     rows = latents // (zh * zl * xl * c)
 
-    def rows_of(core):
+    def picked_rows(core):
         place = lax.broadcasted_iota(jnp.int32, (latents // c, latents), 0)
         latent = lax.broadcasted_iota(jnp.int32, (latents // c, latents), 1)
-        return latent == (place // rows * c + core) * rows + place % rows
-
-    picks = jnp.concatenate([rows_of(1 - my_c), rows_of(my_c)]).astype(BF16)
-    picked = lax.dot_general(
-        picks, normalized, (((1,), (1,)), ((), ())), preferred_element_type=F32
-    ).astype(BF16)
-    picked = lax.optimization_barrier(picked)
+        picks = latent == (place // rows * c + core) * rows + place % rows
+        picked = lax.dot_general(
+            picks.astype(BF16), normalized, (((1,), (1,)), ((), ())), preferred_element_type=F32
+        )
+        return lax.optimization_barrier(picked.astype(BF16))
 
     def product(lhs, rhs):
         return lax.dot_general(lhs, rhs, (((1,), (0,)), ((), ())), preferred_element_type=F32)
 
-    send = product(picked[: latents // c], grad_kv).astype(BF16)
+    send = product(picked_rows(1 - my_c), grad_kv).astype(BF16)
     got = lax.ppermute(send, "c", SWAP)
     grad_kv, _ = lax.optimization_barrier((grad_kv, send))
     grad_part = lax.dot_general(
@@ -79,8 +78,8 @@
     blocks = lax.all_to_all(
         grad_part.reshape(-1, pair, grad_part.shape[1]), "y", 0, 0, tiled=True
     )
-    grad_kv, _ = lax.optimization_barrier((grad_kv, grad_part))
-    own = product(picked[latents // c :], grad_kv)
+    grad_kv, my_c, _ = lax.optimization_barrier((grad_kv, my_c, grad_part))
+    own = product(picked_rows(my_c), grad_kv)
 
     def piece(x, start, z=None, x_lo=None):
         starts = (start, 0 if z is None else z, 0 if x_lo is None else x_lo, 0, 0)
@@ -91,16 +90,20 @@
     def pair_sum(start, z=None, x_lo=None):
         return piece(own, start, z, x_lo) + piece(got, start, z, x_lo)
 
-    p_got = lax.ppermute(pair_sum(0, None, 1 - my_xl).astype(BF16), "xl", SWAP)
-    q_got = lax.ppermute(pair_sum(half, 1 - my_zl, None).astype(BF16), "zl", SWAP)
+    p_send = pair_sum(0, None, 1 - my_xl).astype(BF16)
+    p_got = lax.ppermute(p_send, "xl", SWAP)
+    q_send = pair_sum(half, 1 - my_zl, None).astype(BF16)
+    q_got = lax.ppermute(q_send, "zl", SWAP)
     p_send = (pair_sum(0, 1 - my_zl, my_xl) + at(p_got, 1 - my_zl, 1).astype(F32)).astype(BF16)
     p_last = lax.ppermute(p_send, "zl", SWAP)
+    q_got, _ = lax.optimization_barrier((q_got, p_send))
     q_send = (pair_sum(half, my_zl, 1 - my_xl) + at(q_got, 1 - my_xl, 1).astype(F32)).astype(BF16)
     q_last = lax.ppermute(q_send, "xl", SWAP)
-    p_last, q_last = lax.optimization_barrier((p_last, q_last))
+    p_last, _ = lax.optimization_barrier((p_last, q_send))
     p = pair_sum(0, my_zl, my_xl) + at(p_got, my_zl, 1).astype(F32) + p_last.astype(F32)
+    p = p.astype(BF16)
+    q_last, _ = lax.optimization_barrier((q_last, p))
     q = pair_sum(half, my_zl, my_xl) + at(q_got, my_xl, 1).astype(F32) + q_last.astype(F32)
-    p = p.astype(BF16)
     q = q.astype(BF16)
     both = jnp.concatenate([p, q])
     both, blocks = lax.optimization_barrier((both, blocks))

time: 149 us -> 145 us (0.973)
  the two profiles are of different devices: /device:TPU:1 before, /device:TPU:6 now
where the time goes in v5:
time: 145 us; the launch traced here: 142 us
  starting transfers between devices  70.3 us (48%)
  waiting for transfers between devices  41.6 us (29%)
  other arithmetic  17.2 us (12%)
  matrix products  10.2 us (7%)
  local copies, waits for them, and re-layouts  1.95 us (1%)
    all_to_all x1, starting transfers between devices, local(): both = lax.all_to_all(both, 'zh', 0, 0, tiled=True)  18.2 us
    ppermute x6, starting transfers between devices, gather_pair(): got = jnp.expand_dims(lax.ppermute(x, axis, SWAP), dim)  16.9 us
    all_to_all x2, waiting for transfers between devices, to_all(): lax.all_to_all(jnp.broadcast_to(x[None], (n, *x.shape)), axis, 0, 0, tile...  12.3 us
    ppermute x6, waiting for transfers between devices, gather_pair(): got = jnp.expand_dims(lax.ppermute(x, axis, SWAP), dim)  10.1 us
    all_to_all x1, waiting for transfers between devices, local(): both = lax.all_to_all(both, 'zh', 0, 0, tiled=True)  9.26 us
    all_to_all x2, starting transfers between devices, to_all(): lax.all_to_all(jnp.broadcast_to(x[None], (n, *x.shape)), axis, 0, 0, tile...  8.79 us
    all_to_all x1, starting transfers between devices, local(): lax.all_to_all(grad_part.reshape(-1, pair, grad_part.shape[1]), 'y', 0, 0...  7.23 us
    ppermute x1, waiting for transfers between devices, local(): lax.ppermute(at(grad_pair, 1 - my_xh, 0), 'xh', SWAP)  4.33 us
  transfers between devices with their start and end apart: 16, of which 10 were waited for; matrix products, arithmetic and copies ran while one was open for 14% of the time, Pallas kernels for 0%

profile of v5, /device:TPU:6, one launch (start us, length us, event | category | flops | bytes accessed | tf_op | source)
XLA Modules:
  0.0 142.3 jit_solution(6712453035558053273)
XLA Ops:
  2.1 1.6 %convolution_convert_fusion.3 = bf16[256,512]{1,0:T(8,128)(2,1)S(1)} fusion(s32[256]{0:T(256)S(1)} %get-tuple-element.38, s32[256]{0:T(256)S(1)} %get-tuple-element.39, s32[]{:T(128)S(6)} %sub.34, s32[256]{0:T(256)S(1)} %get-tuple-element.37, s32[256]{0:T(256)S(1)} %get-tuple-element.40, pred[256]{0:T(512)(128)(4,1)S(1)} %get-tuple-element.35, ...), kind=kOutput, calls=%fused_computation.6 | convolution fusion | flops 136314880 | bytes 795140 | tf_op jit(solution)/shard_map/dot_general | solution.py:62
  3.7 1.7 %convolution_convert_fusion = bf16[256,2048]{1,0:T(8,128)(2,1)} fusion(bf16[256,512]{1,0:T(8,128)(2,1)S(1)} %convolution_convert_fusion.3, bf16[512,2048]{1,0:T(8,128)(2,1)S(1)} %copy-done), kind=kOutput, calls=%fused_computation | convolution fusion | flops 537395200 | bytes 3407872 | tf_op jit(solution)/shard_map/dot_general | solution.py:68
  5.4 1.9 %collective-permute-start = (bf16[256,2048]{1,0:T(8,128)(2,1)}, bf16[256,2048]{1,0:T(8,128)(2,1)}, u32[]{:S(2)}, u32[]{:S(2)}) collective-permute-start(bf16[256,2048]{1,0:T(8,128)(2,1)} %convolution_convert_fusion), channel_id=1, source_target_pairs={{0,16},{16,0},{1,17},{17,1},{2,18},{18,2},{3,19},{19,3},{4,20},{20... | collective-permute-start | bytes 3145736 | tf_op jit(solution)/shard_map/ppermute | solution.py:71
  7.3 2.3 %fusion.61 = f32[512,512]{1,0:T(8,128)} fusion(bf16[512,2048]{1,0:T(8,128)(2,1)S(1)} %copy-done, bf16[512,2048]{1,0:T(8,128)(2,1)S(1)} %copy-done.3), kind=kOutput, calls=%fused_computation.104 | convolution fusion | flops 1073741824 | bytes 5242880 | tf_op jit(solution)/shard_map/dot_general | solution.py:73
  9.6 7.2 %all-to-all-start = ((f32[8,64,512]{2,1,0:T(8,128)}), f32[8,64,512]{2,1,0:T(8,128)S(1)}, u32[]{:S(2)}, u32[]{:S(2)}) async-start(f32[8,64,512]{2,1,0:T(8,128)} %bitcast.107), calls=%async_computation | async-start | bytes 2097152 | tf_op jit(solution)/shard_map/all_to_all | solution.py:78
  16.8 1.6 %convolution_convert_fusion.2 = bf16[256,512]{1,0:T(8,128)(2,1)S(1)} fusion(s32[]{:T(128)S(6)} %axis_index.33, s32[256]{0:T(256)S(1)} %get-tuple-element.38, s32[256]{0:T(256)S(1)} %get-tuple-element.39, s32[256]{0:T(256)S(1)} %get-tuple-element.37, s32[256]{0:T(256)S(1)} %get-tuple-element.40, pred[256]{0:T(512)(128)(4,1)S(1)} %get-tuple-element.35, ...), kind=kOutput, calls=%fused_computation.5 | convolution fusion | flops 136314880 | bytes 795140 | tf_op jit(solution)/shard_map/dot_general | solution.py:62
  19.2 1.9 %fusion.9 = bf16[4,2,8,2048]{3,2,0,1:T(8,128)(2,1)} fusion(bf16[8,2,2,8,2048]{4,3,2,1,0:T(8,128)(2,1)} %bitcast.1, s32[]{:T(128)S(6)} %select_n.99, f32[8,2,2,8,2048]{4,3,2,1,0:T(8,128)S(1)} %bitcast.101), kind=kLoop, calls=%fused_computation.23 | loop fusion | flops 393216 | bytes 1049600 | tf_op jit(solution)/shard_map/convert_element_type | solution.py:93
  21.1 2.7 %collective-permute-start.1 = (bf16[4,2,8,2048]{3,2,0,1:T(8,128)(2,1)}, bf16[4,2,8,2048]{3,2,0,1:T(8,128)(2,1)}, u32[]{:S(2)}, u32[]{:S(2)}) collective-permute-start(bf16[4,2,8,2048]{3,2,0,1:T(8,128)(2,1)} %fusion.9), channel_id=1, source_target_pairs={{0,32},{32,0},{1,33},{33,1},{2,34},{34,2},{3,35},{35,3},{4,36},{36... | collective-permute-start | bytes 786440 | tf_op jit(solution)/shard_map/ppermute | solution.py:94
  24.8 4.3 %collective-permute-start.3 = (bf16[4,2,8,2048]{3,2,0,1:T(8,128)(2,1)S(1)}, bf16[4,2,8,2048]{3,2,0,1:T(8,128)(2,1)}, u32[]{:S(2)}, u32[]{:S(2)}) collective-permute-start(bf16[4,2,8,2048]{3,2,0,1:T(8,128)(2,1)S(1)} %fusion.10), channel_id=1, source_target_pairs={{0,64},{64,0},{1,65},{65,1},{2,66},{66,2},{3,67},{67,3},{4,68},{68... | collective-permute-start | bytes 786440 | tf_op jit(solution)/shard_map/ppermute | solution.py:96
  29.1 2.6 %collective-permute-done.1 = bf16[4,2,8,2048]{3,2,0,1:T(8,128)(2,1)} collective-permute-done((bf16[4,2,8,2048]{3,2,0,1:T(8,128)(2,1)}, bf16[4,2,8,2048]{3,2,0,1:T(8,128)(2,1)}, u32[]{:S(2)}, u32[]{:S(2)}) %collective-permute-start.1) | collective-permute-done | bytes 262176 | tf_op jit(solution)/shard_map/ppermute | solution.py:94
  32.8 4.3 %collective-permute-start.2 = (bf16[4,8,2048]{2,1,0:T(8,128)(2,1)S(1)}, bf16[4,8,2048]{2,1,0:T(8,128)(2,1)S(1)}, u32[]{:S(2)}, u32[]{:S(2)}) collective-permute-start(bf16[4,8,2048]{2,1,0:T(8,128)(2,1)S(1)} %fusion.16), channel_id=1, source_target_pairs={{0,64},{64,0},{1,65},{65,1},{2,66},{66,2},{3,67},{67,3},{4,68},{68... | collective-permute-start | bytes 393224 | tf_op jit(solution)/shard_map/ppermute | solution.py:98
  38.2 2.7 %collective-permute-start.4 = (bf16[4,8,2048]{2,1,0:T(8,128)(2,1)S(1)}, bf16[4,8,2048]{2,1,0:T(8,128)(2,1)S(1)}, u32[]{:S(2)}, u32[]{:S(2)}) collective-permute-start(bf16[4,8,2048]{2,1,0:T(8,128)(2,1)S(1)} %fusion.13), channel_id=1, source_target_pairs={{0,32},{32,0},{1,33},{33,1},{2,34},{34,2},{3,35},{35,3},{4,36},{36... | collective-permute-start | bytes 393224 | tf_op jit(solution)/shard_map/ppermute | solution.py:101
  42.1 3.0 %collective-permute-done.4 = bf16[4,8,2048]{2,1,0:T(8,128)(2,1)S(1)} collective-permute-done((bf16[4,8,2048]{2,1,0:T(8,128)(2,1)S(1)}, bf16[4,8,2048]{2,1,0:T(8,128)(2,1)S(1)}, u32[]{:S(2)}, u32[]{:S(2)}) %collective-permute-start.4) | collective-permute-done | bytes 131104 | tf_op jit(solution)/shard_map/ppermute | solution.py:101
  46.9 18.2 %all-to-all-start.1 = ((bf16[8,8,2048]{2,1,0:T(8,128)(2,1)}), bf16[8,8,2048]{2,1,0:T(8,128)(2,1)S(1)}, u32[]{:S(2)}, u32[]{:S(2)}) async-start(bf16[8,8,2048]{2,1,0:T(8,128)(2,1)} %pad_maximum_fusion.1), calls=%async_computation.1 | async-start | bytes 524288 | tf_op jit(solution)/shard_map/all_to_all | solution.py:110
  66.0 3.3 %collective-permute-start.5 = (f32[32,512]{1,0:T(8,128)S(1)}, f32[32,512]{1,0:T(8,128)S(1)}, u32[]{:S(2)}, u32[]{:S(2)}) collective-permute-start(f32[32,512]{1,0:T(8,128)S(1)} %dynamic-slice_bitcast_fusion), channel_id=1, source_target_pairs={{0,8},{8,0},{1,9},{9,1},{2,10},{10,2},{3,11},{11,3},{4,12},{12,4},... | collective-permute-start | bytes 196616 | tf_op jit(solution)/shard_map/ppermute | solution.py:113
  69.4 4.3 %collective-permute-done.5 = f32[32,512]{1,0:T(8,128)S(1)} collective-permute-done((f32[32,512]{1,0:T(8,128)S(1)}, f32[32,512]{1,0:T(8,128)S(1)}, u32[]{:S(2)}, u32[]{:S(2)}) %collective-permute-start.5) | collective-permute-done | bytes 65568 | tf_op jit(solution)/shard_map/ppermute | solution.py:113
  75.5 9.3 %all-to-all-done.1 = bf16[8,8,2048]{2,1,0:T(8,128)(2,1)S(1)} async-done(((bf16[8,8,2048]{2,1,0:T(8,128)(2,1)}), bf16[8,8,2048]{2,1,0:T(8,128)(2,1)S(1)}, u32[]{:S(2)}, u32[]{:S(2)}) %all-to-all-start.1) | async-done | bytes 262176 | tf_op jit(solution)/shard_map/all_to_all | solution.py:110
  84.8 1.6 %fusion.58 = (bf16[8,2048]{1,0:T(8,128)(2,1)S(1)}, f32[8,2048]{1,0:T(8,128)}, f32[8,2048]{1,0:T(8,128)}, f32[8,2048]{1,0:T(8,128)}) fusion(f32[8,2048]{1,0:T(8,128)} %param.13, f32[8,2048]{1,0:T(8,128)S(1)} %convert_reduce_fusion, f32[8,2048]{1,0:T(8,128)} %param.14, f32[8,2048]{1,0:T(8,128)} %param.15), kind=kLoop, calls=%fused_computation.102 | loop fusion | flops 262144 | bytes 491520 | tf_op jit(solution)/shard_map/convert_element_type | solution.py:124
  87.1 4.6 %all-to-all-start.2 = ((bf16[8,8,2048]{2,1,0:T(8,128)(2,1)}), bf16[8,8,2048]{2,1,0:T(8,128)(2,1)S(1)}, u32[]{:S(2)}, u32[]{:S(2)}) async-start(bf16[8,8,2048]{2,1,0:T(8,128)(2,1)} %broadcast_in_dim.127), calls=%async_computation.2 | async-start | bytes 524288 | tf_op jit(solution)/shard_map/all_to_all | solution.py:33
  91.8 3.3 %collective-permute-start.6 = (bf16[32,512]{1,0:T(8,128)(2,1)S(1)}, bf16[32,512]{1,0:T(8,128)(2,1)S(1)}, u32[]{:S(2)}, u32[]{:S(2)}) collective-permute-start(bf16[32,512]{1,0:T(8,128)(2,1)S(1)} %fusion.48), channel_id=1, source_target_pairs={{0,8},{8,0},{1,9},{9,1},{2,10},{10,2},{3,11},{11,3},{4,12},{12,4},... | collective-permute-start | bytes 98312 | tf_op jit(solution)/shard_map/ppermute | solution.py:24
  95.2 3.8 %collective-permute-done.6 = bf16[32,512]{1,0:T(8,128)(2,1)S(1)} collective-permute-done((bf16[32,512]{1,0:T(8,128)(2,1)S(1)}, bf16[32,512]{1,0:T(8,128)(2,1)S(1)}, u32[]{:S(2)}, u32[]{:S(2)}) %collective-permute-start.6) | collective-permute-done | bytes 32800 | tf_op jit(solution)/shard_map/ppermute | solution.py:24
  99.1 12.3 %all-to-all-done.2 = bf16[8,8,2048]{2,1,0:T(8,128)(2,1)S(1)} async-done(((bf16[8,8,2048]{2,1,0:T(8,128)(2,1)}), bf16[8,8,2048]{2,1,0:T(8,128)(2,1)S(1)}, u32[]{:S(2)}, u32[]{:S(2)}) %all-to-all-start.2) | async-done | bytes 262176 | tf_op jit(solution)/shard_map/all_to_all | solution.py:33
  111.4 3.9 %collective-permute-start.7 = (bf16[4,8,2048]{2,1,0:T(8,128)(2,1)S(1)}, bf16[4,8,2048]{2,1,0:T(8,128)(2,1)S(1)}, u32[]{:S(2)}, u32[]{:S(2)}) collective-permute-start(bf16[4,8,2048]{2,1,0:T(8,128)(2,1)S(1)} %get-tuple-element.33), channel_id=1, source_target_pairs={{0,64},{64,0},{1,65},{65,1},{2,66},{66,2},{3,67},{67,3},{4,68},{68... | collective-permute-start | bytes 393224 | tf_op jit(solution)/shard_map/ppermute | solution.py:24
  115.3 2.7 %collective-permute-start.9 = (bf16[4,8,2048]{2,1,0:T(8,128)(2,1)S(1)}, bf16[4,8,2048]{2,1,0:T(8,128)(2,1)S(1)}, u32[]{:S(2)}, u32[]{:S(2)}) collective-permute-start(bf16[4,8,2048]{2,1,0:T(8,128)(2,1)S(1)} %get-tuple-element.34), channel_id=1, source_target_pairs={{0,32},{32,0},{1,33},{33,1},{2,34},{34,2},{3,35},{35,3},{4,36},{36... | collective-permute-start | bytes 393224 | tf_op jit(solution)/shard_map/ppermute | solution.py:24
  118.9 4.1 %all-to-all-start.3 = ((bf16[8,64,512]{2,1,0:T(8,128)(2,1)}), bf16[8,64,512]{2,1,0:T(8,128)(2,1)}, u32[]{:S(2)}, u32[]{:S(2)}) async-start(bf16[8,64,512]{2,1,0:T(8,128)(2,1)} %broadcast_in_dim.132), calls=%async_computation.3 | async-start | bytes 1048576 | tf_op jit(solution)/shard_map/all_to_all | solution.py:33
  123.2 3.1 %collective-permute-start.8 = (bf16[4,2,8,2048]{3,2,1,0:T(8,128)(2,1)S(1)}, bf16[4,2,8,2048]{3,2,1,0:T(8,128)(2,1)S(1)}, u32[]{:S(2)}, u32[]{:S(2)}) collective-permute-start(bf16[4,2,8,2048]{3,2,1,0:T(8,128)(2,1)S(1)} %broadcast_select_fusion.3), channel_id=1, source_target_pairs={{0,32},{32,0},{1,33},{33,1},{2,34},{34,2},{3,35},{35,3},{4,36},{36... | collective-permute-start | bytes 786440 | tf_op jit(solution)/shard_map/ppermute | solution.py:24
  126.4 2.0 %collective-permute-start.10 = (bf16[4,2,8,2048]{3,2,1,0:T(8,128)(2,1)S(1)}, bf16[4,2,8,2048]{3,2,1,0:T(8,128)(2,1)S(1)}, u32[]{:S(2)}, u32[]{:S(2)}) collective-permute-start(bf16[4,2,8,2048]{3,2,1,0:T(8,128)(2,1)S(1)} %broadcast_select_fusion.2), channel_id=1, source_target_pairs={{0,64},{64,0},{1,65},{65,1},{2,66},{66,2},{3,67},{67,3},{4,68},{68... | collective-permute-start | bytes 786440 | tf_op jit(solution)/shard_map/ppermute | solution.py:24
  128.4 3.1 %collective-permute-done.8 = bf16[4,2,8,2048]{3,2,1,0:T(8,128)(2,1)S(1)} collective-permute-done((bf16[4,2,8,2048]{3,2,1,0:T(8,128)(2,1)S(1)}, bf16[4,2,8,2048]{3,2,1,0:T(8,128)(2,1)S(1)}, u32[]{:S(2)}, u32[]{:S(2)}) %collective-permute-start.8) | collective-permute-done | bytes 262176 | tf_op jit(solution)/shard_map/ppermute | solution.py:24
  131.5 3.1 %collective-permute-done.10 = bf16[4,2,8,2048]{3,2,1,0:T(8,128)(2,1)S(1)} collective-permute-done((bf16[4,2,8,2048]{3,2,1,0:T(8,128)(2,1)S(1)}, bf16[4,2,8,2048]{3,2,1,0:T(8,128)(2,1)S(1)}, u32[]{:S(2)}, u32[]{:S(2)}) %collective-permute-start.10) | collective-permute-done | bytes 262176 | tf_op jit(solution)/shard_map/ppermute | solution.py:24
  134.9 1.9 %collective-permute-start.11 = (bf16[8,2,2,8,2048]{4,3,2,1,0:T(8,128)(2,1)S(1)}, bf16[8,2,2,8,2048]{4,3,2,1,0:T(8,128)(2,1)}, u32[]{:S(2)}, u32[]{:S(2)}) collective-permute-start(bf16[8,2,2,8,2048]{4,3,2,1,0:T(8,128)(2,1)S(1)} %pad_maximum_fusion), channel_id=1, source_target_pairs={{0,16},{16,0},{1,17},{17,1},{2,18},{18,2},{3,19},{19,3},{4,20},{20... | collective-permute-start | bytes 3145736 | tf_op jit(solution)/shard_map/ppermute | solution.py:24
  137.0 2.4 %convolution_convert_fusion.1 = bf16[512,448]{0,1:T(8,128)(2,1)} fusion(bf16[512,512]{1,0:T(8,128)(2,1)} %bitcast.18, bf16[448,512]{1,0:T(8,128)(2,1)} %param.11), kind=kOutput, calls=%fused_computation.4 | convolution fusion | flops 235110400 | bytes 1441792 | tf_op jit(solution)/shard_map/dot_general | solution.py:132
  139.5 2.7 %bitcast_select_fusion = bf16[512,2048]{1,0:T(8,128)(2,1)} fusion(pred[512]{0:T(512)(128)(4,1)S(1)} %iota.100, bf16[8,2,2,8,2048]{4,3,2,1,0:T(8,128)(2,1)} %collective-permute-done.11, bf16[8,2,2,8,2048]{4,3,2,1,0:T(8,128)(2,1)S(1)} %pad_maximum_fusion), kind=kLoop, calls=%fused_computation.1 | loop fusion | flops 1048576 | bytes 4194816 | tf_op jit(solution)/shard_map/jit(_where)/select_n | solution.py:28
  (53 shorter events, 13.8 us)
Async XLA Ops:
  0.6 3.0 %copy-start = (bf16[512,2048]{1,0:T(8,128)(2,1)S(1)}, bf16[512,2048]{1,0:T(8,128)(2,1)}, u32[]{:S(2)}) copy-start(bf16[512,2048]{1,0:T(8,128)(2,1)} %param.12) | copy-start | bytes 6291460
  3.7 3.6 %copy-start.3 = (bf16[512,2048]{1,0:T(8,128)(2,1)S(1)}, bf16[512,2048]{1,0:T(8,128)(2,1)}, u32[]{:S(2)}) copy-start(bf16[512,2048]{1,0:T(8,128)(2,1)} %param.10) | copy-start | bytes 6291460
  5.4 13.8 %collective-permute-start = (bf16[256,2048]{1,0:T(8,128)(2,1)}, bf16[256,2048]{1,0:T(8,128)(2,1)}, u32[]{:S(2)}, u32[]{:S(2)}) collective-permute-start(bf16[256,2048]{1,0:T(8,128)(2,1)} %convolution_convert_fusion), channel_id=1, source_target_pairs={{0,16},{16,0},{1,17},{17,1},{2,18},{18,2},{3,19},{19,3},{4,20},{20... | collective-permute-start | bytes 3145736 | tf_op jit(solution)/shard_map/ppermute | solution.py:71
  9.6 7.2 %copy-start.2 = (f32[512]{0:T(512)S(1)}, f32[512]{0:T(512)}, u32[]{:S(2)}) copy-start(f32[512]{0:T(512)} %param.9) | copy-start | bytes 6148
  9.6 37.3 %all-to-all-start = ((f32[8,64,512]{2,1,0:T(8,128)}), f32[8,64,512]{2,1,0:T(8,128)S(1)}, u32[]{:S(2)}, u32[]{:S(2)}) async-start(f32[8,64,512]{2,1,0:T(8,128)} %bitcast.107), calls=%async_computation | async-start | bytes 2097152 | tf_op jit(solution)/shard_map/all_to_all | solution.py:78
  19.1 4.7 %copy-start.1 = (f32[256,2048]{1,0:T(8,128)}, f32[256,2048]{1,0:T(8,128)S(1)}, u32[]{:S(2)}) copy-start(f32[256,2048]{1,0:T(8,128)S(1)} %fusion.62) | copy-start | bytes 6291460
  21.1 10.6 %collective-permute-start.1 = (bf16[4,2,8,2048]{3,2,0,1:T(8,128)(2,1)}, bf16[4,2,8,2048]{3,2,0,1:T(8,128)(2,1)}, u32[]{:S(2)}, u32[]{:S(2)}) collective-permute-start(bf16[4,2,8,2048]{3,2,0,1:T(8,128)(2,1)} %fusion.9), channel_id=1, source_target_pairs={{0,32},{32,0},{1,33},{33,1},{2,34},{34,2},{3,35},{35,3},{4,36},{36... | collective-permute-start | bytes 786440 | tf_op jit(solution)/shard_map/ppermute | solution.py:94
  24.8 12.2 %collective-permute-start.3 = (bf16[4,2,8,2048]{3,2,0,1:T(8,128)(2,1)S(1)}, bf16[4,2,8,2048]{3,2,0,1:T(8,128)(2,1)}, u32[]{:S(2)}, u32[]{:S(2)}) collective-permute-start(bf16[4,2,8,2048]{3,2,0,1:T(8,128)(2,1)S(1)} %fusion.10), channel_id=1, source_target_pairs={{0,64},{64,0},{1,65},{65,1},{2,66},{66,2},{3,67},{67,3},{4,68},{68... | collective-permute-start | bytes 786440 | tf_op jit(solution)/shard_map/ppermute | solution.py:96
  32.8 8.1 %collective-permute-start.2 = (bf16[4,8,2048]{2,1,0:T(8,128)(2,1)S(1)}, bf16[4,8,2048]{2,1,0:T(8,128)(2,1)S(1)}, u32[]{:S(2)}, u32[]{:S(2)}) collective-permute-start(bf16[4,8,2048]{2,1,0:T(8,128)(2,1)S(1)} %fusion.16), channel_id=1, source_target_pairs={{0,64},{64,0},{1,65},{65,1},{2,66},{66,2},{3,67},{67,3},{4,68},{68... | collective-permute-start | bytes 393224 | tf_op jit(solution)/shard_map/ppermute | solution.py:98
  38.2 6.9 %collective-permute-start.4 = (bf16[4,8,2048]{2,1,0:T(8,128)(2,1)S(1)}, bf16[4,8,2048]{2,1,0:T(8,128)(2,1)S(1)}, u32[]{:S(2)}, u32[]{:S(2)}) collective-permute-start(bf16[4,8,2048]{2,1,0:T(8,128)(2,1)S(1)} %fusion.13), channel_id=1, source_target_pairs={{0,32},{32,0},{1,33},{33,1},{2,34},{34,2},{3,35},{35,3},{4,36},{36... | collective-permute-start | bytes 393224 | tf_op jit(solution)/shard_map/ppermute | solution.py:101
  46.9 37.9 %all-to-all-start.1 = ((bf16[8,8,2048]{2,1,0:T(8,128)(2,1)}), bf16[8,8,2048]{2,1,0:T(8,128)(2,1)S(1)}, u32[]{:S(2)}, u32[]{:S(2)}) async-start(bf16[8,8,2048]{2,1,0:T(8,128)(2,1)} %pad_maximum_fusion.1), calls=%async_computation.1 | async-start | bytes 524288 | tf_op jit(solution)/shard_map/all_to_all | solution.py:110
  66.0 7.7 %collective-permute-start.5 = (f32[32,512]{1,0:T(8,128)S(1)}, f32[32,512]{1,0:T(8,128)S(1)}, u32[]{:S(2)}, u32[]{:S(2)}) collective-permute-start(f32[32,512]{1,0:T(8,128)S(1)} %dynamic-slice_bitcast_fusion), channel_id=1, source_target_pairs={{0,8},{8,0},{1,9},{9,1},{2,10},{10,2},{3,11},{11,3},{4,12},{12,4},... | collective-permute-start | bytes 196616 | tf_op jit(solution)/shard_map/ppermute | solution.py:113
  87.1 24.3 %all-to-all-start.2 = ((bf16[8,8,2048]{2,1,0:T(8,128)(2,1)}), bf16[8,8,2048]{2,1,0:T(8,128)(2,1)S(1)}, u32[]{:S(2)}, u32[]{:S(2)}) async-start(bf16[8,8,2048]{2,1,0:T(8,128)(2,1)} %broadcast_in_dim.127), calls=%async_computation.2 | async-start | bytes 524288 | tf_op jit(solution)/shard_map/all_to_all | solution.py:33
  91.8 7.3 %collective-permute-start.6 = (bf16[32,512]{1,0:T(8,128)(2,1)S(1)}, bf16[32,512]{1,0:T(8,128)(2,1)S(1)}, u32[]{:S(2)}, u32[]{:S(2)}) collective-permute-start(bf16[32,512]{1,0:T(8,128)(2,1)S(1)} %fusion.48), channel_id=1, source_target_pairs={{0,8},{8,0},{1,9},{9,1},{2,10},{10,2},{3,11},{11,3},{4,12},{12,4},... | collective-permute-start | bytes 98312 | tf_op jit(solution)/shard_map/ppermute | solution.py:24
  111.4 11.6 %collective-permute-start.7 = (bf16[4,8,2048]{2,1,0:T(8,128)(2,1)S(1)}, bf16[4,8,2048]{2,1,0:T(8,128)(2,1)S(1)}, u32[]{:S(2)}, u32[]{:S(2)}) collective-permute-start(bf16[4,8,2048]{2,1,0:T(8,128)(2,1)S(1)} %get-tuple-element.33), channel_id=1, source_target_pairs={{0,64},{64,0},{1,65},{65,1},{2,66},{66,2},{3,67},{67,3},{4,68},{68... | collective-permute-start | bytes 393224 | tf_op jit(solution)/shard_map/ppermute | solution.py:24
  115.3 10.9 %collective-permute-start.9 = (bf16[4,8,2048]{2,1,0:T(8,128)(2,1)S(1)}, bf16[4,8,2048]{2,1,0:T(8,128)(2,1)S(1)}, u32[]{:S(2)}, u32[]{:S(2)}) collective-permute-start(bf16[4,8,2048]{2,1,0:T(8,128)(2,1)S(1)} %get-tuple-element.34), channel_id=1, source_target_pairs={{0,32},{32,0},{1,33},{33,1},{2,34},{34,2},{3,35},{35,3},{4,36},{36... | collective-permute-start | bytes 393224 | tf_op jit(solution)/shard_map/ppermute | solution.py:24
  118.9 18.1 %all-to-all-start.3 = ((bf16[8,64,512]{2,1,0:T(8,128)(2,1)}), bf16[8,64,512]{2,1,0:T(8,128)(2,1)}, u32[]{:S(2)}, u32[]{:S(2)}) async-start(bf16[8,64,512]{2,1,0:T(8,128)(2,1)} %broadcast_in_dim.132), calls=%async_computation.3 | async-start | bytes 1048576 | tf_op jit(solution)/shard_map/all_to_all | solution.py:33
  123.2 8.3 %collective-permute-start.8 = (bf16[4,2,8,2048]{3,2,1,0:T(8,128)(2,1)S(1)}, bf16[4,2,8,2048]{3,2,1,0:T(8,128)(2,1)S(1)}, u32[]{:S(2)}, u32[]{:S(2)}) collective-permute-start(bf16[4,2,8,2048]{3,2,1,0:T(8,128)(2,1)S(1)} %broadcast_select_fusion.3), channel_id=1, source_target_pairs={{0,32},{32,0},{1,33},{33,1},{2,34},{34,2},{3,35},{35,3},{4,36},{36... | collective-permute-start | bytes 786440 | tf_op jit(solution)/shard_map/ppermute | solution.py:24
  126.4 8.3 %collective-permute-start.10 = (bf16[4,2,8,2048]{3,2,1,0:T(8,128)(2,1)S(1)}, bf16[4,2,8,2048]{3,2,1,0:T(8,128)(2,1)S(1)}, u32[]{:S(2)}, u32[]{:S(2)}) collective-permute-start(bf16[4,2,8,2048]{3,2,1,0:T(8,128)(2,1)S(1)} %broadcast_select_fusion.2), channel_id=1, source_target_pairs={{0,64},{64,0},{1,65},{65,1},{2,66},{66,2},{3,67},{67,3},{4,68},{68... | collective-permute-start | bytes 786440 | tf_op jit(solution)/shard_map/ppermute | solution.py:24
  134.9 4.7 %collective-permute-start.11 = (bf16[8,2,2,8,2048]{4,3,2,1,0:T(8,128)(2,1)S(1)}, bf16[8,2,2,8,2048]{4,3,2,1,0:T(8,128)(2,1)}, u32[]{:S(2)}, u32[]{:S(2)}) collective-permute-start(bf16[8,2,2,8,2048]{4,3,2,1,0:T(8,128)(2,1)S(1)} %pad_maximum_fusion), channel_id=1, source_target_pairs={{0,16},{16,0},{1,17},{17,1},{2,18},{18,2},{3,19},{19,3},{4,20},{20... | collective-permute-start | bytes 3145736 | tf_op jit(solution)/shard_map/ppermute | solution.py:24
